TPU v7x, 32 devices: a whole 2x2x4 slice. The times are simulated.
32 devices in a mesh: groups: 2 (over y), ep: 4 (over z), tok: 4 (over x, core).
Axes of the slice: x: 2, y: 2, z: 4, core: 2. Of those that a mesh axis runs over, the one named last changes fastest.
Arguments:
- tokens: bfloat16 [128, 7168], P(('groups', 'ep', 'tok')), parts along dimension 0, may hold values from -6 to 6
- expert_ids: int32 [128, 2], P(('groups', 'ep', 'tok')), parts along dimension 0, may hold values from 0 to 3, all different within a row; in each aligned block of 4 rows (0 to 3, 4 to 7, ...) at most 3 rows name the same one
- gate_fixed: int32 [128, 2], P(('groups', 'ep', 'tok')), parts along dimension 0, may hold values from 1 to 65535
- w_gate: bfloat16 [4, 7168, 2048], P('ep', None, 'tok'), may hold values from -0.0625 to 0.0625
- w_up: bfloat16 [4, 7168, 2048], P('ep', None, 'tok'), may hold values from -0.0625 to 0.0625
- w_down: bfloat16 [4, 2048, 7168], P('ep', 'tok'), may hold values from -0.125 to 0.125
Outputs:
- layer_out: bfloat16 [128, 7168], P(('groups', 'ep', 'tok')), parts along dimension 0
There are 2 independent parts, one for each index of `groups`. A program takes and returns all parts, laid end to end along the dimension named above; an argument that names none is the same for every part. Nothing has to cross between parts.
Inputs may be any that keep to these rules, and one draw needn't show every extreme that they name: `expert_ids`: each row names 2 different experts. Among the 4 rows of one device no expert is named more than 3 times.
All inputs are finite; a program needn't handle non-finite values.
Results may differ from a plain program's by a relative error of at most 0.014.
Values may be sent and summed in bfloat16 or wider, within the bound.
No kernel may reach another device: no remote copies, remote signals or barrier semaphores. Data moves between devices by JAX's collectives and lax.ppermute only.
A program may use at most 64 MiB of HBM per device.

v0:
```python
import jax
import jax.numpy as jnp
from jax import lax
from jax.sharding import PartitionSpec as P


def placing_one(routes, label, capacity):
    tok_dev = routes.shape[0]
    hit_count = jnp.sum((routes == label).astype(jnp.int32), axis=1)
    earlier = (
        lax.broadcasted_iota(jnp.int32, (tok_dev, tok_dev), 1)
        < lax.broadcasted_iota(jnp.int32, (tok_dev, tok_dev), 0)
    ).astype(jnp.int32)
    position = jnp.sum(earlier * hit_count[None, :], axis=1)
    slot_index = lax.broadcasted_iota(jnp.int32, (capacity, tok_dev), 0)
    return ((hit_count[None, :] == 1) & (position[None, :] == slot_index)).astype(jnp.bfloat16)


def per_device(tokens, expert_ids, gate_fixed, w_gate, w_up, w_down):
    tok_dev, model_width = tokens.shape
    columns = lax.axis_size("ep")
    capacity = (3 * tok_dev + 3) // 4
    labels = lax.iota(jnp.int32, columns)
    placing_all = jax.vmap(lambda label: placing_one(expert_ids, label, capacity))(labels)
    outgoing = jnp.einsum(
        "emt,td->emd", placing_all, tokens, preferred_element_type=jnp.float32
    ).astype(jnp.bfloat16)
    slot_rows = lax.all_to_all(outgoing, "ep", split_axis=0, concat_axis=0, tiled=True)
    slot_flat = slot_rows.reshape(columns * capacity, model_width)
    gate_slice = w_gate[0]
    up_slice = w_up[0]
    down_slice = w_down[0]
    segment = lax.all_gather(slot_flat, "tok", axis=0, tiled=True)
    gate = jnp.dot(segment, gate_slice, preferred_element_type=jnp.float32)
    up_val = jnp.dot(segment, up_slice, preferred_element_type=jnp.float32)
    hidden = (jax.nn.silu(gate) * up_val).astype(jnp.bfloat16)
    segment = hidden
    summed = lax.psum_scatter(
        jnp.dot(segment, down_slice, preferred_element_type=jnp.float32).astype(jnp.bfloat16),
        "tok",
        scatter_dimension=0,
        tiled=True,
    ).astype(jnp.float32)
    returned = lax.all_to_all(
        summed.reshape(columns, capacity, model_width).astype(jnp.bfloat16),
        "ep",
        split_axis=0,
        concat_axis=0,
        tiled=True,
    ).astype(jnp.float32)
    scores = gate_fixed.astype(jnp.float32)
    weights = 2.5 * scores / jnp.sum(scores, axis=1, keepdims=True)
    matches = (expert_ids[:, :, None] == labels[None, None, :]).astype(jnp.float32)
    token_expert = jnp.sum(weights[:, :, None] * matches, axis=1)
    placing_f = placing_all.astype(jnp.float32)
    slot_weight = jnp.sum(placing_f * jnp.transpose(token_expert)[:, None, :], axis=2)
    weighted = returned * slot_weight[:, :, None]
    combined = jnp.einsum(
        "emt,emd->td",
        placing_f,
        weighted,
        precision=lax.Precision.HIGHEST,
        preferred_element_type=jnp.float32,
    )
    return combined.astype(jnp.bfloat16)


def solution(mesh):
    in_specs = (
        P(("groups", "ep", "tok"), None),
        P(("groups", "ep", "tok"), None),
        P(("groups", "ep", "tok"), None),
        P("ep", None, "tok"),
        P("ep", None, "tok"),
        P("ep", "tok", None),
    )
    out_specs = P(("groups", "ep", "tok"), None)
    return jax.shard_map(
        per_device, mesh=mesh, in_specs=in_specs, out_specs=out_specs, check_vma=False
    )
```

profile of v0, /device:TPU:1, one launch (start us, length us, event | category | flops | bytes accessed | tf_op | source)
XLA Modules:
  0.0 69.4 jit_solution(11465273859720313877)
XLA Ops:
  0.0 0.0 copy-start
  0.0 0.7 %convert_reduce_fusion = s32[4,4]{1,0:T(4,128)S(1)} fusion(s32[4,2]{0,1:T(2,128)} %param.7), kind=kLoop, calls=%fused_computation.27 | loop fusion | flops 80 | bytes 96 | tf_op jit(solution)/shard_map/vmap()/reduce_sum | solution.py:9
  0.7 0.1 multiply_reduce_fusion
  0.9 0.1 copy.29
  1.0 0.1 copy.28
  1.1 0.3 convolution_convert_fusion.1
  1.4 0.1 copy.31
  1.5 11.4 %all_to_all.10 = bf16[4,3,7168]{2,1,0:T(4,128)(2,1)S(1)} all-to-all(bf16[4,3,7168]{2,1,0:T(4,128)(2,1)S(1)} %copy.31), channel_id=1, replica_groups=mesh['groups'=2,'ep'=4,'tok'=4] {'ep'}, dimensions={0} | all-to-all | bytes 344064 | tf_op jit(solution)/shard_map/all_to_all | solution.py:28
  13.0 0.2 reshape.26
  13.1 12.1 %all-gather = bf16[4,12,7168]{2,1,0:T(8,128)(2,1)S(1)} all-gather(bf16[1,12,7168]{2,1,0:T(8,128)(2,1)S(1)} %reshape.26), channel_id=1, replica_groups=mesh['groups'=2,'ep'=4,'tok'=4] {'tok'}, dimensions={0}, use_global_device_ids=true | all-gather | bytes 860160 | tf_op jit(solution)/shard_map/all_gather | solution.py:33
  25.2 0.2 reshape.27
  25.3 4.4 %fusion.5 = f32[48,512]{1,0:T(8,128)S(1)} fusion(bf16[48,7168]{1,0:T(8,128)(2,1)S(1)} %reshape.27, bf16[1,7168,512]{2,1,0:T(8,128)(2,1)} %param.9), kind=kOutput, calls=%fused_computation.7 | convolution fusion | flops 352321536 | bytes 8126464 | tf_op jit(solution)/shard_map/dot_general | solution.py:34
  29.8 0.0 copy-start.3
  29.8 0.0 copy-start.2
  29.8 0.0 copy-start.1
  29.8 7.9 %convolution_convert_fusion = bf16[48,7168]{1,0:T(8,128)(2,1)S(1)} fusion(bf16[1,512,7168]{2,1,0:T(8,128)(2,1)} %param.11, bf16[48,7168]{1,0:T(8,128)(2,1)S(1)} %reshape.27, bf16[1,7168,512]{2,1,0:T(8,128)(2,1)} %param.10, f32[48,512]{1,0:T(8,128)S(1)} %fusion.5), kind=kOutput, calls=%fused_computation | convolution fusion | flops 705134592 | bytes 16154624 | tf_op jit(solution)/shard_map/dot_general | solution.py:39
  37.7 11.4 %fusion = bf16[16,7168]{1,0:T(8,128)(2,1)S(1)} fusion(bf16[48,7168]{1,0:T(8,128)(2,1)S(1)} %convolution_convert_fusion), kind=kCustom, calls=%all-reduce-scatter | all-reduce-scatter fusion | flops 458753 | bytes 918016
  49.2 0.1 slice
  49.2 4.4 %collective-permute-start = (bf16[12,7168]{1,0:T(8,128)(2,1)S(1)}, bf16[12,7168]{1,0:T(8,128)(2,1)S(1)}, u32[]{:S(2)}, u32[]{:S(2)}) collective-permute-start(bf16[12,7168]{1,0:T(8,128)(2,1)S(1)} %slice), channel_id=1, source_target_pairs={{0,1},{1,2},{2,3},{4,5},{5,6},{6,7},{8,9},{9,10},{10,11},{12,13},{... | collective-permute-start | bytes 516104
  53.6 0.6 dynamic-slice.4
  54.9 0.0 copy-done.2
  54.9 1.7 %collective-permute-done = bf16[12,7168]{1,0:T(8,128)(2,1)S(1)} collective-permute-done((bf16[12,7168]{1,0:T(8,128)(2,1)S(1)}, bf16[12,7168]{1,0:T(8,128)(2,1)S(1)}, u32[]{:S(2)}, u32[]{:S(2)}) %collective-permute-start) | collective-permute-done | bytes 172064
  56.6 0.6 concatenate
  57.2 0.1 constant_dynamic-slice_fusion
  57.3 0.8 %convert_element_type.45 = bf16[4,3,7168]{2,1,0:T(4,128)(2,1)} reshape(bf16[12,7168]{1,0:T(8,128)(2,1)S(1)} %constant_dynamic-slice_fusion) | data formatting | bytes 344064 | tf_op jit(solution)/shard_map/convert_element_type | solution.py:45
  58.1 3.4 %all-to-all-start.1 = ((bf16[4,3,7168]{2,1,0:T(4,128)(2,1)}), bf16[4,3,7168]{2,1,0:T(4,128)(2,1)S(1)}, u32[]{:S(2)}, u32[]{:S(2)}) async-start(bf16[4,3,7168]{2,1,0:T(4,128)(2,1)} %convert_element_type.45), calls=%async_computation.1 | async-start | bytes 458752 | tf_op jit(solution)/shard_map/all_to_all | solution.py:44
  61.5 0.0 copy-done.1
  61.5 0.1 select_reduce_fusion
  61.6 0.1 copy.32
  61.7 6.3 %all-to-all-done.1 = bf16[4,3,7168]{2,1,0:T(4,128)(2,1)S(1)} async-done(((bf16[4,3,7168]{2,1,0:T(4,128)(2,1)}), bf16[4,3,7168]{2,1,0:T(4,128)(2,1)S(1)}, u32[]{:S(2)}, u32[]{:S(2)}) %all-to-all-start.1) | async-done | bytes 172064 | tf_op jit(solution)/shard_map/all_to_all | solution.py:44
  68.0 0.1 convert_multiply_fusion
  68.1 1.3 %fusion.1 = bf16[4,7168]{1,0:T(4,128)(2,1)} fusion(f32[4,3,7168]{2,1,0:T(4,128)S(1)} %convert_multiply_fusion, s32[4,4]{0,1:T(4,128)S(1)} %copy.29, pred[4,4]{0,1:T(4,128)(4,1)S(1)} %copy.28), kind=kOutput, calls=%fused_computation.3 | convolution fusion | flops 4157536 | bytes 401488 | tf_op jit(solution)/shard_map/emt,emd->td/dot_general | solution.py:58
  (7 shorter events, 0.1 us)
Async XLA Ops:
  0.0 1.1 %copy-start = (bf16[4,7168]{1,0:T(4,128)(2,1)S(1)}, bf16[4,7168]{1,0:T(4,128)(2,1)}, u32[]{:S(2)}) copy-start(bf16[4,7168]{1,0:T(4,128)(2,1)} %param.6) | copy-start | bytes 172036
  29.8 23.9 %copy-start.3 = (u32[32]{0:T(128)S(1)}, u32[32]{0:T(128)}, u32[]{:S(2)}) copy-start(u32[32]{0:T(128)} %constant.20) | copy-start | bytes 388
  29.8 25.1 %copy-start.2 = (s32[4,2]{0,1:T(2,128)S(1)}, s32[4,2]{0,1:T(2,128)}, u32[]{:S(2)}) copy-start(s32[4,2]{0,1:T(2,128)} %param.8) | copy-start | bytes 100
  29.8 31.7 %copy-start.1 = (s32[4,2]{0,1:T(2,128)S(1)}, s32[4,2]{0,1:T(2,128)}, u32[]{:S(2)}) copy-start(s32[4,2]{0,1:T(2,128)} %param.7) | copy-start | bytes 100
  49.2 7.3 %collective-permute-start = (bf16[12,7168]{1,0:T(8,128)(2,1)S(1)}, bf16[12,7168]{1,0:T(8,128)(2,1)S(1)}, u32[]{:S(2)}, u32[]{:S(2)}) collective-permute-start(bf16[12,7168]{1,0:T(8,128)(2,1)S(1)} %slice), channel_id=1, source_target_pairs={{0,1},{1,2},{2,3},{4,5},{5,6},{6,7},{8,9},{9,10},{10,11},{12,13},{... | collective-permute-start | bytes 516104
  58.1 9.9 %all-to-all-start.1 = ((bf16[4,3,7168]{2,1,0:T(4,128)(2,1)}), bf16[4,3,7168]{2,1,0:T(4,128)(2,1)S(1)}, u32[]{:S(2)}, u32[]{:S(2)}) async-start(bf16[4,3,7168]{2,1,0:T(4,128)(2,1)} %convert_element_type.45), calls=%async_computation.1 | async-start | bytes 458752 | tf_op jit(solution)/shard_map/all_to_all | solution.py:44
where the time goes:
time: 69.8 us; the launch traced here: 69.4 us
  blocking collectives  34.9 us (50%)
  matrix products  13.9 us (20%)
  waiting for transfers between devices  7.99 us (11%)
  starting transfers between devices  7.75 us (11%)
  local copies, waits for them, and re-layouts  2.9 us (4%)
  other arithmetic  1.12 us (2%)
  between operations  0.79 us (1%)
    all_gather x1, blocking collectives, per_device(): segment = lax.all_gather(slot_flat, 'tok', axis=0, tiled=True)  12.1 us
    unnamed x1, blocking collectives  11.4 us
    all_to_all x1, blocking collectives, per_device(): lax.all_to_all(outgoing, 'ep', split_axis=0, concat_axis=0, tiled=True)  11.4 us
    dot_general x1, matrix products, per_device(): jnp.dot(segment, down_slice, preferred_element_type=jnp.float32)  7.91 us
    all_to_all x1, waiting for transfers between devices, per_device(): lax.all_to_all(summed.reshape(columns, capacity, model_width).astype(jnp....  6.33 us
    dot_general x1, matrix products, per_device(): gate = jnp.dot(segment, gate_slice, preferred_element_type=jnp.float32)  4.43 us
    unnamed x1, starting transfers between devices  4.37 us
    all_to_all x1, starting transfers between devices, per_device(): lax.all_to_all(summed.reshape(columns, capacity, model_width).astype(jnp....  3.38 us
  transfers between devices with their start and end apart: 2, of which 2 were waited for; matrix products, arithmetic and copies ran while one was open for 1% of the time, Pallas kernels for 0%

commit v1 on v0

v1 whole, which is shorter than its diff:
```python
import functools

import jax
import jax.numpy as jnp
from jax import lax
from jax.experimental import pallas as pl
from jax.experimental.pallas import tpu as pltpu
from jax.sharding import PartitionSpec as P


CORES = 2
MIB = 1 << 20
VMEM_BYTES = 58 * MIB


def shift(value, axis, amount):
    size = lax.axis_size(axis)
    return lax.ppermute(value, axis, [(i, (i + amount) % size) for i in range(size)])


def core_swap(value):
    size = lax.axis_size("tok")
    return lax.ppermute(value, "tok", [(i, i ^ 1) for i in range(size)])


def fetch_all(pairs, semaphores):
    copies = [pltpu.make_async_copy(s, t, semaphores.at[i]) for i, (s, t) in enumerate(pairs)]
    for copy in copies:
        copy.start()
    for copy in copies:
        copy.wait()


def open_kernel(cut, gate_ref, up_ref, gate_out, up_out, semaphores):
    pairs = [(gate_ref, gate_out)]
    if cut:
        pairs.append((up_ref.at[pl.ds(0, cut)], up_out.at[pl.ds(0, cut)]))
    fetch_all(pairs, semaphores)


def rest_kernel(cut, held_ref, up_ref, up_out, semaphores):
    span = pl.ds(cut, up_ref.shape[0] - cut)
    fetch_all([(up_ref.at[span], up_out.at[span])], semaphores)


def kernel_limit(weight, extra=0):
    return VMEM_BYTES - 4 * weight.size - 6 * MIB + extra * MIB


def load_open(gate_w, up_w, cut):
    hbm = pl.BlockSpec(memory_space=pltpu.HBM)
    vmem = pl.BlockSpec(memory_space=pltpu.VMEM)
    return pl.pallas_call(
        functools.partial(open_kernel, cut),
        out_shape=[jax.ShapeDtypeStruct(w.shape, w.dtype) for w in (gate_w, up_w)],
        in_specs=[hbm, hbm],
        out_specs=[vmem, vmem],
        scratch_shapes=[pltpu.SemaphoreType.DMA((2,))],
        compiler_params=pltpu.CompilerParams(vmem_limit_bytes=kernel_limit(gate_w)),
        name="load_open",
    )(gate_w, up_w)


def load_rest(held, up_w, cut):
    hbm = pl.BlockSpec(memory_space=pltpu.HBM)
    vmem = pl.BlockSpec(memory_space=pltpu.VMEM)
    return pl.pallas_call(
        functools.partial(rest_kernel, cut),
        out_shape=jax.ShapeDtypeStruct(up_w.shape, up_w.dtype),
        in_specs=[vmem, hbm],
        out_specs=vmem,
        input_output_aliases={0: 0},
        scratch_shapes=[pltpu.SemaphoreType.DMA((2,))],
        compiler_params=pltpu.CompilerParams(vmem_limit_bytes=kernel_limit(up_w, 3)),
        name="load_rest",
    )(held, up_w)


def ffn_kernel(count, depth, width, *refs):
    chunks = refs[:count]
    gate_ref, up_ref, down_ref = refs[count:count + 3]
    outs = refs[count + 3:2 * count + 3]
    gate_sum, up_sum, hidden, down_vmem, semaphore = refs[2 * count + 3:]
    fetch = pltpu.make_async_copy(down_ref, down_vmem, semaphore)
    fetch.start()
    rows, model = chunks[0].shape
    gate_sum[...] = jnp.zeros_like(gate_sum)
    up_sum[...] = jnp.zeros_like(up_sum)

    def project(i, carry):
        span = pl.ds(pl.multiple_of(i * depth, depth), depth)
        tokens = jnp.concatenate([c[:, span].astype(jnp.float32) for c in chunks], axis=0).astype(jnp.bfloat16)
        gate_sum[...] += jnp.dot(tokens, gate_ref[span, :], preferred_element_type=jnp.float32)
        up_sum[...] += jnp.dot(tokens, up_ref[span, :], preferred_element_type=jnp.float32)
        return carry

    lax.fori_loop(0, model // depth, project, 0)
    gate = gate_sum[...]
    hidden[...] = (gate / (1.0 + jnp.exp(-gate)) * up_sum[...]).astype(jnp.bfloat16)

    fetch.wait()

    def expand(i, carry):
        span = pl.ds(pl.multiple_of(i * width, width), width)
        partial = jnp.dot(hidden[...], down_vmem[:, span], preferred_element_type=jnp.float32)
        for j, out in enumerate(outs):
            out[:, span] = partial[j * rows:(j + 1) * rows].astype(jnp.bfloat16)
        return carry

    lax.fori_loop(0, model // width, expand, 0)


def ffn(chunks, gate_w, up_w, down_w):
    count = len(chunks)
    rows, model = chunks[0].shape
    units = gate_w.shape[1]
    total = count * rows
    block = 1024 if model % 1024 == 0 else model
    vmem = pl.BlockSpec(memory_space=pltpu.VMEM)
    return pl.pallas_call(
        functools.partial(ffn_kernel, count, block, block),
        out_shape=[jax.ShapeDtypeStruct((rows, model), jnp.bfloat16)] * count,
        in_specs=[vmem] * (count + 2) + [pl.BlockSpec(memory_space=pltpu.HBM)],
        out_specs=[vmem] * count,
        scratch_shapes=[
            pltpu.VMEM((total, units), jnp.float32),
            pltpu.VMEM((total, units), jnp.float32),
            pltpu.VMEM((total, units), jnp.bfloat16),
            pltpu.VMEM(down_w.shape, down_w.dtype),
            pltpu.SemaphoreType.DMA,
        ],
        compiler_params=pltpu.CompilerParams(vmem_limit_bytes=kernel_limit(gate_w)),
        cost_estimate=pl.CostEstimate(
            flops=6 * total * model * units,
            bytes_accessed=6 * model * units + 4 * total * model,
            transcendentals=total * units,
        ),
        name="ffn",
    )(*chunks, gate_w, up_w, down_w)


def combine_kernel(ids_ref, gate_ref, *refs):
    terms, out = refs[:-1], refs[-1]
    me = lax.axis_index("ep")
    ids = ids_ref[...]
    scores = gate_ref[...].astype(jnp.float32)
    weights = 2.5 * scores / jnp.sum(scores, axis=1, keepdims=True)
    total = jnp.zeros(out.shape, jnp.float32)
    for k, term in enumerate(terms):
        label = lax.rem(me + k, len(terms))
        weight = jnp.sum(jnp.where(ids == label, weights, 0.0), axis=1, keepdims=True)
        total = total + weight * term[...].astype(jnp.float32)
    out[...] = total.astype(jnp.bfloat16)


def combine(expert_ids, gate_fixed, terms):
    vmem = pl.BlockSpec(memory_space=pltpu.VMEM)
    return pl.pallas_call(
        combine_kernel,
        out_shape=jax.ShapeDtypeStruct(terms[0].shape, jnp.bfloat16),
        in_specs=[vmem] * (len(terms) + 2),
        out_specs=vmem,
        compiler_params=pltpu.CompilerParams(vmem_limit_bytes=8 * MIB),
        name="combine",
    )(expert_ids, gate_fixed, *terms)


def per_device(tokens, expert_ids, gate_fixed, w_gate, w_up, w_down):
    n_ep = lax.axis_size("ep")
    n_x = lax.axis_size("tok") // CORES
    columns = [tokens]
    for k in range(1, n_ep):
        columns.append(shift(tokens, "ep", k))
    planes = []
    for k in range(n_ep):
        for j in range(n_x):
            planes.append(columns[k] if j == 0 else shift(columns[k], "tok", CORES * j))
    mirrored = []
    for n, chunk in enumerate(planes):
        mirrored.append(core_swap(chunk))
    gate_w, held = load_open(w_gate[0], w_up[0], w_up.shape[1] // 4)
    up_w = load_rest(held, w_up[0], w_up.shape[1] // 4)
    parts = ffn(planes + mirrored, gate_w, up_w, w_down[0])
    half = len(planes)
    terms = []
    for k in range(n_ep):
        total = None
        for j in range(n_x):
            n = k * n_x + j
            other = core_swap(parts[half + n])
            both = parts[n].astype(jnp.float32) + other.astype(jnp.float32)
            if j:
                both = shift(both.astype(jnp.bfloat16), "tok", -CORES * j).astype(jnp.float32)
            total = both if total is None else total + both
        total = total.astype(jnp.bfloat16)
        if k:
            total = shift(total, "ep", -k)
        terms.append(total)
    return combine(expert_ids, gate_fixed, terms)


def solution(mesh):
    in_specs = (
        P(("groups", "ep", "tok"), None),
        P(("groups", "ep", "tok"), None),
        P(("groups", "ep", "tok"), None),
        P("ep", None, "tok"),
        P("ep", None, "tok"),
        P("ep", "tok", None),
    )
    out_specs = P(("groups", "ep", "tok"), None)
    return jax.shard_map(
        per_device, mesh=mesh, in_specs=in_specs, out_specs=out_specs, check_vma=False
    )
```

time: 69.8 us -> 46.7 us (0.67)
  the two profiles are of different devices: /device:TPU:1 before, /device:TPU:0 now
where the time goes in v1:
time: 46.7 us; the launch traced here: 46.6 us
  starting transfers between devices  23.2 us (50%)
  Pallas kernels  12.7 us (27%)
  waiting for transfers between devices  9.97 us (21%)
    ppermute x14, starting transfers between devices, shift(): lax.ppermute(value, axis, [(i, (i + amount) % size) for i in range(size)])  19.8 us
    ppermute x14, waiting for transfers between devices, shift(): lax.ppermute(value, axis, [(i, (i + amount) % size) for i in range(size)])  9.19 us
    pallas_call x1, Pallas kernels, ffn(): pl.pallas_call(functools.partial(ffn_kernel, count, block, block), out_sh...  5.58 us
    pallas_call x1, Pallas kernels, load_open(): pl.pallas_call(functools.partial(open_kernel, cut), out_shape=[jax.ShapeD...  3.63 us
    ppermute x16, starting transfers between devices, core_swap(): return lax.ppermute(value, 'tok', [(i, i ^ 1) for i in range(size)])  3.39 us
    pallas_call x1, Pallas kernels, load_rest(): pl.pallas_call(functools.partial(rest_kernel, cut), out_shape=jax.ShapeDt...  2.6 us
  transfers between devices with their start and end apart: 30, of which 10 were waited for; matrix products, arithmetic and copies ran while one was open for 1% of the time, Pallas kernels for 13%

profile of v1, /device:TPU:0, one launch (start us, length us, event | category | flops | bytes accessed | tf_op | source)
XLA Modules:
  0.0 46.6 jit_solution(14029669650910389509)
XLA Ops:
  0.0 3.1 %collective-permute-start.1 = (bf16[4,7168]{1,0:T(4,128)(2,1)}, bf16[4,7168]{1,0:T(4,128)(2,1)S(1)}, u32[]{:S(2)}, u32[]{:S(2)}) collective-permute-start(bf16[4,7168]{1,0:T(4,128)(2,1)} %refs_0_.1), channel_id=1, source_target_pairs={{0,4},{4,8},{8,12},{12,0},{1,5},{5,9},{9,13},{13,1},{2,6},{6,10},{... | collective-permute-start | bytes 172040 | tf_op jit(solution)/shard_map/ppermute | solution.py:18
  3.1 2.6 %collective-permute-start.3 = (bf16[4,7168]{1,0:T(4,128)(2,1)}, bf16[4,7168]{1,0:T(4,128)(2,1)S(1)}, u32[]{:S(2)}, u32[]{:S(2)}) collective-permute-start(bf16[4,7168]{1,0:T(4,128)(2,1)} %refs_0_.1), channel_id=1, source_target_pairs={{0,8},{4,12},{8,0},{12,4},{1,9},{5,13},{9,1},{13,5},{2,10},{6,14},... | collective-permute-start | bytes 172040 | tf_op jit(solution)/shard_map/ppermute | solution.py:18
  5.6 1.3 %collective-permute-start.5 = (bf16[4,7168]{1,0:T(4,128)(2,1)}, bf16[4,7168]{1,0:T(4,128)(2,1)S(1)}, u32[]{:S(2)}, u32[]{:S(2)}) collective-permute-start(bf16[4,7168]{1,0:T(4,128)(2,1)} %refs_0_.1), channel_id=1, source_target_pairs={{0,12},{4,0},{8,4},{12,8},{1,13},{5,1},{9,5},{13,9},{2,14},{6,2},{... | collective-permute-start | bytes 172040 | tf_op jit(solution)/shard_map/ppermute | solution.py:18
  7.0 1.5 %collective-permute-start = (bf16[4,7168]{1,0:T(4,128)(2,1)}, bf16[4,7168]{1,0:T(4,128)(2,1)S(1)}, u32[]{:S(2)}, u32[]{:S(2)}) collective-permute-start(bf16[4,7168]{1,0:T(4,128)(2,1)} %refs_0_.1), channel_id=1, source_target_pairs={{0,2},{1,3},{2,0},{3,1},{4,6},{5,7},{6,4},{7,5},{8,10},{9,11},{10,... | collective-permute-start | bytes 172040 | tf_op jit(solution)/shard_map/ppermute | solution.py:18
  8.5 1.0 %collective-permute-start.2 = (bf16[4,7168]{1,0:T(4,128)(2,1)S(1)}, bf16[4,7168]{1,0:T(4,128)(2,1)S(1)}, u32[]{:S(2)}, u32[]{:S(2)}) collective-permute-start(bf16[4,7168]{1,0:T(4,128)(2,1)S(1)} %collective-permute-done.1.refs_2_), channel_id=1, source_target_pairs={{0,2},{1,3},{2,0},{3,1},{4,6},{5,7},{6,4},{7,5},{8,10},{9,11},{10,... | collective-permute-start | bytes 172040 | tf_op jit(solution)/shard_map/ppermute | solution.py:18
  9.5 0.4 collective-permute-done.3.refs_4_
  9.9 1.7 %collective-permute-start.4 = (bf16[4,7168]{1,0:T(4,128)(2,1)S(1)}, bf16[4,7168]{1,0:T(4,128)(2,1)S(1)}, u32[]{:S(2)}, u32[]{:S(2)}) collective-permute-start(bf16[4,7168]{1,0:T(4,128)(2,1)S(1)} %collective-permute-done.3.refs_4_), channel_id=1, source_target_pairs={{0,2},{1,3},{2,0},{3,1},{4,6},{5,7},{6,4},{7,5},{8,10},{9,11},{10,... | collective-permute-start | bytes 172040 | tf_op jit(solution)/shard_map/ppermute | solution.py:18
  11.6 0.3 collective-permute-start.6
  11.9 0.5 %collective-permute-start.13 = (bf16[4,7168]{1,0:T(4,128)(2,1)S(1)}, bf16[4,7168]{1,0:T(4,128)(2,1)S(1)}, u32[]{:S(2)}, u32[]{:S(2)}) collective-permute-start(bf16[4,7168]{1,0:T(4,128)(2,1)S(1)} %collective-permute-done.5.refs_6_), channel_id=1, source_target_pairs={{0,1},{1,0},{2,3},{3,2},{4,5},{5,4},{6,7},{7,6},{8,9},{9,8},{10,11... | collective-permute-start | bytes 172040 | tf_op jit(solution)/shard_map/ppermute | solution.py:23
  12.4 0.8 %collective-permute-done.2.refs_3_ = bf16[4,7168]{1,0:T(4,128)(2,1)S(1)} collective-permute-done((bf16[4,7168]{1,0:T(4,128)(2,1)S(1)}, bf16[4,7168]{1,0:T(4,128)(2,1)S(1)}, u32[]{:S(2)}, u32[]{:S(2)}) %collective-permute-start.2) | collective-permute-done | bytes 57376 | tf_op jit(solution)/shard_map/ppermute | solution.py:18
  13.3 1.4 %collective-permute-done.4.refs_5_ = bf16[4,7168]{1,0:T(4,128)(2,1)S(1)} collective-permute-done((bf16[4,7168]{1,0:T(4,128)(2,1)S(1)}, bf16[4,7168]{1,0:T(4,128)(2,1)S(1)}, u32[]{:S(2)}, u32[]{:S(2)}) %collective-permute-start.4) | collective-permute-done | bytes 57376 | tf_op jit(solution)/shard_map/ppermute | solution.py:18
  14.7 1.1 %collective-permute-done.6.refs_7_ = bf16[4,7168]{1,0:T(4,128)(2,1)S(1)} collective-permute-done((bf16[4,7168]{1,0:T(4,128)(2,1)S(1)}, bf16[4,7168]{1,0:T(4,128)(2,1)S(1)}, u32[]{:S(2)}, u32[]{:S(2)}) %collective-permute-start.6) | collective-permute-done | bytes 57376 | tf_op jit(solution)/shard_map/ppermute | solution.py:18
  15.8 0.5 %collective-permute-start.12 = (bf16[4,7168]{1,0:T(4,128)(2,1)S(1)}, bf16[4,7168]{1,0:T(4,128)(2,1)S(1)}, u32[]{:S(2)}, u32[]{:S(2)}) collective-permute-start(bf16[4,7168]{1,0:T(4,128)(2,1)S(1)} %collective-permute-done.4.refs_5_), channel_id=1, source_target_pairs={{0,1},{1,0},{2,3},{3,2},{4,5},{5,4},{6,7},{7,6},{8,9},{9,8},{10,11... | collective-permute-start | bytes 172040 | tf_op jit(solution)/shard_map/ppermute | solution.py:23
  16.4 3.6 %load_open.1 = (bf16[7168,512]{1,0:T(8,128)(2,1)S(1)}, bf16[7168,512]{1,0:T(8,128)(2,1)S(1)}) custom-call(bf16[7168,512]{1,0:T(8,128)(2,1)} %bitcast.5, bf16[7168,512]{1,0:T(8,128)(2,1)} %bitcast.3), custom_call_target="tpu_custom_call" | custom-call | tf_op jit(solution)/shard_map/load_open/pallas_call | solution.py:53
  20.0 2.6 %load_rest.1.refs_17_ = bf16[7168,512]{1,0:T(8,128)(2,1)S(1)} custom-call(bf16[7168,512]{1,0:T(8,128)(2,1)S(1)} %get-tuple-element.24.held_ref, bf16[7168,512]{1,0:T(8,128)(2,1)} %bitcast.4), custom_call_target="tpu_custom_call", output_to_operand_aliasing={{}: (0, {})} | custom-call | tf_op jit(solution)/shard_map/load_rest/pallas_call | solution.py:67
  22.7 5.6 %ffn.1 = (bf16[4,7168]{1,0:T(4,128)(2,1)S(1)}, bf16[4,7168]{1,0:T(4,128)(2,1)S(1)}, bf16[4,7168]{1,0:T(4,128)(2,1)S(1)}, bf16[4,7168]{1,0:T(4,128)(2,1)S(1)}, bf...) custom-call(bf16[4,7168]{1,0:T(4,128)(2,1)S(1)} %copy-done, ...), custom_call_target="tpu_custom_call" | custom-call | flops 1409286144 | bytes 23855104 | tf_op jit(solution)/shard_map/ffn/pallas_call | solution.py:120
  28.3 0.5 %collective-permute-start.27 = (bf16[4,7168]{1,0:T(4,128)(2,1)S(1)}, bf16[4,7168]{1,0:T(4,128)(2,1)S(1)}, u32[]{:S(2)}, u32[]{:S(2)}) collective-permute-start(bf16[4,7168]{1,0:T(4,128)(2,1)S(1)} %get-tuple-element.40), channel_id=1, source_target_pairs={{0,1},{1,0},{2,3},{3,2},{4,5},{5,4},{6,7},{7,6},{8,9},{9,8},{10,11... | collective-permute-start | bytes 172040 | tf_op jit(solution)/shard_map/ppermute | solution.py:23
  29.1 0.4 collective-permute-start.23
  29.6 0.4 collective-permute-start.19
  30.1 0.3 collective-permute-done.23
  30.4 0.4 collective-permute-start.16
  30.9 0.4 collective-permute-start.15
  31.3 0.3 collective-permute-done.16
  31.7 0.6 %collective-permute-start.28 = (bf16[4,7168]{1,0:T(4,128)(2,1)S(1)}, bf16[4,7168]{1,0:T(4,128)(2,1)S(1)}, u32[]{:S(2)}, u32[]{:S(2)}) collective-permute-start(bf16[4,7168]{1,0:T(4,128)(2,1)S(1)} %add_convert_fusion.1), channel_id=1, source_target_pairs={{0,2},{1,3},{2,0},{3,1},{4,6},{5,7},{6,4},{7,5},{8,10},{9,11},{10,... | collective-permute-start | bytes 172040 | tf_op jit(solution)/shard_map/ppermute | solution.py:18
  32.3 1.5 %collective-permute-start.24 = (bf16[4,7168]{1,0:T(4,128)(2,1)S(1)}, bf16[4,7168]{1,0:T(4,128)(2,1)S(1)}, u32[]{:S(2)}, u32[]{:S(2)}) collective-permute-start(bf16[4,7168]{1,0:T(4,128)(2,1)S(1)} %add_convert_fusion.3), channel_id=1, source_target_pairs={{0,2},{1,3},{2,0},{3,1},{4,6},{5,7},{6,4},{7,5},{8,10},{9,11},{10,... | collective-permute-start | bytes 172040 | tf_op jit(solution)/shard_map/ppermute | solution.py:18
  33.8 2.6 %collective-permute-done.28 = bf16[4,7168]{1,0:T(4,128)(2,1)S(1)} collective-permute-done((bf16[4,7168]{1,0:T(4,128)(2,1)S(1)}, bf16[4,7168]{1,0:T(4,128)(2,1)S(1)}, u32[]{:S(2)}, u32[]{:S(2)}) %collective-permute-start.28) | collective-permute-done | bytes 57376 | tf_op jit(solution)/shard_map/ppermute | solution.py:18
  36.5 2.1 %collective-permute-start.17 = (bf16[4,7168]{1,0:T(4,128)(2,1)S(1)}, bf16[4,7168]{1,0:T(4,128)(2,1)S(1)}, u32[]{:S(2)}, u32[]{:S(2)}) collective-permute-start(bf16[4,7168]{1,0:T(4,128)(2,1)S(1)} %add_convert_fusion.7), channel_id=1, source_target_pairs={{0,2},{1,3},{2,0},{3,1},{4,6},{5,7},{6,4},{7,5},{8,10},{9,11},{10,... | collective-permute-start | bytes 172040 | tf_op jit(solution)/shard_map/ppermute | solution.py:18
  38.7 2.7 %collective-permute-start.25 = (bf16[4,7168]{1,0:T(4,128)(2,1)S(1)}, bf16[4,7168]{1,0:T(4,128)(2,1)S(1)}, u32[]{:S(2)}, u32[]{:S(2)}) collective-permute-start(bf16[4,7168]{1,0:T(4,128)(2,1)S(1)} %add_convert_fusion.2), channel_id=1, source_target_pairs={{0,8},{4,12},{8,0},{12,4},{1,9},{5,13},{9,1},{13,5},{2,10},{6,14},... | collective-permute-start | bytes 172040 | tf_op jit(solution)/shard_map/ppermute | solution.py:18
  41.5 1.4 %collective-permute-start.21 = (bf16[4,7168]{1,0:T(4,128)(2,1)S(1)}, bf16[4,7168]{1,0:T(4,128)(2,1)S(1)}, u32[]{:S(2)}, u32[]{:S(2)}) collective-permute-start(bf16[4,7168]{1,0:T(4,128)(2,1)S(1)} %add_convert_fusion.4), channel_id=1, source_target_pairs={{0,12},{4,0},{8,4},{12,8},{1,13},{5,1},{9,5},{13,9},{2,14},{6,2},{... | collective-permute-start | bytes 172040 | tf_op jit(solution)/shard_map/ppermute | solution.py:18
  42.9 1.7 %collective-permute-done.29.refs_3_ = bf16[4,7168]{1,0:T(4,128)(2,1)S(1)} collective-permute-done((bf16[4,7168]{1,0:T(4,128)(2,1)S(1)}, bf16[4,7168]{1,0:T(4,128)(2,1)S(1)}, u32[]{:S(2)}, u32[]{:S(2)}) %collective-permute-start.29) | collective-permute-done | bytes 57376 | tf_op jit(solution)/shard_map/ppermute | solution.py:18
  44.6 1.1 %collective-permute-done.21.refs_1_ = bf16[4,7168]{1,0:T(4,128)(2,1)S(1)} collective-permute-done((bf16[4,7168]{1,0:T(4,128)(2,1)S(1)}, bf16[4,7168]{1,0:T(4,128)(2,1)S(1)}, u32[]{:S(2)}, u32[]{:S(2)}) %collective-permute-start.21) | collective-permute-done | bytes 57376 | tf_op jit(solution)/shard_map/ppermute | solution.py:18
  45.7 0.9 %combine.1 = bf16[4,7168]{1,0:T(4,128)(2,1)} custom-call(s32[4,2]{1,0:T(4,128)S(1)} %copy.8.ids_ref, s32[4,2]{1,0:T(4,128)S(1)} %copy.9.gate_ref, bf16[4,7168]{1,0:T(4,128)(2,1)S(1)} %add_convert_fusion.6.refs_0_, bf16[4,7168]{1,0:T(4,128)(2,1)S(1)} %collective-permute-done.21.refs_1_, bf16[4,7168]{1,0:T(4,128)(2,1)S(1)} %collective-permute-done.25.refs_2_, ...), custom_call_target="tpu_custom_call" | custom-call | tf_op jit(solution)/shard_map/combine/pallas_call | solution.py:158
  (48 shorter events, 1.0 us)
Async XLA Ops:
  0.0 8.5 %collective-permute-start.1 = (bf16[4,7168]{1,0:T(4,128)(2,1)}, bf16[4,7168]{1,0:T(4,128)(2,1)S(1)}, u32[]{:S(2)}, u32[]{:S(2)}) collective-permute-start(bf16[4,7168]{1,0:T(4,128)(2,1)} %refs_0_.1), channel_id=1, source_target_pairs={{0,4},{4,8},{8,12},{12,0},{1,5},{5,9},{9,13},{13,1},{2,6},{6,10},{... | collective-permute-start | bytes 172040 | tf_op jit(solution)/shard_map/ppermute | solution.py:18
  3.1 6.8 %collective-permute-start.3 = (bf16[4,7168]{1,0:T(4,128)(2,1)}, bf16[4,7168]{1,0:T(4,128)(2,1)S(1)}, u32[]{:S(2)}, u32[]{:S(2)}) collective-permute-start(bf16[4,7168]{1,0:T(4,128)(2,1)} %refs_0_.1), channel_id=1, source_target_pairs={{0,8},{4,12},{8,0},{12,4},{1,9},{5,13},{9,1},{13,5},{2,10},{6,14},... | collective-permute-start | bytes 172040 | tf_op jit(solution)/shard_map/ppermute | solution.py:18
  5.6 6.0 %collective-permute-start.5 = (bf16[4,7168]{1,0:T(4,128)(2,1)}, bf16[4,7168]{1,0:T(4,128)(2,1)S(1)}, u32[]{:S(2)}, u32[]{:S(2)}) collective-permute-start(bf16[4,7168]{1,0:T(4,128)(2,1)} %refs_0_.1), channel_id=1, source_target_pairs={{0,12},{4,0},{8,4},{12,8},{1,13},{5,1},{9,5},{13,9},{2,14},{6,2},{... | collective-permute-start | bytes 172040 | tf_op jit(solution)/shard_map/ppermute | solution.py:18
  7.0 4.9 %collective-permute-start = (bf16[4,7168]{1,0:T(4,128)(2,1)}, bf16[4,7168]{1,0:T(4,128)(2,1)S(1)}, u32[]{:S(2)}, u32[]{:S(2)}) collective-permute-start(bf16[4,7168]{1,0:T(4,128)(2,1)} %refs_0_.1), channel_id=1, source_target_pairs={{0,2},{1,3},{2,0},{3,1},{4,6},{5,7},{6,4},{7,5},{8,10},{9,11},{10,... | collective-permute-start | bytes 172040 | tf_op jit(solution)/shard_map/ppermute | solution.py:18
  8.5 3.5 %collective-permute-start.7 = (bf16[4,7168]{1,0:T(4,128)(2,1)}, bf16[4,7168]{1,0:T(4,128)(2,1)S(1)}, u32[]{:S(2)}, u32[]{:S(2)}) collective-permute-start(bf16[4,7168]{1,0:T(4,128)(2,1)} %refs_0_.1), channel_id=1, source_target_pairs={{0,1},{1,0},{2,3},{3,2},{4,5},{5,4},{6,7},{7,6},{8,9},{9,8},{10,11... | collective-permute-start | bytes 172040 | tf_op jit(solution)/shard_map/ppermute | solution.py:23
  8.5 4.8 %collective-permute-start.2 = (bf16[4,7168]{1,0:T(4,128)(2,1)S(1)}, bf16[4,7168]{1,0:T(4,128)(2,1)S(1)}, u32[]{:S(2)}, u32[]{:S(2)}) collective-permute-start(bf16[4,7168]{1,0:T(4,128)(2,1)S(1)} %collective-permute-done.1.refs_2_), channel_id=1, source_target_pairs={{0,2},{1,3},{2,0},{3,1},{4,6},{5,7},{6,4},{7,5},{8,10},{9,11},{10,... | collective-permute-start | bytes 172040 | tf_op jit(solution)/shard_map/ppermute | solution.py:18
  9.9 4.8 %collective-permute-start.4 = (bf16[4,7168]{1,0:T(4,128)(2,1)S(1)}, bf16[4,7168]{1,0:T(4,128)(2,1)S(1)}, u32[]{:S(2)}, u32[]{:S(2)}) collective-permute-start(bf16[4,7168]{1,0:T(4,128)(2,1)S(1)} %collective-permute-done.3.refs_4_), channel_id=1, source_target_pairs={{0,2},{1,3},{2,0},{3,1},{4,6},{5,7},{6,4},{7,5},{8,10},{9,11},{10,... | collective-permute-start | bytes 172040 | tf_op jit(solution)/shard_map/ppermute | solution.py:18
  11.6 4.2 %collective-permute-start.6 = (bf16[4,7168]{1,0:T(4,128)(2,1)S(1)}, bf16[4,7168]{1,0:T(4,128)(2,1)S(1)}, u32[]{:S(2)}, u32[]{:S(2)}) collective-permute-start(bf16[4,7168]{1,0:T(4,128)(2,1)S(1)} %collective-permute-done.5.refs_6_), channel_id=1, source_target_pairs={{0,2},{1,3},{2,0},{3,1},{4,6},{5,7},{6,4},{7,5},{8,10},{9,11},{10,... | collective-permute-start | bytes 172040 | tf_op jit(solution)/shard_map/ppermute | solution.py:18
  11.9 3.9 %collective-permute-start.11 = (bf16[4,7168]{1,0:T(4,128)(2,1)S(1)}, bf16[4,7168]{1,0:T(4,128)(2,1)S(1)}, u32[]{:S(2)}, u32[]{:S(2)}) collective-permute-start(bf16[4,7168]{1,0:T(4,128)(2,1)S(1)} %collective-permute-done.3.refs_4_), channel_id=1, source_target_pairs={{0,1},{1,0},{2,3},{3,2},{4,5},{5,4},{6,7},{7,6},{8,9},{9,8},{10,11... | collective-permute-start | bytes 172040 | tf_op jit(solution)/shard_map/ppermute | solution.py:23
  11.9 4.4 %collective-permute-start.13 = (bf16[4,7168]{1,0:T(4,128)(2,1)S(1)}, bf16[4,7168]{1,0:T(4,128)(2,1)S(1)}, u32[]{:S(2)}, u32[]{:S(2)}) collective-permute-start(bf16[4,7168]{1,0:T(4,128)(2,1)S(1)} %collective-permute-done.5.refs_6_), channel_id=1, source_target_pairs={{0,1},{1,0},{2,3},{3,2},{4,5},{5,4},{6,7},{7,6},{8,9},{9,8},{10,11... | collective-permute-start | bytes 172040 | tf_op jit(solution)/shard_map/ppermute | solution.py:23
  13.3 9.4 %collective-permute-start.9 = (bf16[4,7168]{1,0:T(4,128)(2,1)S(1)}, bf16[4,7168]{1,0:T(4,128)(2,1)S(1)}, u32[]{:S(2)}, u32[]{:S(2)}) collective-permute-start(bf16[4,7168]{1,0:T(4,128)(2,1)S(1)} %collective-permute-done.1.refs_2_), channel_id=1, source_target_pairs={{0,1},{1,0},{2,3},{3,2},{4,5},{5,4},{6,7},{7,6},{8,9},{9,8},{10,11... | collective-permute-start | bytes 172040 | tf_op jit(solution)/shard_map/ppermute | solution.py:23
  14.7 8.0 %collective-permute-start.8 = (bf16[4,7168]{1,0:T(4,128)(2,1)S(1)}, bf16[4,7168]{1,0:T(4,128)(2,1)S(1)}, u32[]{:S(2)}, u32[]{:S(2)}) collective-permute-start(bf16[4,7168]{1,0:T(4,128)(2,1)S(1)} %collective-permute-done.refs_1_), channel_id=1, source_target_pairs={{0,1},{1,0},{2,3},{3,2},{4,5},{5,4},{6,7},{7,6},{8,9},{9,8},{10,11... | collective-permute-start | bytes 172040 | tf_op jit(solution)/shard_map/ppermute | solution.py:23
  15.8 6.9 %collective-permute-start.10 = (bf16[4,7168]{1,0:T(4,128)(2,1)S(1)}, bf16[4,7168]{1,0:T(4,128)(2,1)S(1)}, u32[]{:S(2)}, u32[]{:S(2)}) collective-permute-start(bf16[4,7168]{1,0:T(4,128)(2,1)S(1)} %collective-permute-done.2.refs_3_), channel_id=1, source_target_pairs={{0,1},{1,0},{2,3},{3,2},{4,5},{5,4},{6,7},{7,6},{8,9},{9,8},{10,11... | collective-permute-start | bytes 172040 | tf_op jit(solution)/shard_map/ppermute | solution.py:23
  15.8 6.9 %collective-permute-start.12 = (bf16[4,7168]{1,0:T(4,128)(2,1)S(1)}, bf16[4,7168]{1,0:T(4,128)(2,1)S(1)}, u32[]{:S(2)}, u32[]{:S(2)}) collective-permute-start(bf16[4,7168]{1,0:T(4,128)(2,1)S(1)} %collective-permute-done.4.refs_5_), channel_id=1, source_target_pairs={{0,1},{1,0},{2,3},{3,2},{4,5},{5,4},{6,7},{7,6},{8,9},{9,8},{10,11... | collective-permute-start | bytes 172040 | tf_op jit(solution)/shard_map/ppermute | solution.py:23
  16.3 6.4 %collective-permute-start.14 = (bf16[4,7168]{1,0:T(4,128)(2,1)S(1)}, bf16[4,7168]{1,0:T(4,128)(2,1)S(1)}, u32[]{:S(2)}, u32[]{:S(2)}) collective-permute-start(bf16[4,7168]{1,0:T(4,128)(2,1)S(1)} %collective-permute-done.6.refs_7_), channel_id=1, source_target_pairs={{0,1},{1,0},{2,3},{3,2},{4,5},{5,4},{6,7},{7,6},{8,9},{9,8},{10,11... | collective-permute-start | bytes 172040 | tf_op jit(solution)/shard_map/ppermute | solution.py:23
  22.7 6.1 %copy-start.1 = (s32[4,2]{0,1:T(2,128)S(1)}, s32[4,2]{0,1:T(2,128)}, u32[]{:S(2)}) copy-start(s32[4,2]{0,1:T(2,128)} %param.7) | copy-start | bytes 100
  22.7 6.2 %copy-start.2 = (s32[4,2]{0,1:T(2,128)S(1)}, s32[4,2]{0,1:T(2,128)}, u32[]{:S(2)}) copy-start(s32[4,2]{0,1:T(2,128)} %param.8) | copy-start | bytes 100
  28.3 1.7 %collective-permute-start.27 = (bf16[4,7168]{1,0:T(4,128)(2,1)S(1)}, bf16[4,7168]{1,0:T(4,128)(2,1)S(1)}, u32[]{:S(2)}, u32[]{:S(2)}) collective-permute-start(bf16[4,7168]{1,0:T(4,128)(2,1)S(1)} %get-tuple-element.40), channel_id=1, source_target_pairs={{0,1},{1,0},{2,3},{3,2},{4,5},{5,4},{6,7},{7,6},{8,9},{9,8},{10,11... | collective-permute-start | bytes 172040 | tf_op jit(solution)/shard_map/ppermute | solution.py:23
  29.0 3.3 %collective-permute-start.26 = (bf16[4,7168]{1,0:T(4,128)(2,1)S(1)}, bf16[4,7168]{1,0:T(4,128)(2,1)S(1)}, u32[]{:S(2)}, u32[]{:S(2)}) collective-permute-start(bf16[4,7168]{1,0:T(4,128)(2,1)S(1)} %get-tuple-element.38), channel_id=1, source_target_pairs={{0,1},{1,0},{2,3},{3,2},{4,5},{5,4},{6,7},{7,6},{8,9},{9,8},{10,11... | collective-permute-start | bytes 172040 | tf_op jit(solution)/shard_map/ppermute | solution.py:23
  29.1 1.3 %collective-permute-start.23 = (bf16[4,7168]{1,0:T(4,128)(2,1)S(1)}, bf16[4,7168]{1,0:T(4,128)(2,1)S(1)}, u32[]{:S(2)}, u32[]{:S(2)}) collective-permute-start(bf16[4,7168]{1,0:T(4,128)(2,1)S(1)} %get-tuple-element.36), channel_id=1, source_target_pairs={{0,1},{1,0},{2,3},{3,2},{4,5},{5,4},{6,7},{7,6},{8,9},{9,8},{10,11... | collective-permute-start | bytes 172040 | tf_op jit(solution)/shard_map/ppermute | solution.py:23
  29.5 7.0 %collective-permute-start.22 = (bf16[4,7168]{1,0:T(4,128)(2,1)S(1)}, bf16[4,7168]{1,0:T(4,128)(2,1)S(1)}, u32[]{:S(2)}, u32[]{:S(2)}) collective-permute-start(bf16[4,7168]{1,0:T(4,128)(2,1)S(1)} %get-tuple-element.34), channel_id=1, source_target_pairs={{0,1},{1,0},{2,3},{3,2},{4,5},{5,4},{6,7},{7,6},{8,9},{9,8},{10,11... | collective-permute-start | bytes 172040 | tf_op jit(solution)/shard_map/ppermute | solution.py:23
  29.6 1.3 %collective-permute-start.19 = (bf16[4,7168]{1,0:T(4,128)(2,1)S(1)}, bf16[4,7168]{1,0:T(4,128)(2,1)S(1)}, u32[]{:S(2)}, u32[]{:S(2)}) collective-permute-start(bf16[4,7168]{1,0:T(4,128)(2,1)S(1)} %get-tuple-element.32), channel_id=1, source_target_pairs={{0,1},{1,0},{2,3},{3,2},{4,5},{5,4},{6,7},{7,6},{8,9},{9,8},{10,11... | collective-permute-start | bytes 172040 | tf_op jit(solution)/shard_map/ppermute | solution.py:23
  30.0 8.6 %collective-permute-start.18 = (bf16[4,7168]{1,0:T(4,128)(2,1)S(1)}, bf16[4,7168]{1,0:T(4,128)(2,1)S(1)}, u32[]{:S(2)}, u32[]{:S(2)}) collective-permute-start(bf16[4,7168]{1,0:T(4,128)(2,1)S(1)} %get-tuple-element.30), channel_id=1, source_target_pairs={{0,1},{1,0},{2,3},{3,2},{4,5},{5,4},{6,7},{7,6},{8,9},{9,8},{10,11... | collective-permute-start | bytes 172040 | tf_op jit(solution)/shard_map/ppermute | solution.py:23
  30.4 1.2 %collective-permute-start.16 = (bf16[4,7168]{1,0:T(4,128)(2,1)S(1)}, bf16[4,7168]{1,0:T(4,128)(2,1)S(1)}, u32[]{:S(2)}, u32[]{:S(2)}) collective-permute-start(bf16[4,7168]{1,0:T(4,128)(2,1)S(1)} %get-tuple-element.28), channel_id=1, source_target_pairs={{0,1},{1,0},{2,3},{3,2},{4,5},{5,4},{6,7},{7,6},{8,9},{9,8},{10,11... | collective-permute-start | bytes 172040 | tf_op jit(solution)/shard_map/ppermute | solution.py:23
  30.9 11.9 %collective-permute-start.15 = (bf16[4,7168]{1,0:T(4,128)(2,1)S(1)}, bf16[4,7168]{1,0:T(4,128)(2,1)S(1)}, u32[]{:S(2)}, u32[]{:S(2)}) collective-permute-start(bf16[4,7168]{1,0:T(4,128)(2,1)S(1)} %get-tuple-element.26), channel_id=1, source_target_pairs={{0,1},{1,0},{2,3},{3,2},{4,5},{5,4},{6,7},{7,6},{8,9},{9,8},{10,11... | collective-permute-start | bytes 172040 | tf_op jit(solution)/shard_map/ppermute | solution.py:23
  31.7 4.8 %collective-permute-start.28 = (bf16[4,7168]{1,0:T(4,128)(2,1)S(1)}, bf16[4,7168]{1,0:T(4,128)(2,1)S(1)}, u32[]{:S(2)}, u32[]{:S(2)}) collective-permute-start(bf16[4,7168]{1,0:T(4,128)(2,1)S(1)} %add_convert_fusion.1), channel_id=1, source_target_pairs={{0,2},{1,3},{2,0},{3,1},{4,6},{5,7},{6,4},{7,5},{8,10},{9,11},{10,... | collective-permute-start | bytes 172040 | tf_op jit(solution)/shard_map/ppermute | solution.py:18
  32.3 6.3 %collective-permute-start.24 = (bf16[4,7168]{1,0:T(4,128)(2,1)S(1)}, bf16[4,7168]{1,0:T(4,128)(2,1)S(1)}, u32[]{:S(2)}, u32[]{:S(2)}) collective-permute-start(bf16[4,7168]{1,0:T(4,128)(2,1)S(1)} %add_convert_fusion.3), channel_id=1, source_target_pairs={{0,2},{1,3},{2,0},{3,1},{4,6},{5,7},{6,4},{7,5},{8,10},{9,11},{10,... | collective-permute-start | bytes 172040 | tf_op jit(solution)/shard_map/ppermute | solution.py:18
  36.4 5.0 %collective-permute-start.20 = (bf16[4,7168]{1,0:T(4,128)(2,1)S(1)}, bf16[4,7168]{1,0:T(4,128)(2,1)S(1)}, u32[]{:S(2)}, u32[]{:S(2)}) collective-permute-start(bf16[4,7168]{1,0:T(4,128)(2,1)S(1)} %add_convert_fusion.5), channel_id=1, source_target_pairs={{0,2},{1,3},{2,0},{3,1},{4,6},{5,7},{6,4},{7,5},{8,10},{9,11},{10,... | collective-permute-start | bytes 172040 | tf_op jit(solution)/shard_map/ppermute | solution.py:18
  36.5 6.3 %collective-permute-start.17 = (bf16[4,7168]{1,0:T(4,128)(2,1)S(1)}, bf16[4,7168]{1,0:T(4,128)(2,1)S(1)}, u32[]{:S(2)}, u32[]{:S(2)}) collective-permute-start(bf16[4,7168]{1,0:T(4,128)(2,1)S(1)} %add_convert_fusion.7), channel_id=1, source_target_pairs={{0,2},{1,3},{2,0},{3,1},{4,6},{5,7},{6,4},{7,5},{8,10},{9,11},{10,... | collective-permute-start | bytes 172040 | tf_op jit(solution)/shard_map/ppermute | solution.py:18
  38.6 6.0 %collective-permute-start.29 = (bf16[4,7168]{1,0:T(4,128)(2,1)S(1)}, bf16[4,7168]{1,0:T(4,128)(2,1)S(1)}, u32[]{:S(2)}, u32[]{:S(2)}) collective-permute-start(bf16[4,7168]{1,0:T(4,128)(2,1)S(1)} %add_convert_fusion), channel_id=1, source_target_pairs={{0,4},{4,8},{8,12},{12,0},{1,5},{5,9},{9,13},{13,1},{2,6},{6,10},{... | collective-permute-start | bytes 172040 | tf_op jit(solution)/shard_map/ppermute | solution.py:18
  38.7 5.9 %collective-permute-start.25 = (bf16[4,7168]{1,0:T(4,128)(2,1)S(1)}, bf16[4,7168]{1,0:T(4,128)(2,1)S(1)}, u32[]{:S(2)}, u32[]{:S(2)}) collective-permute-start(bf16[4,7168]{1,0:T(4,128)(2,1)S(1)} %add_convert_fusion.2), channel_id=1, source_target_pairs={{0,8},{4,12},{8,0},{12,4},{1,9},{5,13},{9,1},{13,5},{2,10},{6,14},... | collective-permute-start | bytes 172040 | tf_op jit(solution)/shard_map/ppermute | solution.py:18
  41.5 4.2 %collective-permute-start.21 = (bf16[4,7168]{1,0:T(4,128)(2,1)S(1)}, bf16[4,7168]{1,0:T(4,128)(2,1)S(1)}, u32[]{:S(2)}, u32[]{:S(2)}) collective-permute-start(bf16[4,7168]{1,0:T(4,128)(2,1)S(1)} %add_convert_fusion.4), channel_id=1, source_target_pairs={{0,12},{4,0},{8,4},{12,8},{1,13},{5,1},{9,5},{13,9},{2,14},{6,2},{... | collective-permute-start | bytes 172040 | tf_op jit(solution)/shard_map/ppermute | solution.py:18
  (1 other events, 2.7 us)

commit v2 on v1

--- a/solution.py
+++ b/solution.py
@@ -10,7 +10,7 @@
 
 CORES = 2
 MIB = 1 << 20
-VMEM_BYTES = 58 * MIB
+VMEM_BYTES = 62 * MIB
 
 
 def shift(value, axis, amount):
@@ -23,64 +23,31 @@
     return lax.ppermute(value, "tok", [(i, i ^ 1) for i in range(size)])
 
 
-def fetch_all(pairs, semaphores):
-    copies = [pltpu.make_async_copy(s, t, semaphores.at[i]) for i, (s, t) in enumerate(pairs)]
-    for copy in copies:
-        copy.start()
-    for copy in copies:
-        copy.wait()
+def enter_kernel(gate_ref, up_ref, out_ref):
+    out_ref[...] = jnp.zeros_like(out_ref)
 
 
-def open_kernel(cut, gate_ref, up_ref, gate_out, up_out, semaphores):
-    pairs = [(gate_ref, gate_out)]
-    if cut:
-        pairs.append((up_ref.at[pl.ds(0, cut)], up_out.at[pl.ds(0, cut)]))
-    fetch_all(pairs, semaphores)
-
-
-def rest_kernel(cut, held_ref, up_ref, up_out, semaphores):
-    span = pl.ds(cut, up_ref.shape[0] - cut)
-    fetch_all([(up_ref.at[span], up_out.at[span])], semaphores)
+def enter(gate_w, up_w):
+    hbm = pl.BlockSpec(memory_space=pl.ANY)
+    return pl.pallas_call(
+        enter_kernel,
+        out_shape=jax.ShapeDtypeStruct((8, 128), jnp.float32),
+        in_specs=[hbm, hbm],
+        out_specs=pl.BlockSpec(memory_space=pltpu.VMEM),
+        compiler_params=pltpu.CompilerParams(vmem_limit_bytes=VMEM_BYTES - 4 * gate_w.size - int(0.75 * MIB)),
+        name="enter",
+    )(gate_w, up_w)
 
 
 def kernel_limit(weight, extra=0):
-    return VMEM_BYTES - 4 * weight.size - 6 * MIB + extra * MIB
-
-
-def load_open(gate_w, up_w, cut):
-    hbm = pl.BlockSpec(memory_space=pltpu.HBM)
-    vmem = pl.BlockSpec(memory_space=pltpu.VMEM)
-    return pl.pallas_call(
-        functools.partial(open_kernel, cut),
-        out_shape=[jax.ShapeDtypeStruct(w.shape, w.dtype) for w in (gate_w, up_w)],
-        in_specs=[hbm, hbm],
-        out_specs=[vmem, vmem],
-        scratch_shapes=[pltpu.SemaphoreType.DMA((2,))],
-        compiler_params=pltpu.CompilerParams(vmem_limit_bytes=kernel_limit(gate_w)),
-        name="load_open",
-    )(gate_w, up_w)
-
-
-def load_rest(held, up_w, cut):
-    hbm = pl.BlockSpec(memory_space=pltpu.HBM)
-    vmem = pl.BlockSpec(memory_space=pltpu.VMEM)
-    return pl.pallas_call(
-        functools.partial(rest_kernel, cut),
-        out_shape=jax.ShapeDtypeStruct(up_w.shape, up_w.dtype),
-        in_specs=[vmem, hbm],
-        out_specs=vmem,
-        input_output_aliases={0: 0},
-        scratch_shapes=[pltpu.SemaphoreType.DMA((2,))],
-        compiler_params=pltpu.CompilerParams(vmem_limit_bytes=kernel_limit(up_w, 3)),
-        name="load_rest",
-    )(held, up_w)
+    return VMEM_BYTES - 4 * weight.size - 15 * MIB + extra * MIB
 
 
 def ffn_kernel(count, depth, width, *refs):
     chunks = refs[:count]
-    gate_ref, up_ref, down_ref = refs[count:count + 3]
-    outs = refs[count + 3:2 * count + 3]
-    gate_sum, up_sum, hidden, down_vmem, semaphore = refs[2 * count + 3:]
+    gate_ref, up_ref, down_ref, _ = refs[count:count + 4]
+    outs = refs[count + 4:2 * count + 4]
+    gate_sum, up_sum, hidden, down_vmem, semaphore = refs[2 * count + 4:]
     fetch = pltpu.make_async_copy(down_ref, down_vmem, semaphore)
     fetch.start()
     rows, model = chunks[0].shape
@@ -110,7 +77,7 @@
     lax.fori_loop(0, model // width, expand, 0)
 
 
-def ffn(chunks, gate_w, up_w, down_w):
+def ffn(chunks, gate_w, up_w, down_w, entered):
     count = len(chunks)
     rows, model = chunks[0].shape
     units = gate_w.shape[1]
@@ -120,7 +87,7 @@
     return pl.pallas_call(
         functools.partial(ffn_kernel, count, block, block),
         out_shape=[jax.ShapeDtypeStruct((rows, model), jnp.bfloat16)] * count,
-        in_specs=[vmem] * (count + 2) + [pl.BlockSpec(memory_space=pltpu.HBM)],
+        in_specs=[vmem] * (count + 2) + [pl.BlockSpec(memory_space=pl.ANY)] * 2,
         out_specs=[vmem] * count,
         scratch_shapes=[
             pltpu.VMEM((total, units), jnp.float32),
@@ -136,7 +103,7 @@
             transcendentals=total * units,
         ),
         name="ffn",
-    )(*chunks, gate_w, up_w, down_w)
+    )(*chunks, gate_w, up_w, down_w, entered)
 
 
 def combine_kernel(ids_ref, gate_ref, *refs):
@@ -168,6 +135,7 @@
 def per_device(tokens, expert_ids, gate_fixed, w_gate, w_up, w_down):
     n_ep = lax.axis_size("ep")
     n_x = lax.axis_size("tok") // CORES
+    entered = enter(w_gate[0], w_up[0])
     columns = [tokens]
     for k in range(1, n_ep):
         columns.append(shift(tokens, "ep", k))
@@ -178,9 +146,7 @@
     mirrored = []
     for n, chunk in enumerate(planes):
         mirrored.append(core_swap(chunk))
-    gate_w, held = load_open(w_gate[0], w_up[0], w_up.shape[1] // 4)
-    up_w = load_rest(held, w_up[0], w_up.shape[1] // 4)
-    parts = ffn(planes + mirrored, gate_w, up_w, w_down[0])
+    parts = ffn(planes + mirrored, w_gate[0], w_up[0], w_down[0], entered)
     half = len(planes)
     terms = []
     for k in range(n_ep):

time: 46.7 us -> 46.4 us (level)
  Pallas kernels: 12.7 us -> 6.47 us
  local copies, waits for them, and re-layouts: 0.2 us -> 5.01 us
  waiting for transfers between devices: 9.97 us -> 11.1 us
    pallas_call x2 -> x1, Pallas kernels: 6.23 us -> 0.01 us  [enter(): pl.pallas_call(enter_kernel, out_shape=jax.ShapeDtypeStruct((8, 128), jnp...]
    unnamed x8 -> x12, local copies, waits for them, and re-layouts: 0.2 us -> 5.01 us
    ppermute x16, waiting for transfers between devices: 0.77 us -> 1.92 us  [core_swap(): return lax.ppermute(value, 'tok', [(i, i ^ 1) for i in range(size)])]
  transfers between devices with their start and end apart: 30 -> 30, of which waited for: 10 -> 13; matrix products, arithmetic and copies ran while one was open for 1% -> 1% of each run, Pallas kernels for 13% -> 0%
where the time goes in v2:
time: 46.4 us; the launch traced here: 46.2 us
  starting transfers between devices  23.2 us (50%)
  waiting for transfers between devices  11.1 us (24%)
  Pallas kernels  6.47 us (14%)
  local copies, waits for them, and re-layouts  5.01 us (11%)
    ppermute x14, starting transfers between devices, shift(): lax.ppermute(value, axis, [(i, (i + amount) % size) for i in range(size)])  19.8 us
    ppermute x14, waiting for transfers between devices, shift(): lax.ppermute(value, axis, [(i, (i + amount) % size) for i in range(size)])  9.19 us
    pallas_call x1, Pallas kernels, ffn(): pl.pallas_call(functools.partial(ffn_kernel, count, block, block), out_sh...  5.59 us
    unnamed x12, local copies, waits for them, and re-layouts  5.01 us
    ppermute x16, starting transfers between devices, core_swap(): return lax.ppermute(value, 'tok', [(i, i ^ 1) for i in range(size)])  3.39 us
    ppermute x16, waiting for transfers between devices, core_swap(): return lax.ppermute(value, 'tok', [(i, i ^ 1) for i in range(size)])  1.92 us
  transfers between devices with their start and end apart: 30, of which 13 were waited for; matrix products, arithmetic and copies ran while one was open for 1% of the time, Pallas kernels for 0%

profile of v2, /device:TPU:0, one launch (start us, length us, event | category | flops | bytes accessed | tf_op | source)
XLA Modules:
  0.0 46.2 jit_solution(15957345688289403658)
XLA Ops:
  0.0 3.1 %collective-permute-start.1 = (bf16[4,7168]{1,0:T(4,128)(2,1)}, bf16[4,7168]{1,0:T(4,128)(2,1)S(1)}, u32[]{:S(2)}, u32[]{:S(2)}) collective-permute-start(bf16[4,7168]{1,0:T(4,128)(2,1)} %refs_0_.1), channel_id=1, source_target_pairs={{0,4},{4,8},{8,12},{12,0},{1,5},{5,9},{9,13},{13,1},{2,6},{6,10},{... | collective-permute-start | bytes 172040 | tf_op jit(solution)/shard_map/ppermute | solution.py:18
  3.1 2.6 %collective-permute-start.3 = (bf16[4,7168]{1,0:T(4,128)(2,1)}, bf16[4,7168]{1,0:T(4,128)(2,1)S(1)}, u32[]{:S(2)}, u32[]{:S(2)}) collective-permute-start(bf16[4,7168]{1,0:T(4,128)(2,1)} %refs_0_.1), channel_id=1, source_target_pairs={{0,8},{4,12},{8,0},{12,4},{1,9},{5,13},{9,1},{13,5},{2,10},{6,14},... | collective-permute-start | bytes 172040 | tf_op jit(solution)/shard_map/ppermute | solution.py:18
  5.6 1.3 %collective-permute-start.5 = (bf16[4,7168]{1,0:T(4,128)(2,1)}, bf16[4,7168]{1,0:T(4,128)(2,1)S(1)}, u32[]{:S(2)}, u32[]{:S(2)}) collective-permute-start(bf16[4,7168]{1,0:T(4,128)(2,1)} %refs_0_.1), channel_id=1, source_target_pairs={{0,12},{4,0},{8,4},{12,8},{1,13},{5,1},{9,5},{13,9},{2,14},{6,2},{... | collective-permute-start | bytes 172040 | tf_op jit(solution)/shard_map/ppermute | solution.py:18
  7.0 1.5 %collective-permute-start = (bf16[4,7168]{1,0:T(4,128)(2,1)}, bf16[4,7168]{1,0:T(4,128)(2,1)S(1)}, u32[]{:S(2)}, u32[]{:S(2)}) collective-permute-start(bf16[4,7168]{1,0:T(4,128)(2,1)} %refs_0_.1), channel_id=1, source_target_pairs={{0,2},{1,3},{2,0},{3,1},{4,6},{5,7},{6,4},{7,5},{8,10},{9,11},{10,... | collective-permute-start | bytes 172040 | tf_op jit(solution)/shard_map/ppermute | solution.py:18
  8.5 1.0 %collective-permute-start.2 = (bf16[4,7168]{1,0:T(4,128)(2,1)S(1)}, bf16[4,7168]{1,0:T(4,128)(2,1)S(1)}, u32[]{:S(2)}, u32[]{:S(2)}) collective-permute-start(bf16[4,7168]{1,0:T(4,128)(2,1)S(1)} %collective-permute-done.1.refs_2_), channel_id=1, source_target_pairs={{0,2},{1,3},{2,0},{3,1},{4,6},{5,7},{6,4},{7,5},{8,10},{9,11},{10,... | collective-permute-start | bytes 172040 | tf_op jit(solution)/shard_map/ppermute | solution.py:18
  9.5 0.4 collective-permute-done.3.refs_4_
  9.9 1.7 %collective-permute-start.4 = (bf16[4,7168]{1,0:T(4,128)(2,1)S(1)}, bf16[4,7168]{1,0:T(4,128)(2,1)S(1)}, u32[]{:S(2)}, u32[]{:S(2)}) collective-permute-start(bf16[4,7168]{1,0:T(4,128)(2,1)S(1)} %collective-permute-done.3.refs_4_), channel_id=1, source_target_pairs={{0,2},{1,3},{2,0},{3,1},{4,6},{5,7},{6,4},{7,5},{8,10},{9,11},{10,... | collective-permute-start | bytes 172040 | tf_op jit(solution)/shard_map/ppermute | solution.py:18
  11.9 0.5 %collective-permute-start.13 = (bf16[4,7168]{1,0:T(4,128)(2,1)S(1)}, bf16[4,7168]{1,0:T(4,128)(2,1)S(1)}, u32[]{:S(2)}, u32[]{:S(2)}) collective-permute-start(bf16[4,7168]{1,0:T(4,128)(2,1)S(1)} %collective-permute-done.5.refs_6_), channel_id=1, source_target_pairs={{0,1},{1,0},{2,3},{3,2},{4,5},{5,4},{6,7},{7,6},{8,9},{9,8},{10,11... | collective-permute-start | bytes 172040 | tf_op jit(solution)/shard_map/ppermute | solution.py:23
  12.4 0.8 %collective-permute-done.2.refs_3_ = bf16[4,7168]{1,0:T(4,128)(2,1)S(1)} collective-permute-done((bf16[4,7168]{1,0:T(4,128)(2,1)S(1)}, bf16[4,7168]{1,0:T(4,128)(2,1)S(1)}, u32[]{:S(2)}, u32[]{:S(2)}) %collective-permute-start.2) | collective-permute-done | bytes 57376 | tf_op jit(solution)/shard_map/ppermute | solution.py:18
  13.3 1.4 %collective-permute-done.4.refs_5_ = bf16[4,7168]{1,0:T(4,128)(2,1)S(1)} collective-permute-done((bf16[4,7168]{1,0:T(4,128)(2,1)S(1)}, bf16[4,7168]{1,0:T(4,128)(2,1)S(1)}, u32[]{:S(2)}, u32[]{:S(2)}) %collective-permute-start.4) | collective-permute-done | bytes 57376 | tf_op jit(solution)/shard_map/ppermute | solution.py:18
  14.7 1.1 %collective-permute-done.6.refs_7_ = bf16[4,7168]{1,0:T(4,128)(2,1)S(1)} collective-permute-done((bf16[4,7168]{1,0:T(4,128)(2,1)S(1)}, bf16[4,7168]{1,0:T(4,128)(2,1)S(1)}, u32[]{:S(2)}, u32[]{:S(2)}) %collective-permute-start.6) | collective-permute-done | bytes 57376 | tf_op jit(solution)/shard_map/ppermute | solution.py:18
  15.8 0.5 %collective-permute-start.12 = (bf16[4,7168]{1,0:T(4,128)(2,1)S(1)}, bf16[4,7168]{1,0:T(4,128)(2,1)S(1)}, u32[]{:S(2)}, u32[]{:S(2)}) collective-permute-start(bf16[4,7168]{1,0:T(4,128)(2,1)S(1)} %collective-permute-done.4.refs_5_), channel_id=1, source_target_pairs={{0,1},{1,0},{2,3},{3,2},{4,5},{5,4},{6,7},{7,6},{8,9},{9,8},{10,11... | collective-permute-start | bytes 172040 | tf_op jit(solution)/shard_map/ppermute | solution.py:23
  16.4 0.6 %collective-permute-done.10.refs_11_ = bf16[4,7168]{1,0:T(4,128)(2,1)S(1)} collective-permute-done((bf16[4,7168]{1,0:T(4,128)(2,1)S(1)}, bf16[4,7168]{1,0:T(4,128)(2,1)S(1)}, u32[]{:S(2)}, u32[]{:S(2)}) %collective-permute-start.10) | collective-permute-done | bytes 57376 | tf_op jit(solution)/shard_map/ppermute | solution.py:23
  17.2 0.4 collective-permute-done.14.refs_15_
  17.6 1.9 %copy-done = bf16[1,7168,512]{2,1,0:T(8,128)(2,1)S(1)} copy-done((bf16[1,7168,512]{2,1,0:T(8,128)(2,1)S(1)}, bf16[1,7168,512]{2,1,0:T(8,128)(2,1)}, u32[]{:S(2)}) %copy-start) | copy-done | bytes 7340056
  19.5 2.1 %copy-done.1 = bf16[1,7168,512]{2,1,0:T(8,128)(2,1)S(1)} copy-done((bf16[1,7168,512]{2,1,0:T(8,128)(2,1)S(1)}, bf16[1,7168,512]{2,1,0:T(8,128)(2,1)}, u32[]{:S(2)}) %copy-start.1) | copy-done | bytes 7340056
  21.6 0.8 %copy-done.2 = bf16[4,7168]{1,0:T(4,128)(2,1)S(1)} copy-done((bf16[4,7168]{1,0:T(4,128)(2,1)S(1)}, bf16[4,7168]{1,0:T(4,128)(2,1)}, u32[]{:S(2)}) %copy-start.2) | copy-done | bytes 57368
  22.4 5.6 %ffn.1 = (bf16[4,7168]{1,0:T(4,128)(2,1)S(1)}, bf16[4,7168]{1,0:T(4,128)(2,1)S(1)}, bf16[4,7168]{1,0:T(4,128)(2,1)S(1)}, bf16[4,7168]{1,0:T(4,128)(2,1)S(1)}, bf...) custom-call(bf16[4,7168]{1,0:T(4,128)(2,1)S(1)} %copy-done.2, ...), custom_call_target="tpu_custom_call" | custom-call | flops 1409286144 | bytes 23855104 | tf_op jit(solution)/shard_map/ffn/pallas_call | solution.py:87
  28.0 0.5 %collective-permute-start.27 = (bf16[4,7168]{1,0:T(4,128)(2,1)S(1)}, bf16[4,7168]{1,0:T(4,128)(2,1)S(1)}, u32[]{:S(2)}, u32[]{:S(2)}) collective-permute-start(bf16[4,7168]{1,0:T(4,128)(2,1)S(1)} %get-tuple-element.36), channel_id=1, source_target_pairs={{0,1},{1,0},{2,3},{3,2},{4,5},{5,4},{6,7},{7,6},{8,9},{9,8},{10,11... | collective-permute-start | bytes 172040 | tf_op jit(solution)/shard_map/ppermute | solution.py:23
  28.7 0.4 collective-permute-start.23
  29.3 0.4 collective-permute-start.19
  30.1 0.4 collective-permute-start.16
  30.6 0.4 collective-permute-start.15
  31.3 0.6 %collective-permute-start.28 = (bf16[4,7168]{1,0:T(4,128)(2,1)S(1)}, bf16[4,7168]{1,0:T(4,128)(2,1)S(1)}, u32[]{:S(2)}, u32[]{:S(2)}) collective-permute-start(bf16[4,7168]{1,0:T(4,128)(2,1)S(1)} %add_convert_fusion.1), channel_id=1, source_target_pairs={{0,2},{1,3},{2,0},{3,1},{4,6},{5,7},{6,4},{7,5},{8,10},{9,11},{10,... | collective-permute-start | bytes 172040 | tf_op jit(solution)/shard_map/ppermute | solution.py:18
  32.0 1.5 %collective-permute-start.24 = (bf16[4,7168]{1,0:T(4,128)(2,1)S(1)}, bf16[4,7168]{1,0:T(4,128)(2,1)S(1)}, u32[]{:S(2)}, u32[]{:S(2)}) collective-permute-start(bf16[4,7168]{1,0:T(4,128)(2,1)S(1)} %add_convert_fusion.3), channel_id=1, source_target_pairs={{0,2},{1,3},{2,0},{3,1},{4,6},{5,7},{6,4},{7,5},{8,10},{9,11},{10,... | collective-permute-start | bytes 172040 | tf_op jit(solution)/shard_map/ppermute | solution.py:18
  33.5 2.6 %collective-permute-done.28 = bf16[4,7168]{1,0:T(4,128)(2,1)S(1)} collective-permute-done((bf16[4,7168]{1,0:T(4,128)(2,1)S(1)}, bf16[4,7168]{1,0:T(4,128)(2,1)S(1)}, u32[]{:S(2)}, u32[]{:S(2)}) %collective-permute-start.28) | collective-permute-done | bytes 57376 | tf_op jit(solution)/shard_map/ppermute | solution.py:18
  36.2 2.1 %collective-permute-start.17 = (bf16[4,7168]{1,0:T(4,128)(2,1)S(1)}, bf16[4,7168]{1,0:T(4,128)(2,1)S(1)}, u32[]{:S(2)}, u32[]{:S(2)}) collective-permute-start(bf16[4,7168]{1,0:T(4,128)(2,1)S(1)} %add_convert_fusion.7), channel_id=1, source_target_pairs={{0,2},{1,3},{2,0},{3,1},{4,6},{5,7},{6,4},{7,5},{8,10},{9,11},{10,... | collective-permute-start | bytes 172040 | tf_op jit(solution)/shard_map/ppermute | solution.py:18
  38.3 2.7 %collective-permute-start.25 = (bf16[4,7168]{1,0:T(4,128)(2,1)S(1)}, bf16[4,7168]{1,0:T(4,128)(2,1)S(1)}, u32[]{:S(2)}, u32[]{:S(2)}) collective-permute-start(bf16[4,7168]{1,0:T(4,128)(2,1)S(1)} %add_convert_fusion.2), channel_id=1, source_target_pairs={{0,8},{4,12},{8,0},{12,4},{1,9},{5,13},{9,1},{13,5},{2,10},{6,14},... | collective-permute-start | bytes 172040 | tf_op jit(solution)/shard_map/ppermute | solution.py:18
  41.1 1.4 %collective-permute-start.21 = (bf16[4,7168]{1,0:T(4,128)(2,1)S(1)}, bf16[4,7168]{1,0:T(4,128)(2,1)S(1)}, u32[]{:S(2)}, u32[]{:S(2)}) collective-permute-start(bf16[4,7168]{1,0:T(4,128)(2,1)S(1)} %add_convert_fusion.4), channel_id=1, source_target_pairs={{0,12},{4,0},{8,4},{12,8},{1,13},{5,1},{9,5},{13,9},{2,14},{6,2},{... | collective-permute-start | bytes 172040 | tf_op jit(solution)/shard_map/ppermute | solution.py:18
  42.6 1.7 %collective-permute-done.29.refs_3_ = bf16[4,7168]{1,0:T(4,128)(2,1)S(1)} collective-permute-done((bf16[4,7168]{1,0:T(4,128)(2,1)S(1)}, bf16[4,7168]{1,0:T(4,128)(2,1)S(1)}, u32[]{:S(2)}, u32[]{:S(2)}) %collective-permute-start.29) | collective-permute-done | bytes 57376 | tf_op jit(solution)/shard_map/ppermute | solution.py:18
  44.2 1.1 %collective-permute-done.21.refs_1_ = bf16[4,7168]{1,0:T(4,128)(2,1)S(1)} collective-permute-done((bf16[4,7168]{1,0:T(4,128)(2,1)S(1)}, bf16[4,7168]{1,0:T(4,128)(2,1)S(1)}, u32[]{:S(2)}, u32[]{:S(2)}) %collective-permute-start.21) | collective-permute-done | bytes 57376 | tf_op jit(solution)/shard_map/ppermute | solution.py:18
  45.3 0.9 %combine.1 = bf16[4,7168]{1,0:T(4,128)(2,1)} custom-call(s32[4,2]{1,0:T(4,128)S(1)} %copy.7.ids_ref, s32[4,2]{1,0:T(4,128)S(1)} %copy.8.gate_ref, bf16[4,7168]{1,0:T(4,128)(2,1)S(1)} %add_convert_fusion.6.refs_0_, bf16[4,7168]{1,0:T(4,128)(2,1)S(1)} %collective-permute-done.21.refs_1_, bf16[4,7168]{1,0:T(4,128)(2,1)S(1)} %collective-permute-done.25.refs_2_, ...), custom_call_target="tpu_custom_call" | custom-call | tf_op jit(solution)/shard_map/combine/pallas_call | solution.py:125
  (51 shorter events, 2.1 us)
Async XLA Ops:
  0.0 8.5 %collective-permute-start.1 = (bf16[4,7168]{1,0:T(4,128)(2,1)}, bf16[4,7168]{1,0:T(4,128)(2,1)S(1)}, u32[]{:S(2)}, u32[]{:S(2)}) collective-permute-start(bf16[4,7168]{1,0:T(4,128)(2,1)} %refs_0_.1), channel_id=1, source_target_pairs={{0,4},{4,8},{8,12},{12,0},{1,5},{5,9},{9,13},{13,1},{2,6},{6,10},{... | collective-permute-start | bytes 172040 | tf_op jit(solution)/shard_map/ppermute | solution.py:18
  3.1 6.8 %collective-permute-start.3 = (bf16[4,7168]{1,0:T(4,128)(2,1)}, bf16[4,7168]{1,0:T(4,128)(2,1)S(1)}, u32[]{:S(2)}, u32[]{:S(2)}) collective-permute-start(bf16[4,7168]{1,0:T(4,128)(2,1)} %refs_0_.1), channel_id=1, source_target_pairs={{0,8},{4,12},{8,0},{12,4},{1,9},{5,13},{9,1},{13,5},{2,10},{6,14},... | collective-permute-start | bytes 172040 | tf_op jit(solution)/shard_map/ppermute | solution.py:18
  5.6 6.0 %collective-permute-start.5 = (bf16[4,7168]{1,0:T(4,128)(2,1)}, bf16[4,7168]{1,0:T(4,128)(2,1)S(1)}, u32[]{:S(2)}, u32[]{:S(2)}) collective-permute-start(bf16[4,7168]{1,0:T(4,128)(2,1)} %refs_0_.1), channel_id=1, source_target_pairs={{0,12},{4,0},{8,4},{12,8},{1,13},{5,1},{9,5},{13,9},{2,14},{6,2},{... | collective-permute-start | bytes 172040 | tf_op jit(solution)/shard_map/ppermute | solution.py:18
  7.0 4.9 %collective-permute-start = (bf16[4,7168]{1,0:T(4,128)(2,1)}, bf16[4,7168]{1,0:T(4,128)(2,1)S(1)}, u32[]{:S(2)}, u32[]{:S(2)}) collective-permute-start(bf16[4,7168]{1,0:T(4,128)(2,1)} %refs_0_.1), channel_id=1, source_target_pairs={{0,2},{1,3},{2,0},{3,1},{4,6},{5,7},{6,4},{7,5},{8,10},{9,11},{10,... | collective-permute-start | bytes 172040 | tf_op jit(solution)/shard_map/ppermute | solution.py:18
  8.5 3.5 %collective-permute-start.7 = (bf16[4,7168]{1,0:T(4,128)(2,1)}, bf16[4,7168]{1,0:T(4,128)(2,1)S(1)}, u32[]{:S(2)}, u32[]{:S(2)}) collective-permute-start(bf16[4,7168]{1,0:T(4,128)(2,1)} %refs_0_.1), channel_id=1, source_target_pairs={{0,1},{1,0},{2,3},{3,2},{4,5},{5,4},{6,7},{7,6},{8,9},{9,8},{10,11... | collective-permute-start | bytes 172040 | tf_op jit(solution)/shard_map/ppermute | solution.py:23
  8.5 4.8 %collective-permute-start.2 = (bf16[4,7168]{1,0:T(4,128)(2,1)S(1)}, bf16[4,7168]{1,0:T(4,128)(2,1)S(1)}, u32[]{:S(2)}, u32[]{:S(2)}) collective-permute-start(bf16[4,7168]{1,0:T(4,128)(2,1)S(1)} %collective-permute-done.1.refs_2_), channel_id=1, source_target_pairs={{0,2},{1,3},{2,0},{3,1},{4,6},{5,7},{6,4},{7,5},{8,10},{9,11},{10,... | collective-permute-start | bytes 172040 | tf_op jit(solution)/shard_map/ppermute | solution.py:18
  9.9 4.8 %collective-permute-start.4 = (bf16[4,7168]{1,0:T(4,128)(2,1)S(1)}, bf16[4,7168]{1,0:T(4,128)(2,1)S(1)}, u32[]{:S(2)}, u32[]{:S(2)}) collective-permute-start(bf16[4,7168]{1,0:T(4,128)(2,1)S(1)} %collective-permute-done.3.refs_4_), channel_id=1, source_target_pairs={{0,2},{1,3},{2,0},{3,1},{4,6},{5,7},{6,4},{7,5},{8,10},{9,11},{10,... | collective-permute-start | bytes 172040 | tf_op jit(solution)/shard_map/ppermute | solution.py:18
  11.6 4.2 %collective-permute-start.6 = (bf16[4,7168]{1,0:T(4,128)(2,1)S(1)}, bf16[4,7168]{1,0:T(4,128)(2,1)S(1)}, u32[]{:S(2)}, u32[]{:S(2)}) collective-permute-start(bf16[4,7168]{1,0:T(4,128)(2,1)S(1)} %collective-permute-done.5.refs_6_), channel_id=1, source_target_pairs={{0,2},{1,3},{2,0},{3,1},{4,6},{5,7},{6,4},{7,5},{8,10},{9,11},{10,... | collective-permute-start | bytes 172040 | tf_op jit(solution)/shard_map/ppermute | solution.py:18
  11.9 3.9 %collective-permute-start.11 = (bf16[4,7168]{1,0:T(4,128)(2,1)S(1)}, bf16[4,7168]{1,0:T(4,128)(2,1)S(1)}, u32[]{:S(2)}, u32[]{:S(2)}) collective-permute-start(bf16[4,7168]{1,0:T(4,128)(2,1)S(1)} %collective-permute-done.3.refs_4_), channel_id=1, source_target_pairs={{0,1},{1,0},{2,3},{3,2},{4,5},{5,4},{6,7},{7,6},{8,9},{9,8},{10,11... | collective-permute-start | bytes 172040 | tf_op jit(solution)/shard_map/ppermute | solution.py:23
  11.9 4.4 %collective-permute-start.13 = (bf16[4,7168]{1,0:T(4,128)(2,1)S(1)}, bf16[4,7168]{1,0:T(4,128)(2,1)S(1)}, u32[]{:S(2)}, u32[]{:S(2)}) collective-permute-start(bf16[4,7168]{1,0:T(4,128)(2,1)S(1)} %collective-permute-done.5.refs_6_), channel_id=1, source_target_pairs={{0,1},{1,0},{2,3},{3,2},{4,5},{5,4},{6,7},{7,6},{8,9},{9,8},{10,11... | collective-permute-start | bytes 172040 | tf_op jit(solution)/shard_map/ppermute | solution.py:23
  13.3 3.1 %collective-permute-start.9 = (bf16[4,7168]{1,0:T(4,128)(2,1)S(1)}, bf16[4,7168]{1,0:T(4,128)(2,1)S(1)}, u32[]{:S(2)}, u32[]{:S(2)}) collective-permute-start(bf16[4,7168]{1,0:T(4,128)(2,1)S(1)} %collective-permute-done.1.refs_2_), channel_id=1, source_target_pairs={{0,1},{1,0},{2,3},{3,2},{4,5},{5,4},{6,7},{7,6},{8,9},{9,8},{10,11... | collective-permute-start | bytes 172040 | tf_op jit(solution)/shard_map/ppermute | solution.py:23
  14.7 1.7 %collective-permute-start.8 = (bf16[4,7168]{1,0:T(4,128)(2,1)S(1)}, bf16[4,7168]{1,0:T(4,128)(2,1)S(1)}, u32[]{:S(2)}, u32[]{:S(2)}) collective-permute-start(bf16[4,7168]{1,0:T(4,128)(2,1)S(1)} %collective-permute-done.refs_1_), channel_id=1, source_target_pairs={{0,1},{1,0},{2,3},{3,2},{4,5},{5,4},{6,7},{7,6},{8,9},{9,8},{10,11... | collective-permute-start | bytes 172040 | tf_op jit(solution)/shard_map/ppermute | solution.py:23
  15.8 1.2 %collective-permute-start.10 = (bf16[4,7168]{1,0:T(4,128)(2,1)S(1)}, bf16[4,7168]{1,0:T(4,128)(2,1)S(1)}, u32[]{:S(2)}, u32[]{:S(2)}) collective-permute-start(bf16[4,7168]{1,0:T(4,128)(2,1)S(1)} %collective-permute-done.2.refs_3_), channel_id=1, source_target_pairs={{0,1},{1,0},{2,3},{3,2},{4,5},{5,4},{6,7},{7,6},{8,9},{9,8},{10,11... | collective-permute-start | bytes 172040 | tf_op jit(solution)/shard_map/ppermute | solution.py:23
  15.8 1.4 %collective-permute-start.12 = (bf16[4,7168]{1,0:T(4,128)(2,1)S(1)}, bf16[4,7168]{1,0:T(4,128)(2,1)S(1)}, u32[]{:S(2)}, u32[]{:S(2)}) collective-permute-start(bf16[4,7168]{1,0:T(4,128)(2,1)S(1)} %collective-permute-done.4.refs_5_), channel_id=1, source_target_pairs={{0,1},{1,0},{2,3},{3,2},{4,5},{5,4},{6,7},{7,6},{8,9},{9,8},{10,11... | collective-permute-start | bytes 172040 | tf_op jit(solution)/shard_map/ppermute | solution.py:23
  16.3 1.2 %collective-permute-start.14 = (bf16[4,7168]{1,0:T(4,128)(2,1)S(1)}, bf16[4,7168]{1,0:T(4,128)(2,1)S(1)}, u32[]{:S(2)}, u32[]{:S(2)}) collective-permute-start(bf16[4,7168]{1,0:T(4,128)(2,1)S(1)} %collective-permute-done.6.refs_7_), channel_id=1, source_target_pairs={{0,1},{1,0},{2,3},{3,2},{4,5},{5,4},{6,7},{7,6},{8,9},{9,8},{10,11... | collective-permute-start | bytes 172040 | tf_op jit(solution)/shard_map/ppermute | solution.py:23
  22.4 6.1 %copy-start.3 = (s32[4,2]{0,1:T(2,128)S(1)}, s32[4,2]{0,1:T(2,128)}, u32[]{:S(2)}) copy-start(s32[4,2]{0,1:T(2,128)} %param.7) | copy-start | bytes 100
  22.4 6.2 %copy-start.4 = (s32[4,2]{0,1:T(2,128)S(1)}, s32[4,2]{0,1:T(2,128)}, u32[]{:S(2)}) copy-start(s32[4,2]{0,1:T(2,128)} %param.8) | copy-start | bytes 100
  28.0 1.7 %collective-permute-start.27 = (bf16[4,7168]{1,0:T(4,128)(2,1)S(1)}, bf16[4,7168]{1,0:T(4,128)(2,1)S(1)}, u32[]{:S(2)}, u32[]{:S(2)}) collective-permute-start(bf16[4,7168]{1,0:T(4,128)(2,1)S(1)} %get-tuple-element.36), channel_id=1, source_target_pairs={{0,1},{1,0},{2,3},{3,2},{4,5},{5,4},{6,7},{7,6},{8,9},{9,8},{10,11... | collective-permute-start | bytes 172040 | tf_op jit(solution)/shard_map/ppermute | solution.py:23
  28.7 3.3 %collective-permute-start.26 = (bf16[4,7168]{1,0:T(4,128)(2,1)S(1)}, bf16[4,7168]{1,0:T(4,128)(2,1)S(1)}, u32[]{:S(2)}, u32[]{:S(2)}) collective-permute-start(bf16[4,7168]{1,0:T(4,128)(2,1)S(1)} %get-tuple-element.34), channel_id=1, source_target_pairs={{0,1},{1,0},{2,3},{3,2},{4,5},{5,4},{6,7},{7,6},{8,9},{9,8},{10,11... | collective-permute-start | bytes 172040 | tf_op jit(solution)/shard_map/ppermute | solution.py:23
  28.7 1.3 %collective-permute-start.23 = (bf16[4,7168]{1,0:T(4,128)(2,1)S(1)}, bf16[4,7168]{1,0:T(4,128)(2,1)S(1)}, u32[]{:S(2)}, u32[]{:S(2)}) collective-permute-start(bf16[4,7168]{1,0:T(4,128)(2,1)S(1)} %get-tuple-element.32), channel_id=1, source_target_pairs={{0,1},{1,0},{2,3},{3,2},{4,5},{5,4},{6,7},{7,6},{8,9},{9,8},{10,11... | collective-permute-start | bytes 172040 | tf_op jit(solution)/shard_map/ppermute | solution.py:23
  29.2 7.0 %collective-permute-start.22 = (bf16[4,7168]{1,0:T(4,128)(2,1)S(1)}, bf16[4,7168]{1,0:T(4,128)(2,1)S(1)}, u32[]{:S(2)}, u32[]{:S(2)}) collective-permute-start(bf16[4,7168]{1,0:T(4,128)(2,1)S(1)} %get-tuple-element.30), channel_id=1, source_target_pairs={{0,1},{1,0},{2,3},{3,2},{4,5},{5,4},{6,7},{7,6},{8,9},{9,8},{10,11... | collective-permute-start | bytes 172040 | tf_op jit(solution)/shard_map/ppermute | solution.py:23
  29.3 1.3 %collective-permute-start.19 = (bf16[4,7168]{1,0:T(4,128)(2,1)S(1)}, bf16[4,7168]{1,0:T(4,128)(2,1)S(1)}, u32[]{:S(2)}, u32[]{:S(2)}) collective-permute-start(bf16[4,7168]{1,0:T(4,128)(2,1)S(1)} %get-tuple-element.28), channel_id=1, source_target_pairs={{0,1},{1,0},{2,3},{3,2},{4,5},{5,4},{6,7},{7,6},{8,9},{9,8},{10,11... | collective-permute-start | bytes 172040 | tf_op jit(solution)/shard_map/ppermute | solution.py:23
  29.7 8.6 %collective-permute-start.18 = (bf16[4,7168]{1,0:T(4,128)(2,1)S(1)}, bf16[4,7168]{1,0:T(4,128)(2,1)S(1)}, u32[]{:S(2)}, u32[]{:S(2)}) collective-permute-start(bf16[4,7168]{1,0:T(4,128)(2,1)S(1)} %get-tuple-element.26), channel_id=1, source_target_pairs={{0,1},{1,0},{2,3},{3,2},{4,5},{5,4},{6,7},{7,6},{8,9},{9,8},{10,11... | collective-permute-start | bytes 172040 | tf_op jit(solution)/shard_map/ppermute | solution.py:23
  30.1 1.2 %collective-permute-start.16 = (bf16[4,7168]{1,0:T(4,128)(2,1)S(1)}, bf16[4,7168]{1,0:T(4,128)(2,1)S(1)}, u32[]{:S(2)}, u32[]{:S(2)}) collective-permute-start(bf16[4,7168]{1,0:T(4,128)(2,1)S(1)} %get-tuple-element.24), channel_id=1, source_target_pairs={{0,1},{1,0},{2,3},{3,2},{4,5},{5,4},{6,7},{7,6},{8,9},{9,8},{10,11... | collective-permute-start | bytes 172040 | tf_op jit(solution)/shard_map/ppermute | solution.py:23
  30.6 11.9 %collective-permute-start.15 = (bf16[4,7168]{1,0:T(4,128)(2,1)S(1)}, bf16[4,7168]{1,0:T(4,128)(2,1)S(1)}, u32[]{:S(2)}, u32[]{:S(2)}) collective-permute-start(bf16[4,7168]{1,0:T(4,128)(2,1)S(1)} %get-tuple-element.22), channel_id=1, source_target_pairs={{0,1},{1,0},{2,3},{3,2},{4,5},{5,4},{6,7},{7,6},{8,9},{9,8},{10,11... | collective-permute-start | bytes 172040 | tf_op jit(solution)/shard_map/ppermute | solution.py:23
  31.3 4.8 %collective-permute-start.28 = (bf16[4,7168]{1,0:T(4,128)(2,1)S(1)}, bf16[4,7168]{1,0:T(4,128)(2,1)S(1)}, u32[]{:S(2)}, u32[]{:S(2)}) collective-permute-start(bf16[4,7168]{1,0:T(4,128)(2,1)S(1)} %add_convert_fusion.1), channel_id=1, source_target_pairs={{0,2},{1,3},{2,0},{3,1},{4,6},{5,7},{6,4},{7,5},{8,10},{9,11},{10,... | collective-permute-start | bytes 172040 | tf_op jit(solution)/shard_map/ppermute | solution.py:18
  32.0 6.3 %collective-permute-start.24 = (bf16[4,7168]{1,0:T(4,128)(2,1)S(1)}, bf16[4,7168]{1,0:T(4,128)(2,1)S(1)}, u32[]{:S(2)}, u32[]{:S(2)}) collective-permute-start(bf16[4,7168]{1,0:T(4,128)(2,1)S(1)} %add_convert_fusion.3), channel_id=1, source_target_pairs={{0,2},{1,3},{2,0},{3,1},{4,6},{5,7},{6,4},{7,5},{8,10},{9,11},{10,... | collective-permute-start | bytes 172040 | tf_op jit(solution)/shard_map/ppermute | solution.py:18
  36.1 5.0 %collective-permute-start.20 = (bf16[4,7168]{1,0:T(4,128)(2,1)S(1)}, bf16[4,7168]{1,0:T(4,128)(2,1)S(1)}, u32[]{:S(2)}, u32[]{:S(2)}) collective-permute-start(bf16[4,7168]{1,0:T(4,128)(2,1)S(1)} %add_convert_fusion.5), channel_id=1, source_target_pairs={{0,2},{1,3},{2,0},{3,1},{4,6},{5,7},{6,4},{7,5},{8,10},{9,11},{10,... | collective-permute-start | bytes 172040 | tf_op jit(solution)/shard_map/ppermute | solution.py:18
  36.2 6.3 %collective-permute-start.17 = (bf16[4,7168]{1,0:T(4,128)(2,1)S(1)}, bf16[4,7168]{1,0:T(4,128)(2,1)S(1)}, u32[]{:S(2)}, u32[]{:S(2)}) collective-permute-start(bf16[4,7168]{1,0:T(4,128)(2,1)S(1)} %add_convert_fusion.7), channel_id=1, source_target_pairs={{0,2},{1,3},{2,0},{3,1},{4,6},{5,7},{6,4},{7,5},{8,10},{9,11},{10,... | collective-permute-start | bytes 172040 | tf_op jit(solution)/shard_map/ppermute | solution.py:18
  38.3 6.0 %collective-permute-start.29 = (bf16[4,7168]{1,0:T(4,128)(2,1)S(1)}, bf16[4,7168]{1,0:T(4,128)(2,1)S(1)}, u32[]{:S(2)}, u32[]{:S(2)}) collective-permute-start(bf16[4,7168]{1,0:T(4,128)(2,1)S(1)} %add_convert_fusion), channel_id=1, source_target_pairs={{0,4},{4,8},{8,12},{12,0},{1,5},{5,9},{9,13},{13,1},{2,6},{6,10},{... | collective-permute-start | bytes 172040 | tf_op jit(solution)/shard_map/ppermute | solution.py:18
  38.3 5.9 %collective-permute-start.25 = (bf16[4,7168]{1,0:T(4,128)(2,1)S(1)}, bf16[4,7168]{1,0:T(4,128)(2,1)S(1)}, u32[]{:S(2)}, u32[]{:S(2)}) collective-permute-start(bf16[4,7168]{1,0:T(4,128)(2,1)S(1)} %add_convert_fusion.2), channel_id=1, source_target_pairs={{0,8},{4,12},{8,0},{12,4},{1,9},{5,13},{9,1},{13,5},{2,10},{6,14},... | collective-permute-start | bytes 172040 | tf_op jit(solution)/shard_map/ppermute | solution.py:18
  41.1 4.2 %collective-permute-start.21 = (bf16[4,7168]{1,0:T(4,128)(2,1)S(1)}, bf16[4,7168]{1,0:T(4,128)(2,1)S(1)}, u32[]{:S(2)}, u32[]{:S(2)}) collective-permute-start(bf16[4,7168]{1,0:T(4,128)(2,1)S(1)} %add_convert_fusion.4), channel_id=1, source_target_pairs={{0,12},{4,0},{8,4},{12,8},{1,13},{5,1},{9,5},{13,9},{2,14},{6,2},{... | collective-permute-start | bytes 172040 | tf_op jit(solution)/shard_map/ppermute | solution.py:18
  (3 other events, 9.1 us)

commit v3 on v2

v3 whole, which is shorter than its diff:
```python
import functools

import jax
import jax.numpy as jnp
from jax import lax
from jax.experimental import pallas as pl
from jax.experimental.pallas import tpu as pltpu
from jax.sharding import PartitionSpec as P


CORES = 2
MIB = 1 << 20
VMEM_BYTES = 62 * MIB


def shift(value, axis, amount, stride=1):
    size = lax.axis_size(axis) // stride
    pairs = [(i * stride + r, (i + amount) % size * stride + r) for i in range(size) for r in range(stride)]
    return lax.ppermute(value, axis, pairs)


def core_swap(value):
    size = lax.axis_size("tok")
    return lax.ppermute(value, "tok", [(i, i ^ 1) for i in range(size)])


def enter_kernel(gate_ref, up_ref, out_ref):
    out_ref[...] = jnp.zeros_like(out_ref)


def enter(gate_w, up_w):
    hbm = pl.BlockSpec(memory_space=pl.ANY)
    return pl.pallas_call(
        enter_kernel,
        out_shape=jax.ShapeDtypeStruct((8, 128), jnp.float32),
        in_specs=[hbm, hbm],
        out_specs=pl.BlockSpec(memory_space=pltpu.VMEM),
        compiler_params=pltpu.CompilerParams(vmem_limit_bytes=VMEM_BYTES - 4 * gate_w.size - 3 * MIB // 4),
        name="enter",
    )(gate_w, up_w)


def gather_kernel(*refs):
    for i, ref in enumerate(refs[:-1]):
        refs[-1][i] = ref[...]


def gather_rows(chunks):
    rows, model = chunks[0].shape
    vmem = pl.BlockSpec(memory_space=pltpu.VMEM)
    return pl.pallas_call(
        gather_kernel,
        out_shape=jax.ShapeDtypeStruct((len(chunks), rows, model), chunks[0].dtype),
        in_specs=[vmem] * len(chunks),
        out_specs=vmem,
        compiler_params=pltpu.CompilerParams(vmem_limit_bytes=2 * MIB),
    )(*chunks)


def pieces(refs):
    return [ref.at[i] for ref in refs for i in range(ref.shape[0])]


def ffn_kernel(n_in, n_out, depth, width, *refs):
    chunks = pieces(refs[:n_in])
    gate_ref, up_ref, down_ref, _ = refs[n_in:n_in + 4]
    outs = pieces(refs[n_in + 4:n_in + 4 + n_out])
    gate_sum, up_sum, hidden, down_vmem, semaphore = refs[n_in + 4 + n_out:]
    fetch = pltpu.make_async_copy(down_ref, down_vmem, semaphore)
    fetch.start()
    rows, model = chunks[0].shape
    gate_sum[...] = jnp.zeros_like(gate_sum)
    up_sum[...] = jnp.zeros_like(up_sum)

    def project(i, carry):
        span = pl.ds(pl.multiple_of(i * depth, depth), depth)
        tokens = jnp.concatenate([c[:, span].astype(jnp.float32) for c in chunks], axis=0).astype(jnp.bfloat16)
        gate_sum[...] += jnp.dot(tokens, gate_ref[span, :], preferred_element_type=jnp.float32)
        up_sum[...] += jnp.dot(tokens, up_ref[span, :], preferred_element_type=jnp.float32)
        return carry

    lax.fori_loop(0, model // depth, project, 0)
    gate = gate_sum[...]
    hidden[...] = (gate / (1.0 + jnp.exp(-gate)) * up_sum[...]).astype(jnp.bfloat16)
    fetch.wait()

    def expand(i, carry):
        span = pl.ds(pl.multiple_of(i * width, width), width)
        partial = jnp.dot(hidden[...], down_vmem[:, span], preferred_element_type=jnp.float32)
        for j, out in enumerate(outs):
            out[:, span] = partial[j * rows:(j + 1) * rows].astype(jnp.bfloat16)
        return carry

    lax.fori_loop(0, model // width, expand, 0)


def block_of(model, most):
    return max(b for b in range(128, most + 1, 128) if model % b == 0)


def ffn(blocks, out_counts, gate_w, up_w, down_w, entered):
    _, rows, model = blocks[0].shape
    units = gate_w.shape[1]
    total = rows * sum(b.shape[0] for b in blocks)
    vmem = pl.BlockSpec(memory_space=pltpu.VMEM)
    return pl.pallas_call(
        functools.partial(ffn_kernel, len(blocks), len(out_counts), block_of(model, DEPTH), block_of(model, WIDTH)),
        out_shape=[jax.ShapeDtypeStruct((n, rows, model), jnp.bfloat16) for n in out_counts],
        in_specs=[vmem] * (len(blocks) + 2) + [pl.BlockSpec(memory_space=pl.ANY)] * 2,
        out_specs=[vmem] * len(out_counts),
        scratch_shapes=[
            pltpu.VMEM((total, units), jnp.float32),
            pltpu.VMEM((total, units), jnp.float32),
            pltpu.VMEM((total, units), jnp.bfloat16),
            pltpu.VMEM(down_w.shape, down_w.dtype),
            pltpu.SemaphoreType.DMA,
        ],
        compiler_params=pltpu.CompilerParams(vmem_limit_bytes=VMEM_BYTES - 4 * gate_w.size - 15 * MIB),
        cost_estimate=pl.CostEstimate(
            flops=6 * total * model * units,
            bytes_accessed=6 * model * units + 4 * total * model,
            transcendentals=total * units,
        ),
        name="ffn",
    )(*blocks, gate_w, up_w, down_w, entered)


DEPTH = 1792
WIDTH = 1792


def combine_kernel(ids_ref, gate_ref, *refs):
    terms, out = refs[:-1], refs[-1]
    me = lax.axis_index("ep")
    ids = ids_ref[...]
    scores = gate_ref[...].astype(jnp.float32)
    weights = 2.5 * scores / jnp.sum(scores, axis=1, keepdims=True)
    total = jnp.zeros(out.shape, jnp.float32)
    for k, term in enumerate(terms):
        label = lax.rem(me + k, len(terms))
        weight = jnp.sum(jnp.where(ids == label, weights, 0.0), axis=1, keepdims=True)
        total = total + weight * term[0].astype(jnp.float32)
    out[...] = total.astype(jnp.bfloat16)


def combine(expert_ids, gate_fixed, terms):
    vmem = pl.BlockSpec(memory_space=pltpu.VMEM)
    return pl.pallas_call(
        combine_kernel,
        out_shape=jax.ShapeDtypeStruct(terms[0].shape[1:], jnp.bfloat16),
        in_specs=[vmem] * (len(terms) + 2),
        out_specs=vmem,
        compiler_params=pltpu.CompilerParams(vmem_limit_bytes=8 * MIB),
        name="combine",
    )(expert_ids, gate_fixed, *terms)


def sum_kernel(spans, *refs):
    out = refs[-1]
    for i in range(out.shape[0]):
        total = refs[0][spans[0] + i].astype(jnp.float32)
        for ref, first in zip(refs[1:-1], spans[1:]):
            total = total + ref[first + i].astype(jnp.float32)
        out[i] = total.astype(out.dtype)


def add(count, *terms):
    vmem = pl.BlockSpec(memory_space=pltpu.VMEM)
    arrays = [array for array, _ in terms]
    rows, model = arrays[0].shape[1:]
    return pl.pallas_call(
        functools.partial(sum_kernel, [first for _, first in terms]),
        out_shape=jax.ShapeDtypeStruct((count, rows, model), arrays[0].dtype),
        in_specs=[vmem] * len(arrays),
        out_specs=vmem,
        compiler_params=pltpu.CompilerParams(vmem_limit_bytes=4 * MIB),
    )(*arrays)


def per_device(tokens, expert_ids, gate_fixed, w_gate, w_up, w_down):
    n_ep = lax.axis_size("ep")
    n_x = lax.axis_size("tok") // CORES
    entered = enter(w_gate[0], w_up[0])
    arrived = [shift(tokens, "ep", k) for k in range(1, n_ep)]
    lines = [tokens] + [shift(tokens, "tok", j, CORES) for j in range(1, n_x)]
    stacks = [gather_rows([tokens]), gather_rows(arrived)]
    for j in range(1, n_x):
        stacks += [lines[j][None], shift(stacks[1], "tok", j, CORES)]
    mirrored = [core_swap(s) for s in stacks]
    sizes = [n_ep] + [n_ep - 1, 1] * (n_x - 1)
    parts = ffn(stacks + mirrored, sizes * CORES, w_gate[0], w_up[0], w_down[0], entered)
    mine, theirs = parts[:len(sizes)], parts[len(sizes):]
    far = [[] for _ in range(n_ep)]
    spans = ((0, n_ep - 1, 1), (1, n_ep - 2, 1), (2, 0, n_ep - 2))
    for j in range(1, n_x):
        last, rest = 2 * j, 2 * j - 1
        tail = core_swap(theirs[last])
        body = core_swap(theirs[rest])
        for part, first, count in spans:
            pair = ((mine[last], 0), (tail, 0)) if part == 0 else ((mine[rest], first), (body, first))
            value = shift(add(count, *pair), "tok", -j, CORES)
            for k in range(count):
                far[first + k].append((value, k))
    near = core_swap(theirs[0])
    terms = []
    for k in range(n_ep):
        total = add(1, (mine[0], k), (near, k), *far[k])
        terms.append(shift(total, "ep", -k) if k else total)
    return combine(expert_ids, gate_fixed, terms)


def solution(mesh):
    in_specs = (
        P(("groups", "ep", "tok"), None),
        P(("groups", "ep", "tok"), None),
        P(("groups", "ep", "tok"), None),
        P("ep", None, "tok"),
        P("ep", None, "tok"),
        P("ep", "tok", None),
    )
    out_specs = P(("groups", "ep", "tok"), None)
    return jax.shard_map(
        per_device, mesh=mesh, in_specs=in_specs, out_specs=out_specs, check_vma=False
    )
```

time: 46.4 us -> 47.8 us (1.030)
  waiting for transfers between devices: 11.1 us -> 17.4 us
  starting transfers between devices: 23.2 us -> 20.2 us
  local copies, waits for them, and re-layouts: 5.01 us -> 3.84 us
    ppermute x14 -> x11, waiting for transfers between devices: 9.19 us -> 15.6 us  [shift(): return lax.ppermute(value, axis, pairs)]
    ppermute x16 -> x7, starting transfers between devices: 3.39 us -> 1.31 us  [core_swap(): return lax.ppermute(value, 'tok', [(i, i ^ 1) for i in range(size)])]
    unnamed x12 -> x14, local copies, waits for them, and re-layouts: 5.01 us -> 3.84 us
    ppermute x14 -> x11, starting transfers between devices: 19.8 us -> 18.9 us  [shift(): return lax.ppermute(value, axis, pairs)]
    pallas_call x1 -> x10, Pallas kernels: 5.59 us -> 5.22 us  [the longest x1 4.93 us: ffn(): pl.pallas_call(functools.partial(ffn_kernel, len(blocks), len(out_counts)...]
    ppermute x16 -> x7, waiting for transfers between devices: 1.92 us -> 1.76 us  [core_swap(): return lax.ppermute(value, 'tok', [(i, i ^ 1) for i in range(size)])]
  transfers between devices with their start and end apart: 30 -> 18, of which waited for: 13 -> 11; matrix products, arithmetic and copies ran while one was open for 1% -> 0% of each run, Pallas kernels for 0% -> 1%
where the time goes in v3:
time: 47.8 us; the launch traced here: 47.6 us
  starting transfers between devices  20.2 us (42%)
  waiting for transfers between devices  17.4 us (36%)
  Pallas kernels  6.1 us (13%)
  local copies, waits for them, and re-layouts  3.84 us (8%)
    ppermute x11, starting transfers between devices, shift(): return lax.ppermute(value, axis, pairs)  18.9 us
    ppermute x11, waiting for transfers between devices, shift(): return lax.ppermute(value, axis, pairs)  15.6 us
    pallas_call x1, Pallas kernels, ffn(): pl.pallas_call(functools.partial(ffn_kernel, len(blocks), len(out_counts)...  4.93 us
    unnamed x14, local copies, waits for them, and re-layouts  3.84 us
    ppermute x7, waiting for transfers between devices, core_swap(): return lax.ppermute(value, 'tok', [(i, i ^ 1) for i in range(size)])  1.76 us
    ppermute x7, starting transfers between devices, core_swap(): return lax.ppermute(value, 'tok', [(i, i ^ 1) for i in range(size)])  1.31 us
  transfers between devices with their start and end apart: 18, of which 11 were waited for; matrix products, arithmetic and copies ran while one was open for 0% of the time, Pallas kernels for 1%

profile of v3, /device:TPU:0, one launch (start us, length us, event | category | flops | bytes accessed | tf_op | source)
XLA Modules:
  0.0 47.6 jit_solution(16139800902294116)
XLA Ops:
  0.0 3.1 %collective-permute-start = (bf16[4,7168]{1,0:T(4,128)(2,1)}, bf16[4,7168]{1,0:T(4,128)(2,1)S(1)}, u32[]{:S(2)}, u32[]{:S(2)}) collective-permute-start(bf16[4,7168]{1,0:T(4,128)(2,1)} %refs_0_.1), channel_id=1, source_target_pairs={{0,4},{4,8},{8,12},{12,0},{1,5},{5,9},{9,13},{13,1},{2,6},{6,10},{... | collective-permute-start | bytes 172040 | tf_op jit(solution)/shard_map/ppermute | solution.py:19
  3.1 2.6 %collective-permute-start.1 = (bf16[4,7168]{1,0:T(4,128)(2,1)}, bf16[4,7168]{1,0:T(4,128)(2,1)S(1)}, u32[]{:S(2)}, u32[]{:S(2)}) collective-permute-start(bf16[4,7168]{1,0:T(4,128)(2,1)} %refs_0_.1), channel_id=1, source_target_pairs={{0,8},{4,12},{8,0},{12,4},{1,9},{5,13},{9,1},{13,5},{2,10},{6,14},... | collective-permute-start | bytes 172040 | tf_op jit(solution)/shard_map/ppermute | solution.py:19
  5.6 1.3 %collective-permute-start.2 = (bf16[4,7168]{1,0:T(4,128)(2,1)}, bf16[4,7168]{1,0:T(4,128)(2,1)S(1)}, u32[]{:S(2)}, u32[]{:S(2)}) collective-permute-start(bf16[4,7168]{1,0:T(4,128)(2,1)} %refs_0_.1), channel_id=1, source_target_pairs={{0,12},{4,0},{8,4},{12,8},{1,13},{5,1},{9,5},{13,9},{2,14},{6,2},{... | collective-permute-start | bytes 172040 | tf_op jit(solution)/shard_map/ppermute | solution.py:19
  7.0 0.6 %collective-permute-done.refs_0_ = bf16[4,7168]{1,0:T(4,128)(2,1)S(1)} collective-permute-done((bf16[4,7168]{1,0:T(4,128)(2,1)}, bf16[4,7168]{1,0:T(4,128)(2,1)S(1)}, u32[]{:S(2)}, u32[]{:S(2)}) %collective-permute-start) | collective-permute-done | bytes 57376 | tf_op jit(solution)/shard_map/ppermute | solution.py:19
  7.6 2.3 %collective-permute-done.1.refs_1_ = bf16[4,7168]{1,0:T(4,128)(2,1)S(1)} collective-permute-done((bf16[4,7168]{1,0:T(4,128)(2,1)}, bf16[4,7168]{1,0:T(4,128)(2,1)S(1)}, u32[]{:S(2)}, u32[]{:S(2)}) %collective-permute-start.1) | collective-permute-done | bytes 57376 | tf_op jit(solution)/shard_map/ppermute | solution.py:19
  9.9 0.4 collective-permute-done.2.refs_2_
  10.3 1.6 %collective-permute-start.4 = (bf16[3,4,7168]{2,1,0:T(4,128)(2,1)S(1)}, bf16[3,4,7168]{2,1,0:T(4,128)(2,1)S(1)}, u32[]{:S(2)}, u32[]{:S(2)}) collective-permute-start(bf16[3,4,7168]{2,1,0:T(4,128)(2,1)S(1)} %shard_map.65.refs_1_), channel_id=1, source_target_pairs={{0,2},{1,3},{2,0},{3,1},{4,6},{5,7},{6,4},{7,5},{8,10},{9,11},{10,... | collective-permute-start | bytes 516104 | tf_op jit(solution)/shard_map/ppermute | solution.py:19
  11.9 3.9 %collective-permute-done.4.refs_3_ = bf16[3,4,7168]{2,1,0:T(4,128)(2,1)S(1)} collective-permute-done((bf16[3,4,7168]{2,1,0:T(4,128)(2,1)S(1)}, bf16[3,4,7168]{2,1,0:T(4,128)(2,1)S(1)}, u32[]{:S(2)}, u32[]{:S(2)}) %collective-permute-start.4) | collective-permute-done | bytes 172064 | tf_op jit(solution)/shard_map/ppermute | solution.py:19
  15.7 1.5 %collective-permute-start.3 = (bf16[4,7168]{1,0:T(4,128)(2,1)}, bf16[4,7168]{1,0:T(4,128)(2,1)S(1)}, u32[]{:S(2)}, u32[]{:S(2)}) collective-permute-start(bf16[4,7168]{1,0:T(4,128)(2,1)} %refs_0_.1), channel_id=1, source_target_pairs={{0,2},{1,3},{2,0},{3,1},{4,6},{5,7},{6,4},{7,5},{8,10},{9,11},{10,... | collective-permute-start | bytes 172040 | tf_op jit(solution)/shard_map/ppermute | solution.py:19
  17.3 0.9 %copy-done.1 = bf16[4,7168]{1,0:T(4,128)(2,1)S(1)} copy-done((bf16[4,7168]{1,0:T(4,128)(2,1)S(1)}, bf16[4,7168]{1,0:T(4,128)(2,1)}, u32[]{:S(2)}) %copy-start.1) | copy-done | bytes 57368
  18.1 0.2 collective-permute-start.5
  18.4 1.9 %collective-permute-done.3 = bf16[4,7168]{1,0:T(4,128)(2,1)S(1)} collective-permute-done((bf16[4,7168]{1,0:T(4,128)(2,1)}, bf16[4,7168]{1,0:T(4,128)(2,1)S(1)}, u32[]{:S(2)}, u32[]{:S(2)}) %collective-permute-start.3) | collective-permute-done | bytes 57376 | tf_op jit(solution)/shard_map/ppermute | solution.py:19
  20.3 1.2 %collective-permute-done.7.refs_6_ = bf16[1,4,7168]{2,1,0:T(4,128)(2,1)S(1)} collective-permute-done((bf16[1,4,7168]{2,1,0:T(4,128)(2,1)S(1)}, bf16[1,4,7168]{2,1,0:T(4,128)(2,1)S(1)}, u32[]{:S(2)}, u32[]{:S(2)}) %collective-permute-start.7) | collective-permute-done | bytes 57376 | tf_op jit(solution)/shard_map/ppermute | solution.py:24
  21.5 0.6 %slice-done.1 = s8[3145728]{0:T(1024)(128)(4,1)S(1)} async-done(((s8[7340032]{0:T(1024)(128)(4,1)}), s8[3145728]{0:T(1024)(128)(4,1)S(1)}, s32[]{:S(2)}) %slice-start.1) | async-done | bytes 3145752
  22.2 2.2 %copy-done = bf16[1,7168,512]{2,1,0:T(8,128)(2,1)S(1)} copy-done((bf16[1,7168,512]{2,1,0:T(8,128)(2,1)S(1)}, bf16[1,7168,512]{2,1,0:T(8,128)(2,1)}, u32[]{:S(2)}) %copy-start) | copy-done | bytes 7340056
  24.3 4.9 %ffn.1 = (bf16[4,4,7168]{2,1,0:T(4,128)(2,1)S(1)}, bf16[3,4,7168]{2,1,0:T(4,128)(2,1)S(1)}, bf16[1,4,7168]{2,1,0:T(4,128)(2,1)S(1)}, bf16[4,4,7168]{2,1,0:T(4,12...) custom-call(bf16[1,4,7168]{2,1,0:T(4,128)(2,1)S(1)} %shard_map.64.refs_0_, ...), custom_call_target="tpu_custom_call" | custom-call | flops 1409286144 | bytes 23855104 | tf_op jit(solution)/shard_map/ffn/pallas_call | solution.py:106
  29.3 0.6 %collective-permute-start.10 = (bf16[3,4,7168]{2,1,0:T(4,128)(2,1)S(1)}, bf16[3,4,7168]{2,1,0:T(4,128)(2,1)S(1)}, u32[]{:S(2)}, u32[]{:S(2)}) collective-permute-start(bf16[3,4,7168]{2,1,0:T(4,128)(2,1)S(1)} %get-tuple-element.14), channel_id=1, source_target_pairs={{0,1},{1,0},{2,3},{3,2},{4,5},{5,4},{6,7},{7,6},{8,9},{9,8},{10,11... | collective-permute-start | bytes 516104 | tf_op jit(solution)/shard_map/ppermute | solution.py:24
  29.9 0.4 collective-permute-start.15
  30.4 0.5 %collective-permute-done.10.refs_1_ = bf16[3,4,7168]{2,1,0:T(4,128)(2,1)S(1)} collective-permute-done((bf16[3,4,7168]{2,1,0:T(4,128)(2,1)S(1)}, bf16[3,4,7168]{2,1,0:T(4,128)(2,1)S(1)}, u32[]{:S(2)}, u32[]{:S(2)}) %collective-permute-start.10) | collective-permute-done | bytes 172064 | tf_op jit(solution)/shard_map/ppermute | solution.py:24
  30.9 1.6 %collective-permute-start.11 = (bf16[2,4,7168]{2,1,0:T(4,128)(2,1)S(1)}, bf16[2,4,7168]{2,1,0:T(4,128)(2,1)S(1)}, u32[]{:S(2)}, u32[]{:S(2)}) collective-permute-start(bf16[2,4,7168]{2,1,0:T(4,128)(2,1)S(1)} %shard_map.66), channel_id=1, source_target_pairs={{0,2},{1,3},{2,0},{3,1},{4,6},{5,7},{6,4},{7,5},{8,10},{9,11},{10,... | collective-permute-start | bytes 344072 | tf_op jit(solution)/shard_map/ppermute | solution.py:19
  32.6 0.6 %collective-permute-start.16 = (bf16[1,4,7168]{2,1,0:T(4,128)(2,1)S(1)}, bf16[1,4,7168]{2,1,0:T(4,128)(2,1)S(1)}, u32[]{:S(2)}, u32[]{:S(2)}) collective-permute-start(bf16[1,4,7168]{2,1,0:T(4,128)(2,1)S(1)} %shard_map.71), channel_id=1, source_target_pairs={{0,2},{1,3},{2,0},{3,1},{4,6},{5,7},{6,4},{7,5},{8,10},{9,11},{10,... | collective-permute-start | bytes 172040 | tf_op jit(solution)/shard_map/ppermute | solution.py:19
  33.2 1.6 %collective-permute-start.13 = (bf16[1,4,7168]{2,1,0:T(4,128)(2,1)S(1)}, bf16[1,4,7168]{2,1,0:T(4,128)(2,1)S(1)}, u32[]{:S(2)}, u32[]{:S(2)}) collective-permute-start(bf16[1,4,7168]{2,1,0:T(4,128)(2,1)S(1)} %shard_map.69), channel_id=1, source_target_pairs={{0,2},{1,3},{2,0},{3,1},{4,6},{5,7},{6,4},{7,5},{8,10},{9,11},{10,... | collective-permute-start | bytes 172040 | tf_op jit(solution)/shard_map/ppermute | solution.py:19
  34.8 3.5 %collective-permute-done.16.refs_2_ = bf16[1,4,7168]{2,1,0:T(4,128)(2,1)S(1)} collective-permute-done((bf16[1,4,7168]{2,1,0:T(4,128)(2,1)S(1)}, bf16[1,4,7168]{2,1,0:T(4,128)(2,1)S(1)}, u32[]{:S(2)}, u32[]{:S(2)}) %collective-permute-start.16) | collective-permute-done | bytes 57376 | tf_op jit(solution)/shard_map/ppermute | solution.py:19
  38.3 2.0 %collective-permute-start.17 = (bf16[1,4,7168]{2,1,0:T(4,128)(2,1)S(1)}, bf16[1,4,7168]{2,1,0:T(4,128)(2,1)S(1)}, u32[]{:S(2)}, u32[]{:S(2)}) collective-permute-start(bf16[1,4,7168]{2,1,0:T(4,128)(2,1)S(1)} %shard_map.72), channel_id=1, source_target_pairs={{0,4},{4,8},{8,12},{12,0},{1,5},{5,9},{9,13},{13,1},{2,6},{6,10},{... | collective-permute-start | bytes 172040 | tf_op jit(solution)/shard_map/ppermute | solution.py:19
  40.3 1.6 %collective-permute-start.14 = (bf16[1,4,7168]{2,1,0:T(4,128)(2,1)S(1)}, bf16[1,4,7168]{2,1,0:T(4,128)(2,1)S(1)}, u32[]{:S(2)}, u32[]{:S(2)}) collective-permute-start(bf16[1,4,7168]{2,1,0:T(4,128)(2,1)S(1)} %shard_map.70), channel_id=1, source_target_pairs={{0,8},{4,12},{8,0},{12,4},{1,9},{5,13},{9,1},{13,5},{2,10},{6,14},... | collective-permute-start | bytes 172040 | tf_op jit(solution)/shard_map/ppermute | solution.py:19
  42.0 1.4 %collective-permute-start.12 = (bf16[1,4,7168]{2,1,0:T(4,128)(2,1)S(1)}, bf16[1,4,7168]{2,1,0:T(4,128)(2,1)S(1)}, u32[]{:S(2)}, u32[]{:S(2)}) collective-permute-start(bf16[1,4,7168]{2,1,0:T(4,128)(2,1)S(1)} %shard_map.68), channel_id=1, source_target_pairs={{0,12},{4,0},{8,4},{12,8},{1,13},{5,1},{9,5},{13,9},{2,14},{6,2},{... | collective-permute-start | bytes 172040 | tf_op jit(solution)/shard_map/ppermute | solution.py:19
  43.4 0.1 copy.7.ids_ref
  43.5 0.1 copy.8.gate_ref
  43.6 1.3 %collective-permute-done.17.refs_3_ = bf16[1,4,7168]{2,1,0:T(4,128)(2,1)S(1)} collective-permute-done((bf16[1,4,7168]{2,1,0:T(4,128)(2,1)S(1)}, bf16[1,4,7168]{2,1,0:T(4,128)(2,1)S(1)}, u32[]{:S(2)}, u32[]{:S(2)}) %collective-permute-start.17) | collective-permute-done | bytes 57376 | tf_op jit(solution)/shard_map/ppermute | solution.py:19
  44.9 1.6 %collective-permute-done.14.refs_2_ = bf16[1,4,7168]{2,1,0:T(4,128)(2,1)S(1)} collective-permute-done((bf16[1,4,7168]{2,1,0:T(4,128)(2,1)S(1)}, bf16[1,4,7168]{2,1,0:T(4,128)(2,1)S(1)}, u32[]{:S(2)}, u32[]{:S(2)}) %collective-permute-start.14) | collective-permute-done | bytes 57376 | tf_op jit(solution)/shard_map/ppermute | solution.py:19
  46.6 0.1 collective-permute-done.12.refs_1_
  46.7 0.9 %combine.1 = bf16[4,7168]{1,0:T(4,128)(2,1)} custom-call(s32[4,2]{1,0:T(4,128)S(1)} %copy.7.ids_ref, s32[4,2]{1,0:T(4,128)S(1)} %copy.8.gate_ref, bf16[1,4,7168]{2,1,0:T(4,128)(2,1)S(1)} %shard_map.67.refs_0_, bf16[1,4,7168]{2,1,0:T(4,128)(2,1)S(1)} %collective-permute-done.12.refs_1_, bf16[1,4,7168]{2,1,0:T(4,128)(2,1)S(1)} %collective-permute-done.14.refs_2_, ...), custom_call_target="tpu_custom_call" | custom-call | tf_op jit(solution)/shard_map/combine/pallas_call | solution.py:148
  (31 shorter events, 0.4 us)
Async XLA Ops:
  0.0 7.6 %collective-permute-start = (bf16[4,7168]{1,0:T(4,128)(2,1)}, bf16[4,7168]{1,0:T(4,128)(2,1)S(1)}, u32[]{:S(2)}, u32[]{:S(2)}) collective-permute-start(bf16[4,7168]{1,0:T(4,128)(2,1)} %refs_0_.1), channel_id=1, source_target_pairs={{0,4},{4,8},{8,12},{12,0},{1,5},{5,9},{9,13},{13,1},{2,6},{6,10},{... | collective-permute-start | bytes 172040 | tf_op jit(solution)/shard_map/ppermute | solution.py:19
  3.1 6.8 %collective-permute-start.1 = (bf16[4,7168]{1,0:T(4,128)(2,1)}, bf16[4,7168]{1,0:T(4,128)(2,1)S(1)}, u32[]{:S(2)}, u32[]{:S(2)}) collective-permute-start(bf16[4,7168]{1,0:T(4,128)(2,1)} %refs_0_.1), channel_id=1, source_target_pairs={{0,8},{4,12},{8,0},{12,4},{1,9},{5,13},{9,1},{13,5},{2,10},{6,14},... | collective-permute-start | bytes 172040 | tf_op jit(solution)/shard_map/ppermute | solution.py:19
  5.6 4.6 %collective-permute-start.2 = (bf16[4,7168]{1,0:T(4,128)(2,1)}, bf16[4,7168]{1,0:T(4,128)(2,1)S(1)}, u32[]{:S(2)}, u32[]{:S(2)}) collective-permute-start(bf16[4,7168]{1,0:T(4,128)(2,1)} %refs_0_.1), channel_id=1, source_target_pairs={{0,12},{4,0},{8,4},{12,8},{1,13},{5,1},{9,5},{13,9},{2,14},{6,2},{... | collective-permute-start | bytes 172040 | tf_op jit(solution)/shard_map/ppermute | solution.py:19
  10.3 11.3 %slice-start = ((s8[7340032]{0:T(1024)(128)(4,1)}), s8[4194304]{0:T(1024)(128)(4,1)S(1)}, s32[]{:S(2)}) async-start(s8[7340032]{0:T(1024)(128)(4,1)} %bitcast.5), calls=%async_computation | async-start | bytes 8388608
  10.3 5.5 %collective-permute-start.4 = (bf16[3,4,7168]{2,1,0:T(4,128)(2,1)S(1)}, bf16[3,4,7168]{2,1,0:T(4,128)(2,1)S(1)}, u32[]{:S(2)}, u32[]{:S(2)}) collective-permute-start(bf16[3,4,7168]{2,1,0:T(4,128)(2,1)S(1)} %shard_map.65.refs_1_), channel_id=1, source_target_pairs={{0,2},{1,3},{2,0},{3,1},{4,6},{5,7},{6,4},{7,5},{8,10},{9,11},{10,... | collective-permute-start | bytes 516104 | tf_op jit(solution)/shard_map/ppermute | solution.py:19
  11.9 9.7 %collective-permute-start.6 = (bf16[3,4,7168]{2,1,0:T(4,128)(2,1)S(1)}, bf16[3,4,7168]{2,1,0:T(4,128)(2,1)S(1)}, u32[]{:S(2)}, u32[]{:S(2)}) collective-permute-start(bf16[3,4,7168]{2,1,0:T(4,128)(2,1)S(1)} %shard_map.65.refs_1_), channel_id=1, source_target_pairs={{0,1},{1,0},{2,3},{3,2},{4,5},{5,4},{6,7},{7,6},{8,9},{9,8},{10,11... | collective-permute-start | bytes 516104 | tf_op jit(solution)/shard_map/ppermute | solution.py:24
  15.7 5.8 %collective-permute-start.8 = (bf16[3,4,7168]{2,1,0:T(4,128)(2,1)S(1)}, bf16[3,4,7168]{2,1,0:T(4,128)(2,1)S(1)}, u32[]{:S(2)}, u32[]{:S(2)}) collective-permute-start(bf16[3,4,7168]{2,1,0:T(4,128)(2,1)S(1)} %collective-permute-done.4.refs_3_), channel_id=1, source_target_pairs={{0,1},{1,0},{2,3},{3,2},{4,5},{5,4},{6,7},{7,6},{8,9},{9,8},{10,11... | collective-permute-start | bytes 516104 | tf_op jit(solution)/shard_map/ppermute | solution.py:24
  15.7 4.5 %collective-permute-start.3 = (bf16[4,7168]{1,0:T(4,128)(2,1)}, bf16[4,7168]{1,0:T(4,128)(2,1)S(1)}, u32[]{:S(2)}, u32[]{:S(2)}) collective-permute-start(bf16[4,7168]{1,0:T(4,128)(2,1)} %refs_0_.1), channel_id=1, source_target_pairs={{0,2},{1,3},{2,0},{3,1},{4,6},{5,7},{6,4},{7,5},{8,10},{9,11},{10,... | collective-permute-start | bytes 172040 | tf_op jit(solution)/shard_map/ppermute | solution.py:19
  17.3 0.9 %copy-start.1 = (bf16[4,7168]{1,0:T(4,128)(2,1)S(1)}, bf16[4,7168]{1,0:T(4,128)(2,1)}, u32[]{:S(2)}) copy-start(bf16[4,7168]{1,0:T(4,128)(2,1)} %refs_0_.1) | copy-start | bytes 172036
  18.1 2.2 %collective-permute-start.5 = (bf16[1,4,7168]{2,1,0:T(4,128)(2,1)S(1)}, bf16[1,4,7168]{2,1,0:T(4,128)(2,1)S(1)}, u32[]{:S(2)}, u32[]{:S(2)}) collective-permute-start(bf16[1,4,7168]{2,1,0:T(4,128)(2,1)S(1)} %shard_map.64.refs_0_), channel_id=1, source_target_pairs={{0,1},{1,0},{2,3},{3,2},{4,5},{5,4},{6,7},{7,6},{8,9},{9,8},{10,11... | collective-permute-start | bytes 172040 | tf_op jit(solution)/shard_map/ppermute | solution.py:24
  20.3 1.2 %collective-permute-start.7 = (bf16[1,4,7168]{2,1,0:T(4,128)(2,1)S(1)}, bf16[1,4,7168]{2,1,0:T(4,128)(2,1)S(1)}, u32[]{:S(2)}, u32[]{:S(2)}) collective-permute-start(bf16[1,4,7168]{2,1,0:T(4,128)(2,1)S(1)} %bitcast.10), channel_id=1, source_target_pairs={{0,1},{1,0},{2,3},{3,2},{4,5},{5,4},{6,7},{7,6},{8,9},{9,8},{10,11... | collective-permute-start | bytes 172040 | tf_op jit(solution)/shard_map/ppermute | solution.py:24
  20.3 1.9 %slice-start.1 = ((s8[7340032]{0:T(1024)(128)(4,1)}), s8[3145728]{0:T(1024)(128)(4,1)S(1)}, s32[]{:S(2)}) async-start(s8[7340032]{0:T(1024)(128)(4,1)} %bitcast.5), calls=%async_computation.1 | async-start | bytes 6291456
  20.3 4.0 %copy-start = (bf16[1,7168,512]{2,1,0:T(8,128)(2,1)S(1)}, bf16[1,7168,512]{2,1,0:T(8,128)(2,1)}, u32[]{:S(2)}) copy-start(bf16[1,7168,512]{2,1,0:T(8,128)(2,1)} %param.10) | copy-start | bytes 22020100
  24.3 19.1 %copy-start.2 = (s32[4,2]{0,1:T(2,128)S(1)}, s32[4,2]{0,1:T(2,128)}, u32[]{:S(2)}) copy-start(s32[4,2]{0,1:T(2,128)} %param.7) | copy-start | bytes 100
  24.3 19.2 %copy-start.3 = (s32[4,2]{0,1:T(2,128)S(1)}, s32[4,2]{0,1:T(2,128)}, u32[]{:S(2)}) copy-start(s32[4,2]{0,1:T(2,128)} %param.8) | copy-start | bytes 100
  29.3 1.6 %collective-permute-start.10 = (bf16[3,4,7168]{2,1,0:T(4,128)(2,1)S(1)}, bf16[3,4,7168]{2,1,0:T(4,128)(2,1)S(1)}, u32[]{:S(2)}, u32[]{:S(2)}) collective-permute-start(bf16[3,4,7168]{2,1,0:T(4,128)(2,1)S(1)} %get-tuple-element.14), channel_id=1, source_target_pairs={{0,1},{1,0},{2,3},{3,2},{4,5},{5,4},{6,7},{7,6},{8,9},{9,8},{10,11... | collective-permute-start | bytes 516104 | tf_op jit(solution)/shard_map/ppermute | solution.py:24
  29.8 8.4 %collective-permute-start.9 = (bf16[4,4,7168]{2,1,0:T(4,128)(2,1)S(1)}, bf16[4,4,7168]{2,1,0:T(4,128)(2,1)S(1)}, u32[]{:S(2)}, u32[]{:S(2)}) collective-permute-start(bf16[4,4,7168]{2,1,0:T(4,128)(2,1)S(1)} %get-tuple-element.12), channel_id=1, source_target_pairs={{0,1},{1,0},{2,3},{3,2},{4,5},{5,4},{6,7},{7,6},{8,9},{9,8},{10,11... | collective-permute-start | bytes 688136 | tf_op jit(solution)/shard_map/ppermute | solution.py:24
  29.9 2.6 %collective-permute-start.15 = (bf16[1,4,7168]{2,1,0:T(4,128)(2,1)S(1)}, bf16[1,4,7168]{2,1,0:T(4,128)(2,1)S(1)}, u32[]{:S(2)}, u32[]{:S(2)}) collective-permute-start(bf16[1,4,7168]{2,1,0:T(4,128)(2,1)S(1)} %get-tuple-element.16), channel_id=1, source_target_pairs={{0,1},{1,0},{2,3},{3,2},{4,5},{5,4},{6,7},{7,6},{8,9},{9,8},{10,11... | collective-permute-start | bytes 172040 | tf_op jit(solution)/shard_map/ppermute | solution.py:24
  30.9 11.0 %collective-permute-start.11 = (bf16[2,4,7168]{2,1,0:T(4,128)(2,1)S(1)}, bf16[2,4,7168]{2,1,0:T(4,128)(2,1)S(1)}, u32[]{:S(2)}, u32[]{:S(2)}) collective-permute-start(bf16[2,4,7168]{2,1,0:T(4,128)(2,1)S(1)} %shard_map.66), channel_id=1, source_target_pairs={{0,2},{1,3},{2,0},{3,1},{4,6},{5,7},{6,4},{7,5},{8,10},{9,11},{10,... | collective-permute-start | bytes 344072 | tf_op jit(solution)/shard_map/ppermute | solution.py:19
  32.6 5.7 %collective-permute-start.16 = (bf16[1,4,7168]{2,1,0:T(4,128)(2,1)S(1)}, bf16[1,4,7168]{2,1,0:T(4,128)(2,1)S(1)}, u32[]{:S(2)}, u32[]{:S(2)}) collective-permute-start(bf16[1,4,7168]{2,1,0:T(4,128)(2,1)S(1)} %shard_map.71), channel_id=1, source_target_pairs={{0,2},{1,3},{2,0},{3,1},{4,6},{5,7},{6,4},{7,5},{8,10},{9,11},{10,... | collective-permute-start | bytes 172040 | tf_op jit(solution)/shard_map/ppermute | solution.py:19
  33.2 7.1 %collective-permute-start.13 = (bf16[1,4,7168]{2,1,0:T(4,128)(2,1)S(1)}, bf16[1,4,7168]{2,1,0:T(4,128)(2,1)S(1)}, u32[]{:S(2)}, u32[]{:S(2)}) collective-permute-start(bf16[1,4,7168]{2,1,0:T(4,128)(2,1)S(1)} %shard_map.69), channel_id=1, source_target_pairs={{0,2},{1,3},{2,0},{3,1},{4,6},{5,7},{6,4},{7,5},{8,10},{9,11},{10,... | collective-permute-start | bytes 172040 | tf_op jit(solution)/shard_map/ppermute | solution.py:19
  38.3 6.6 %collective-permute-start.17 = (bf16[1,4,7168]{2,1,0:T(4,128)(2,1)S(1)}, bf16[1,4,7168]{2,1,0:T(4,128)(2,1)S(1)}, u32[]{:S(2)}, u32[]{:S(2)}) collective-permute-start(bf16[1,4,7168]{2,1,0:T(4,128)(2,1)S(1)} %shard_map.72), channel_id=1, source_target_pairs={{0,4},{4,8},{8,12},{12,0},{1,5},{5,9},{9,13},{13,1},{2,6},{6,10},{... | collective-permute-start | bytes 172040 | tf_op jit(solution)/shard_map/ppermute | solution.py:19
  40.3 6.2 %collective-permute-start.14 = (bf16[1,4,7168]{2,1,0:T(4,128)(2,1)S(1)}, bf16[1,4,7168]{2,1,0:T(4,128)(2,1)S(1)}, u32[]{:S(2)}, u32[]{:S(2)}) collective-permute-start(bf16[1,4,7168]{2,1,0:T(4,128)(2,1)S(1)} %shard_map.70), channel_id=1, source_target_pairs={{0,8},{4,12},{8,0},{12,4},{1,9},{5,13},{9,1},{13,5},{2,10},{6,14},... | collective-permute-start | bytes 172040 | tf_op jit(solution)/shard_map/ppermute | solution.py:19
  42.0 4.7 %collective-permute-start.12 = (bf16[1,4,7168]{2,1,0:T(4,128)(2,1)S(1)}, bf16[1,4,7168]{2,1,0:T(4,128)(2,1)S(1)}, u32[]{:S(2)}, u32[]{:S(2)}) collective-permute-start(bf16[1,4,7168]{2,1,0:T(4,128)(2,1)S(1)} %shard_map.68), channel_id=1, source_target_pairs={{0,12},{4,0},{8,4},{12,8},{1,13},{5,1},{9,5},{13,9},{2,14},{6,2},{... | collective-permute-start | bytes 172040 | tf_op jit(solution)/shard_map/ppermute | solution.py:19

commit v4 on v3

--- a/solution.py
+++ b/solution.py
@@ -13,9 +13,14 @@
 VMEM_BYTES = 62 * MIB
 
 
+def mirrors(size):
+    return XOR and size & (size - 1) == 0
+
+
 def shift(value, axis, amount, stride=1):
     size = lax.axis_size(axis) // stride
-    pairs = [(i * stride + r, (i + amount) % size * stride + r) for i in range(size) for r in range(stride)]
+    target = (lambda i: i ^ abs(amount)) if mirrors(size) else (lambda i: (i + amount) % size)
+    pairs = [(i * stride + r, target(i) * stride + r) for i in range(size) for r in range(stride)]
     return lax.ppermute(value, axis, pairs)
 
 
@@ -35,24 +40,27 @@
         out_shape=jax.ShapeDtypeStruct((8, 128), jnp.float32),
         in_specs=[hbm, hbm],
         out_specs=pl.BlockSpec(memory_space=pltpu.VMEM),
-        compiler_params=pltpu.CompilerParams(vmem_limit_bytes=VMEM_BYTES - 4 * gate_w.size - 3 * MIB // 4),
+        compiler_params=pltpu.CompilerParams(vmem_limit_bytes=VMEM_BYTES - 4 * gate_w.size - E1 * MIB // 4),
         name="enter",
     )(gate_w, up_w)
 
 
-def gather_kernel(*refs):
-    for i, ref in enumerate(refs[:-1]):
-        refs[-1][i] = ref[...]
-
-
-def gather_rows(chunks):
+def gather_kernel(halves, *refs):
+    chunks, outs = refs[:-halves], refs[-halves:]
+    for out, half in zip(outs, range(halves)):
+        width = out.shape[2]
+        for i, ref in enumerate(chunks):
+            out[i] = ref[:, half * width:(half + 1) * width]
+
+
+def gather_rows(chunks, halves):
     rows, model = chunks[0].shape
     vmem = pl.BlockSpec(memory_space=pltpu.VMEM)
     return pl.pallas_call(
-        gather_kernel,
-        out_shape=jax.ShapeDtypeStruct((len(chunks), rows, model), chunks[0].dtype),
+        functools.partial(gather_kernel, halves),
+        out_shape=[jax.ShapeDtypeStruct((len(chunks), rows, model // halves), chunks[0].dtype)] * halves,
         in_specs=[vmem] * len(chunks),
-        out_specs=vmem,
+        out_specs=[vmem] * halves,
         compiler_params=pltpu.CompilerParams(vmem_limit_bytes=2 * MIB),
     )(*chunks)
 
@@ -61,70 +69,118 @@
     return [ref.at[i] for ref in refs for i in range(ref.shape[0])]
 
 
-def ffn_kernel(n_in, n_out, depth, width, *refs):
-    chunks = pieces(refs[:n_in])
-    gate_ref, up_ref, down_ref, _ = refs[n_in:n_in + 4]
-    outs = pieces(refs[n_in + 4:n_in + 4 + n_out])
-    gate_sum, up_sum, hidden, down_vmem, semaphore = refs[n_in + 4 + n_out:]
-    fetch = pltpu.make_async_copy(down_ref, down_vmem, semaphore)
-    fetch.start()
-    rows, model = chunks[0].shape
-    gate_sum[...] = jnp.zeros_like(gate_sum)
-    up_sum[...] = jnp.zeros_like(up_sum)
-
-    def project(i, carry):
-        span = pl.ds(pl.multiple_of(i * depth, depth), depth)
-        tokens = jnp.concatenate([c[:, span].astype(jnp.float32) for c in chunks], axis=0).astype(jnp.bfloat16)
+def project(refs, half, depth, gate_ref, up_ref, gate_sum, up_sum):
+    span_of = gate_ref.shape[0] // HALVES
+    starts = [half * span_of if ref.shape[2] > span_of else 0 for ref in refs for _ in range(ref.shape[0])]
+    chunks = list(zip(pieces(refs), starts))
+
+    def step(i, carry):
+        at = pl.multiple_of(i * depth, depth)
+        tokens = [c[:, pl.ds(pl.multiple_of(first + at, 128), depth)].astype(jnp.float32) for c, first in chunks]
+        tokens = jnp.concatenate(tokens, axis=0).astype(jnp.bfloat16)
+        span = pl.ds(pl.multiple_of(half * span_of + at, 128), depth)
         gate_sum[...] += jnp.dot(tokens, gate_ref[span, :], preferred_element_type=jnp.float32)
         up_sum[...] += jnp.dot(tokens, up_ref[span, :], preferred_element_type=jnp.float32)
         return carry
 
-    lax.fori_loop(0, model // depth, project, 0)
+    lax.fori_loop(0, span_of // depth, step, 0)
+
+
+def first_kernel(n_in, depth, *refs):
+    gate_ref, up_ref, down_ref, gate_sum, up_sum, down_low, semaphore = refs[n_in:]
+    fetch = pltpu.make_async_copy(down_ref.at[:, pl.ds(0, down_low.shape[1])], down_low, semaphore)
+    fetch.start()
+    gate_sum[...] = jnp.zeros_like(gate_sum)
+    up_sum[...] = jnp.zeros_like(up_sum)
+    project(refs[:n_in], 0, depth, gate_ref, up_ref, gate_sum, up_sum)
+    fetch.wait()
+
+
+def second_kernel(n_in, n_out, depth, width, *refs):
+    gate_ref, up_ref, down_ref, gate_first, up_first, down_low, _ = refs[n_in:n_in + 7]
+    outs = pieces(refs[n_in + 7:n_in + 7 + n_out])
+    gate_sum, up_sum, hidden, down_high, semaphores = refs[n_in + 7 + n_out:]
+    low = down_low.shape[1]
+    count = down_high.shape[1] // width
+
+    def fetch(i):
+        source = down_ref.at[:, pl.ds(low + i * width, width)]
+        return pltpu.make_async_copy(source, down_high.at[:, pl.ds(i * width, width)], semaphores.at[i])
+
+    for i in range(count):
+        fetch(i).start()
+    gate_sum[...] = gate_first[...]
+    up_sum[...] = up_first[...]
+    project(refs[:n_in], 1, depth, gate_ref, up_ref, gate_sum, up_sum)
     gate = gate_sum[...]
     hidden[...] = (gate / (1.0 + jnp.exp(-gate)) * up_sum[...]).astype(jnp.bfloat16)
-    fetch.wait()
-
-    def expand(i, carry):
-        span = pl.ds(pl.multiple_of(i * width, width), width)
-        partial = jnp.dot(hidden[...], down_vmem[:, span], preferred_element_type=jnp.float32)
+    rows = outs[0].shape[0]
+
+    def expand(source, at, base):
+        partial = jnp.dot(hidden[...], source[:, pl.ds(at, width)], preferred_element_type=jnp.float32)
         for j, out in enumerate(outs):
-            out[:, span] = partial[j * rows:(j + 1) * rows].astype(jnp.bfloat16)
-        return carry
-
-    lax.fori_loop(0, model // width, expand, 0)
+            out[:, pl.ds(base + at, width)] = partial[j * rows:(j + 1) * rows].astype(jnp.bfloat16)
+
+    for i in range(low // width):
+        expand(down_low, i * width, 0)
+    for i in range(count):
+        fetch(i).wait()
+        expand(down_high, i * width, low)
 
 
 def block_of(model, most):
     return max(b for b in range(128, most + 1, 128) if model % b == 0)
 
 
-def ffn(blocks, out_counts, gate_w, up_w, down_w, entered):
-    _, rows, model = blocks[0].shape
-    units = gate_w.shape[1]
-    total = rows * sum(b.shape[0] for b in blocks)
-    vmem = pl.BlockSpec(memory_space=pltpu.VMEM)
-    return pl.pallas_call(
-        functools.partial(ffn_kernel, len(blocks), len(out_counts), block_of(model, DEPTH), block_of(model, WIDTH)),
+def expert(first_blocks, second_blocks, out_counts, gate_w, up_w, down_w, entered):
+    rows = first_blocks[0].shape[1]
+    model, units = gate_w.shape
+    half = model // HALVES
+    low = model // LOW
+    depth, width = block_of(half, DEPTH), block_of(low, WIDTH)
+    total = rows * sum(b.shape[0] for b in first_blocks)
+    sums = jax.ShapeDtypeStruct((total, units), jnp.float32)
+    vmem, hbm = pl.BlockSpec(memory_space=pltpu.VMEM), pl.BlockSpec(memory_space=pl.ANY)
+    room = VMEM_BYTES - 4 * gate_w.size
+    cost = pl.CostEstimate(
+        flops=3 * total * model * units,
+        bytes_accessed=3 * model * units + 2 * total * model,
+        transcendentals=total * units,
+    )
+    gate_sum, up_sum, down_low = pl.pallas_call(
+        functools.partial(first_kernel, len(first_blocks), depth),
+        out_shape=[sums, sums, jax.ShapeDtypeStruct((units, low), down_w.dtype)],
+        in_specs=[vmem] * (len(first_blocks) + 2) + [hbm],
+        out_specs=[vmem] * 3,
+        scratch_shapes=[pltpu.SemaphoreType.DMA],
+        compiler_params=pltpu.CompilerParams(vmem_limit_bytes=room - L1 * MIB),
+        cost_estimate=cost,
+        name="ffn_first",
+    )(*first_blocks, gate_w, up_w, down_w)
+    return pl.pallas_call(
+        functools.partial(second_kernel, len(second_blocks), len(out_counts), depth, width),
         out_shape=[jax.ShapeDtypeStruct((n, rows, model), jnp.bfloat16) for n in out_counts],
-        in_specs=[vmem] * (len(blocks) + 2) + [pl.BlockSpec(memory_space=pl.ANY)] * 2,
+        in_specs=[vmem] * (len(second_blocks) + 2) + [hbm] + [vmem] * 3 + [hbm],
         out_specs=[vmem] * len(out_counts),
         scratch_shapes=[
             pltpu.VMEM((total, units), jnp.float32),
             pltpu.VMEM((total, units), jnp.float32),
             pltpu.VMEM((total, units), jnp.bfloat16),
-            pltpu.VMEM(down_w.shape, down_w.dtype),
-            pltpu.SemaphoreType.DMA,
+            pltpu.VMEM((units, model - low), down_w.dtype),
+            pltpu.SemaphoreType.DMA((model // width,)),
         ],
-        compiler_params=pltpu.CompilerParams(vmem_limit_bytes=VMEM_BYTES - 4 * gate_w.size - 15 * MIB),
-        cost_estimate=pl.CostEstimate(
-            flops=6 * total * model * units,
-            bytes_accessed=6 * model * units + 4 * total * model,
-            transcendentals=total * units,
-        ),
+        compiler_params=pltpu.CompilerParams(vmem_limit_bytes=room - L2 * MIB),
+        cost_estimate=cost,
         name="ffn",
-    )(*blocks, gate_w, up_w, down_w, entered)
-
-
+    )(*second_blocks, gate_w, up_w, down_w, gate_sum, up_sum, down_low, entered)
+
+
+HALVES = 2
+LOW = 4
+L1 = 15
+L2 = 16
+E1 = 3
+XOR = True
 DEPTH = 1792
 WIDTH = 1792
 
@@ -137,7 +193,7 @@
     weights = 2.5 * scores / jnp.sum(scores, axis=1, keepdims=True)
     total = jnp.zeros(out.shape, jnp.float32)
     for k, term in enumerate(terms):
-        label = lax.rem(me + k, len(terms))
+        label = me ^ k if mirrors(len(terms)) else lax.rem(me + k, len(terms))
         weight = jnp.sum(jnp.where(ids == label, weights, 0.0), axis=1, keepdims=True)
         total = total + weight * term[0].astype(jnp.float32)
     out[...] = total.astype(jnp.bfloat16)
@@ -183,12 +239,18 @@
     entered = enter(w_gate[0], w_up[0])
     arrived = [shift(tokens, "ep", k) for k in range(1, n_ep)]
     lines = [tokens] + [shift(tokens, "tok", j, CORES) for j in range(1, n_x)]
-    stacks = [gather_rows([tokens]), gather_rows(arrived)]
-    for j in range(1, n_x):
-        stacks += [lines[j][None], shift(stacks[1], "tok", j, CORES)]
-    mirrored = [core_swap(s) for s in stacks]
+    stage = gather_rows([tokens], 1)[0]
+    arrived = gather_rows(arrived, HALVES)
+    whole = [stage] + [lines[j][None] for j in range(1, n_x)]
+    whole += [core_swap(w) for w in whole]
+    parted = []
+    for half in range(HALVES):
+        blocks = [arrived[half]]
+        blocks += [shift(arrived[half], "tok", j, CORES) for j in range(1, n_x)]
+        blocks += [core_swap(b) for b in blocks]
+        parted.append([b for pair in zip(whole, blocks) for b in pair])
     sizes = [n_ep] + [n_ep - 1, 1] * (n_x - 1)
-    parts = ffn(stacks + mirrored, sizes * CORES, w_gate[0], w_up[0], w_down[0], entered)
+    parts = expert(*parted, sizes * CORES, w_gate[0], w_up[0], w_down[0], entered)
     mine, theirs = parts[:len(sizes)], parts[len(sizes):]
     far = [[] for _ in range(n_ep)]
     spans = ((0, n_ep - 1, 1), (1, n_ep - 2, 1), (2, 0, n_ep - 2))

time: 47.8 us -> 45.8 us (0.958)
  waiting for transfers between devices: 17.4 us -> 15 us
  local copies, waits for them, and re-layouts: 3.84 us -> 5.02 us
  starting transfers between devices: 20.2 us -> 19.3 us
    ppermute x11 -> x12, waiting for transfers between devices: 15.6 us -> 13.6 us  [shift(): return lax.ppermute(value, axis, pairs)]
    ppermute x11 -> x12, starting transfers between devices: 18.9 us -> 17.3 us  [shift(): return lax.ppermute(value, axis, pairs)]
    unnamed x14, local copies, waits for them, and re-layouts: 3.84 us -> 5.02 us
    ppermute x7 -> x9, starting transfers between devices: 1.31 us -> 2.03 us  [core_swap(): return lax.ppermute(value, 'tok', [(i, i ^ 1) for i in range(size)])]
    ppermute x7 -> x9, waiting for transfers between devices: 1.76 us -> 1.37 us  [core_swap(): return lax.ppermute(value, 'tok', [(i, i ^ 1) for i in range(size)])]
    pallas_call x3 -> x4, Pallas kernels: 4.95 us -> 4.99 us  [the longest x1 3.44 us: expert(): pl.pallas_call(functools.partial(second_kernel, len(second_blocks), len(o...]
  transfers between devices with their start and end apart: 18 -> 21, of which waited for: 11 -> 8; matrix products, arithmetic and copies ran while one was open for 0% -> 0% of each run, Pallas kernels for 1% -> 4%
where the time goes in v4:
time: 45.8 us; the launch traced here: 45.6 us
  starting transfers between devices  19.3 us (42%)
  waiting for transfers between devices  15 us (33%)
  Pallas kernels  6.14 us (13%)
  local copies, waits for them, and re-layouts  5.02 us (11%)
    ppermute x12, starting transfers between devices, shift(): return lax.ppermute(value, axis, pairs)  17.3 us
    ppermute x12, waiting for transfers between devices, shift(): return lax.ppermute(value, axis, pairs)  13.6 us
    unnamed x14, local copies, waits for them, and re-layouts  5.02 us
    pallas_call x1, Pallas kernels, expert(): pl.pallas_call(functools.partial(second_kernel, len(second_blocks), len(o...  3.44 us
    ppermute x9, starting transfers between devices, core_swap(): return lax.ppermute(value, 'tok', [(i, i ^ 1) for i in range(size)])  2.03 us
    pallas_call x1, Pallas kernels, expert(): pl.pallas_call(functools.partial(first_kernel, len(first_blocks), depth),...  1.53 us
    ppermute x9, waiting for transfers between devices, core_swap(): return lax.ppermute(value, 'tok', [(i, i ^ 1) for i in range(size)])  1.37 us
  transfers between devices with their start and end apart: 21, of which 8 were waited for; matrix products, arithmetic and copies ran while one was open for 0% of the time, Pallas kernels for 4%

profile of v4, /device:TPU:0, one launch (start us, length us, event | category | flops | bytes accessed | tf_op | source)
XLA Modules:
  0.0 45.6 jit_solution(12704205537679768120)
XLA Ops:
  0.0 3.1 %collective-permute-start = (bf16[4,7168]{1,0:T(4,128)(2,1)}, bf16[4,7168]{1,0:T(4,128)(2,1)S(1)}, u32[]{:S(2)}, u32[]{:S(2)}) collective-permute-start(bf16[4,7168]{1,0:T(4,128)(2,1)} %refs_0_.1), channel_id=1, source_target_pairs={{0,4},{4,0},{8,12},{12,8},{1,5},{5,1},{9,13},{13,9},{2,6},{6,2},{1... | collective-permute-start | bytes 172040 | tf_op jit(solution)/shard_map/ppermute | solution.py:24
  3.1 2.6 %collective-permute-start.1 = (bf16[4,7168]{1,0:T(4,128)(2,1)}, bf16[4,7168]{1,0:T(4,128)(2,1)S(1)}, u32[]{:S(2)}, u32[]{:S(2)}) collective-permute-start(bf16[4,7168]{1,0:T(4,128)(2,1)} %refs_0_.1), channel_id=1, source_target_pairs={{0,8},{4,12},{8,0},{12,4},{1,9},{5,13},{9,1},{13,5},{2,10},{6,14},... | collective-permute-start | bytes 172040 | tf_op jit(solution)/shard_map/ppermute | solution.py:24
  5.6 3.8 %collective-permute-done.1.refs_1_ = bf16[4,7168]{1,0:T(4,128)(2,1)S(1)} collective-permute-done((bf16[4,7168]{1,0:T(4,128)(2,1)}, bf16[4,7168]{1,0:T(4,128)(2,1)S(1)}, u32[]{:S(2)}, u32[]{:S(2)}) %collective-permute-start.1) | collective-permute-done | bytes 57376 | tf_op jit(solution)/shard_map/ppermute | solution.py:24
  9.5 2.4 %collective-permute-done.2.refs_2_ = bf16[4,7168]{1,0:T(4,128)(2,1)S(1)} collective-permute-done((bf16[4,7168]{1,0:T(4,128)(2,1)}, bf16[4,7168]{1,0:T(4,128)(2,1)S(1)}, u32[]{:S(2)}, u32[]{:S(2)}) %collective-permute-start.2) | collective-permute-done | bytes 57376 | tf_op jit(solution)/shard_map/ppermute | solution.py:24
  11.8 1.6 %collective-permute-start.9 = (bf16[3,4,3584]{2,1,0:T(4,128)(2,1)S(1)}, bf16[3,4,3584]{2,1,0:T(4,128)(2,1)S(1)}, u32[]{:S(2)}, u32[]{:S(2)}) collective-permute-start(bf16[3,4,3584]{2,1,0:T(4,128)(2,1)S(1)} %get-tuple-element.17.refs_1_), channel_id=1, source_target_pairs={{0,2},{1,3},{2,0},{3,1},{4,6},{5,7},{6,4},{7,5},{8,10},{9,11},{10,... | collective-permute-start | bytes 258056 | tf_op jit(solution)/shard_map/ppermute | solution.py:24
  13.4 0.5 %collective-permute-start.3 = (bf16[4,7168]{1,0:T(4,128)(2,1)}, bf16[4,7168]{1,0:T(4,128)(2,1)S(1)}, u32[]{:S(2)}, u32[]{:S(2)}) collective-permute-start(bf16[4,7168]{1,0:T(4,128)(2,1)} %refs_0_.1), channel_id=1, source_target_pairs={{0,2},{1,3},{2,0},{3,1},{4,6},{5,7},{6,4},{7,5},{8,10},{9,11},{10,... | collective-permute-start | bytes 172040 | tf_op jit(solution)/shard_map/ppermute | solution.py:24
  13.9 1.5 %collective-permute-start.4 = (bf16[3,4,3584]{2,1,0:T(4,128)(2,1)S(1)}, bf16[3,4,3584]{2,1,0:T(4,128)(2,1)S(1)}, u32[]{:S(2)}, u32[]{:S(2)}) collective-permute-start(bf16[3,4,3584]{2,1,0:T(4,128)(2,1)S(1)} %get-tuple-element.16.refs_1_), channel_id=1, source_target_pairs={{0,2},{1,3},{2,0},{3,1},{4,6},{5,7},{6,4},{7,5},{8,10},{9,11},{10,... | collective-permute-start | bytes 258056 | tf_op jit(solution)/shard_map/ppermute | solution.py:24
  15.4 1.2 %collective-permute-done.9.refs_3_ = bf16[3,4,3584]{2,1,0:T(4,128)(2,1)S(1)} collective-permute-done((bf16[3,4,3584]{2,1,0:T(4,128)(2,1)S(1)}, bf16[3,4,3584]{2,1,0:T(4,128)(2,1)S(1)}, u32[]{:S(2)}, u32[]{:S(2)}) %collective-permute-start.9) | collective-permute-done | bytes 86048 | tf_op jit(solution)/shard_map/ppermute | solution.py:24
  16.6 0.8 %copy-done.1 = bf16[4,7168]{1,0:T(4,128)(2,1)S(1)} copy-done((bf16[4,7168]{1,0:T(4,128)(2,1)S(1)}, bf16[4,7168]{1,0:T(4,128)(2,1)}, u32[]{:S(2)}) %copy-start.1) | copy-done | bytes 57368
  17.4 0.5 %collective-permute-start.5 = (bf16[1,4,7168]{2,1,0:T(4,128)(2,1)S(1)}, bf16[1,4,7168]{2,1,0:T(4,128)(2,1)S(1)}, u32[]{:S(2)}, u32[]{:S(2)}) collective-permute-start(bf16[1,4,7168]{2,1,0:T(4,128)(2,1)S(1)} %shard_map.64.refs_0_), channel_id=1, source_target_pairs={{0,1},{1,0},{2,3},{3,2},{4,5},{5,4},{6,7},{7,6},{8,9},{9,8},{10,11... | collective-permute-start | bytes 172040 | tf_op jit(solution)/shard_map/ppermute | solution.py:29
  18.0 0.8 %collective-permute-done.5.refs_4_ = bf16[1,4,7168]{2,1,0:T(4,128)(2,1)S(1)} collective-permute-done((bf16[1,4,7168]{2,1,0:T(4,128)(2,1)S(1)}, bf16[1,4,7168]{2,1,0:T(4,128)(2,1)S(1)}, u32[]{:S(2)}, u32[]{:S(2)}) %collective-permute-start.5) | collective-permute-done | bytes 57376 | tf_op jit(solution)/shard_map/ppermute | solution.py:29
  18.8 0.4 collective-permute-start.6
  19.2 0.2 collective-permute-start.8
  19.4 1.8 %slice-done.1 = s8[3145728]{0:T(1024)(128)(4,1)S(1)} async-done(((s8[7340032]{0:T(1024)(128)(4,1)}), s8[3145728]{0:T(1024)(128)(4,1)S(1)}, s32[]{:S(2)}) %slice-start.1) | async-done | bytes 3145752
  21.2 2.2 %copy-done = bf16[1,7168,512]{2,1,0:T(8,128)(2,1)S(1)} copy-done((bf16[1,7168,512]{2,1,0:T(8,128)(2,1)S(1)}, bf16[1,7168,512]{2,1,0:T(8,128)(2,1)}, u32[]{:S(2)}) %copy-start) | copy-done | bytes 7340056
  23.4 1.5 %ffn_first.1 = (f32[64,512]{1,0:T(8,128)S(1)}, f32[64,512]{1,0:T(8,128)S(1)}, bf16[512,1792]{1,0:T(8,128)(2,1)S(1)}) custom-call(bf16[1,4,7168]{2,1,0:T(4,128)(2,1)S(1)} %shard_map.64.refs_0_, bf16[3,4,3584]{2,1,0:T(4,128)(2,1)S(1)} %get-tuple-element.17.refs_1_, bf16[1,4,7168]{2,1,0:T(4,128)(2,1)S(1)} %bitcast.13, ...), custom_call_target="tpu_custom_call" | custom-call | flops 704643072 | bytes 11927552 | tf_op jit(solution)/shard_map/ffn_first/pallas_call | solution.py:150
  25.0 3.4 %ffn.1 = (bf16[4,4,7168]{2,1,0:T(4,128)(2,1)S(1)}, bf16[3,4,7168]{2,1,0:T(4,128)(2,1)S(1)}, bf16[1,4,7168]{2,1,0:T(4,128)(2,1)S(1)}, bf16[4,4,7168]{2,1,0:T(4,12...) custom-call(bf16[1,4,7168]{2,1,0:T(4,128)(2,1)S(1)} %shard_map.64.refs_0_, ...), custom_call_target="tpu_custom_call" | custom-call | flops 704643072 | bytes 11927552 | tf_op jit(solution)/shard_map/ffn/pallas_call | solution.py:160
  28.4 0.4 collective-permute-start.13
  28.8 0.2 collective-permute-start.12
  29.0 0.3 collective-permute-start.18
  29.4 0.5 %collective-permute-done.13.refs_1_ = bf16[3,4,7168]{2,1,0:T(4,128)(2,1)S(1)} collective-permute-done((bf16[3,4,7168]{2,1,0:T(4,128)(2,1)S(1)}, bf16[3,4,7168]{2,1,0:T(4,128)(2,1)S(1)}, u32[]{:S(2)}, u32[]{:S(2)}) %collective-permute-start.13) | collective-permute-done | bytes 172064 | tf_op jit(solution)/shard_map/ppermute | solution.py:29
  30.0 1.3 %collective-permute-start.14 = (bf16[2,4,7168]{2,1,0:T(4,128)(2,1)S(1)}, bf16[2,4,7168]{2,1,0:T(4,128)(2,1)S(1)}, u32[]{:S(2)}, u32[]{:S(2)}) collective-permute-start(bf16[2,4,7168]{2,1,0:T(4,128)(2,1)S(1)} %shard_map.66), channel_id=1, source_target_pairs={{0,2},{1,3},{2,0},{3,1},{4,6},{5,7},{6,4},{7,5},{8,10},{9,11},{10,... | collective-permute-start | bytes 344072 | tf_op jit(solution)/shard_map/ppermute | solution.py:24
  31.3 0.8 %collective-permute-start.19 = (bf16[1,4,7168]{2,1,0:T(4,128)(2,1)S(1)}, bf16[1,4,7168]{2,1,0:T(4,128)(2,1)S(1)}, u32[]{:S(2)}, u32[]{:S(2)}) collective-permute-start(bf16[1,4,7168]{2,1,0:T(4,128)(2,1)S(1)} %shard_map.71), channel_id=1, source_target_pairs={{0,2},{1,3},{2,0},{3,1},{4,6},{5,7},{6,4},{7,5},{8,10},{9,11},{10,... | collective-permute-start | bytes 172040 | tf_op jit(solution)/shard_map/ppermute | solution.py:24
  32.2 1.3 %collective-permute-start.16 = (bf16[1,4,7168]{2,1,0:T(4,128)(2,1)S(1)}, bf16[1,4,7168]{2,1,0:T(4,128)(2,1)S(1)}, u32[]{:S(2)}, u32[]{:S(2)}) collective-permute-start(bf16[1,4,7168]{2,1,0:T(4,128)(2,1)S(1)} %shard_map.69), channel_id=1, source_target_pairs={{0,2},{1,3},{2,0},{3,1},{4,6},{5,7},{6,4},{7,5},{8,10},{9,11},{10,... | collective-permute-start | bytes 172040 | tf_op jit(solution)/shard_map/ppermute | solution.py:24
  33.5 3.7 %collective-permute-done.19.refs_2_ = bf16[1,4,7168]{2,1,0:T(4,128)(2,1)S(1)} collective-permute-done((bf16[1,4,7168]{2,1,0:T(4,128)(2,1)S(1)}, bf16[1,4,7168]{2,1,0:T(4,128)(2,1)S(1)}, u32[]{:S(2)}, u32[]{:S(2)}) %collective-permute-start.19) | collective-permute-done | bytes 57376 | tf_op jit(solution)/shard_map/ppermute | solution.py:24
  37.3 1.1 %collective-permute-start.20 = (bf16[1,4,7168]{2,1,0:T(4,128)(2,1)S(1)}, bf16[1,4,7168]{2,1,0:T(4,128)(2,1)S(1)}, u32[]{:S(2)}, u32[]{:S(2)}) collective-permute-start(bf16[1,4,7168]{2,1,0:T(4,128)(2,1)S(1)} %shard_map.72), channel_id=1, source_target_pairs={{0,12},{4,8},{8,4},{12,0},{1,13},{5,9},{9,5},{13,1},{2,14},{6,10},... | collective-permute-start | bytes 172040 | tf_op jit(solution)/shard_map/ppermute | solution.py:24
  38.5 1.0 %collective-permute-start.17 = (bf16[1,4,7168]{2,1,0:T(4,128)(2,1)S(1)}, bf16[1,4,7168]{2,1,0:T(4,128)(2,1)S(1)}, u32[]{:S(2)}, u32[]{:S(2)}) collective-permute-start(bf16[1,4,7168]{2,1,0:T(4,128)(2,1)S(1)} %shard_map.70), channel_id=1, source_target_pairs={{0,8},{4,12},{8,0},{12,4},{1,9},{5,13},{9,1},{13,5},{2,10},{6,14},... | collective-permute-start | bytes 172040 | tf_op jit(solution)/shard_map/ppermute | solution.py:24
  39.5 2.5 %collective-permute-start.15 = (bf16[1,4,7168]{2,1,0:T(4,128)(2,1)S(1)}, bf16[1,4,7168]{2,1,0:T(4,128)(2,1)S(1)}, u32[]{:S(2)}, u32[]{:S(2)}) collective-permute-start(bf16[1,4,7168]{2,1,0:T(4,128)(2,1)S(1)} %shard_map.68), channel_id=1, source_target_pairs={{0,4},{4,0},{8,12},{12,8},{1,5},{5,1},{9,13},{13,9},{2,6},{6,2},{1... | collective-permute-start | bytes 172040 | tf_op jit(solution)/shard_map/ppermute | solution.py:24
  42.0 0.1 copy.7.ids_ref
  42.2 1.4 %collective-permute-done.20.refs_3_ = bf16[1,4,7168]{2,1,0:T(4,128)(2,1)S(1)} collective-permute-done((bf16[1,4,7168]{2,1,0:T(4,128)(2,1)S(1)}, bf16[1,4,7168]{2,1,0:T(4,128)(2,1)S(1)}, u32[]{:S(2)}, u32[]{:S(2)}) %collective-permute-start.20) | collective-permute-done | bytes 57376 | tf_op jit(solution)/shard_map/ppermute | solution.py:24
  43.6 1.1 %collective-permute-done.17.refs_2_ = bf16[1,4,7168]{2,1,0:T(4,128)(2,1)S(1)} collective-permute-done((bf16[1,4,7168]{2,1,0:T(4,128)(2,1)S(1)}, bf16[1,4,7168]{2,1,0:T(4,128)(2,1)S(1)}, u32[]{:S(2)}, u32[]{:S(2)}) %collective-permute-start.17) | collective-permute-done | bytes 57376 | tf_op jit(solution)/shard_map/ppermute | solution.py:24
  44.7 0.9 %combine.1 = bf16[4,7168]{1,0:T(4,128)(2,1)} custom-call(s32[4,2]{1,0:T(4,128)S(1)} %copy.7.ids_ref, s32[4,2]{1,0:T(4,128)S(1)} %copy.8.gate_ref, bf16[1,4,7168]{2,1,0:T(4,128)(2,1)S(1)} %shard_map.67.refs_0_, bf16[1,4,7168]{2,1,0:T(4,128)(2,1)S(1)} %collective-permute-done.15.refs_1_, bf16[1,4,7168]{2,1,0:T(4,128)(2,1)S(1)} %collective-permute-done.17.refs_2_, ...), custom_call_target="tpu_custom_call" | custom-call | tf_op jit(solution)/shard_map/combine/pallas_call | solution.py:204
  (38 shorter events, 0.5 us)
Async XLA Ops:
  0.0 5.6 %collective-permute-start = (bf16[4,7168]{1,0:T(4,128)(2,1)}, bf16[4,7168]{1,0:T(4,128)(2,1)S(1)}, u32[]{:S(2)}, u32[]{:S(2)}) collective-permute-start(bf16[4,7168]{1,0:T(4,128)(2,1)} %refs_0_.1), channel_id=1, source_target_pairs={{0,4},{4,0},{8,12},{12,8},{1,5},{5,1},{9,13},{13,9},{2,6},{6,2},{1... | collective-permute-start | bytes 172040 | tf_op jit(solution)/shard_map/ppermute | solution.py:24
  3.1 6.4 %collective-permute-start.1 = (bf16[4,7168]{1,0:T(4,128)(2,1)}, bf16[4,7168]{1,0:T(4,128)(2,1)S(1)}, u32[]{:S(2)}, u32[]{:S(2)}) collective-permute-start(bf16[4,7168]{1,0:T(4,128)(2,1)} %refs_0_.1), channel_id=1, source_target_pairs={{0,8},{4,12},{8,0},{12,4},{1,9},{5,13},{9,1},{13,5},{2,10},{6,14},... | collective-permute-start | bytes 172040 | tf_op jit(solution)/shard_map/ppermute | solution.py:24
  5.6 6.2 %collective-permute-start.2 = (bf16[4,7168]{1,0:T(4,128)(2,1)}, bf16[4,7168]{1,0:T(4,128)(2,1)S(1)}, u32[]{:S(2)}, u32[]{:S(2)}) collective-permute-start(bf16[4,7168]{1,0:T(4,128)(2,1)} %refs_0_.1), channel_id=1, source_target_pairs={{0,12},{4,8},{8,4},{12,0},{1,13},{5,9},{9,5},{13,1},{2,14},{6,10},... | collective-permute-start | bytes 172040 | tf_op jit(solution)/shard_map/ppermute | solution.py:24
  11.8 7.6 %slice-start = ((s8[7340032]{0:T(1024)(128)(4,1)}), s8[4194304]{0:T(1024)(128)(4,1)S(1)}, s32[]{:S(2)}) async-start(s8[7340032]{0:T(1024)(128)(4,1)} %bitcast.5), calls=%async_computation | async-start | bytes 8388608
  11.8 4.8 %collective-permute-start.9 = (bf16[3,4,3584]{2,1,0:T(4,128)(2,1)S(1)}, bf16[3,4,3584]{2,1,0:T(4,128)(2,1)S(1)}, u32[]{:S(2)}, u32[]{:S(2)}) collective-permute-start(bf16[3,4,3584]{2,1,0:T(4,128)(2,1)S(1)} %get-tuple-element.17.refs_1_), channel_id=1, source_target_pairs={{0,2},{1,3},{2,0},{3,1},{4,6},{5,7},{6,4},{7,5},{8,10},{9,11},{10,... | collective-permute-start | bytes 258056 | tf_op jit(solution)/shard_map/ppermute | solution.py:24
  13.4 4.5 %collective-permute-start.3 = (bf16[4,7168]{1,0:T(4,128)(2,1)}, bf16[4,7168]{1,0:T(4,128)(2,1)S(1)}, u32[]{:S(2)}, u32[]{:S(2)}) collective-permute-start(bf16[4,7168]{1,0:T(4,128)(2,1)} %refs_0_.1), channel_id=1, source_target_pairs={{0,2},{1,3},{2,0},{3,1},{4,6},{5,7},{6,4},{7,5},{8,10},{9,11},{10,... | collective-permute-start | bytes 172040 | tf_op jit(solution)/shard_map/ppermute | solution.py:24
  13.9 5.3 %collective-permute-start.4 = (bf16[3,4,3584]{2,1,0:T(4,128)(2,1)S(1)}, bf16[3,4,3584]{2,1,0:T(4,128)(2,1)S(1)}, u32[]{:S(2)}, u32[]{:S(2)}) collective-permute-start(bf16[3,4,3584]{2,1,0:T(4,128)(2,1)S(1)} %get-tuple-element.16.refs_1_), channel_id=1, source_target_pairs={{0,2},{1,3},{2,0},{3,1},{4,6},{5,7},{6,4},{7,5},{8,10},{9,11},{10,... | collective-permute-start | bytes 258056 | tf_op jit(solution)/shard_map/ppermute | solution.py:24
  15.4 3.9 %collective-permute-start.10 = (bf16[3,4,3584]{2,1,0:T(4,128)(2,1)S(1)}, bf16[3,4,3584]{2,1,0:T(4,128)(2,1)S(1)}, u32[]{:S(2)}, u32[]{:S(2)}) collective-permute-start(bf16[3,4,3584]{2,1,0:T(4,128)(2,1)S(1)} %get-tuple-element.17.refs_1_), channel_id=1, source_target_pairs={{0,1},{1,0},{2,3},{3,2},{4,5},{5,4},{6,7},{7,6},{8,9},{9,8},{10,11... | collective-permute-start | bytes 258056 | tf_op jit(solution)/shard_map/ppermute | solution.py:29
  16.6 2.8 %collective-permute-start.11 = (bf16[3,4,3584]{2,1,0:T(4,128)(2,1)S(1)}, bf16[3,4,3584]{2,1,0:T(4,128)(2,1)S(1)}, u32[]{:S(2)}, u32[]{:S(2)}) collective-permute-start(bf16[3,4,3584]{2,1,0:T(4,128)(2,1)S(1)} %collective-permute-done.9.refs_3_), channel_id=1, source_target_pairs={{0,1},{1,0},{2,3},{3,2},{4,5},{5,4},{6,7},{7,6},{8,9},{9,8},{10,11... | collective-permute-start | bytes 258056 | tf_op jit(solution)/shard_map/ppermute | solution.py:29
  16.6 0.8 %copy-start.1 = (bf16[4,7168]{1,0:T(4,128)(2,1)S(1)}, bf16[4,7168]{1,0:T(4,128)(2,1)}, u32[]{:S(2)}) copy-start(bf16[4,7168]{1,0:T(4,128)(2,1)} %refs_0_.1) | copy-start | bytes 172036
  17.4 1.4 %collective-permute-start.5 = (bf16[1,4,7168]{2,1,0:T(4,128)(2,1)S(1)}, bf16[1,4,7168]{2,1,0:T(4,128)(2,1)S(1)}, u32[]{:S(2)}, u32[]{:S(2)}) collective-permute-start(bf16[1,4,7168]{2,1,0:T(4,128)(2,1)S(1)} %shard_map.64.refs_0_), channel_id=1, source_target_pairs={{0,1},{1,0},{2,3},{3,2},{4,5},{5,4},{6,7},{7,6},{8,9},{9,8},{10,11... | collective-permute-start | bytes 172040 | tf_op jit(solution)/shard_map/ppermute | solution.py:29
  18.0 1.4 %collective-permute-start.7 = (bf16[1,4,7168]{2,1,0:T(4,128)(2,1)S(1)}, bf16[1,4,7168]{2,1,0:T(4,128)(2,1)S(1)}, u32[]{:S(2)}, u32[]{:S(2)}) collective-permute-start(bf16[1,4,7168]{2,1,0:T(4,128)(2,1)S(1)} %bitcast.12), channel_id=1, source_target_pairs={{0,1},{1,0},{2,3},{3,2},{4,5},{5,4},{6,7},{7,6},{8,9},{9,8},{10,11... | collective-permute-start | bytes 172040 | tf_op jit(solution)/shard_map/ppermute | solution.py:29
  18.8 6.1 %collective-permute-start.6 = (bf16[3,4,3584]{2,1,0:T(4,128)(2,1)S(1)}, bf16[3,4,3584]{2,1,0:T(4,128)(2,1)S(1)}, u32[]{:S(2)}, u32[]{:S(2)}) collective-permute-start(bf16[3,4,3584]{2,1,0:T(4,128)(2,1)S(1)} %get-tuple-element.16.refs_1_), channel_id=1, source_target_pairs={{0,1},{1,0},{2,3},{3,2},{4,5},{5,4},{6,7},{7,6},{8,9},{9,8},{10,11... | collective-permute-start | bytes 258056 | tf_op jit(solution)/shard_map/ppermute | solution.py:29
  19.2 5.8 %collective-permute-start.8 = (bf16[3,4,3584]{2,1,0:T(4,128)(2,1)S(1)}, bf16[3,4,3584]{2,1,0:T(4,128)(2,1)S(1)}, u32[]{:S(2)}, u32[]{:S(2)}) collective-permute-start(bf16[3,4,3584]{2,1,0:T(4,128)(2,1)S(1)} %collective-permute-done.4.refs_3_), channel_id=1, source_target_pairs={{0,1},{1,0},{2,3},{3,2},{4,5},{5,4},{6,7},{7,6},{8,9},{9,8},{10,11... | collective-permute-start | bytes 258056 | tf_op jit(solution)/shard_map/ppermute | solution.py:29
  19.4 1.9 %slice-start.1 = ((s8[7340032]{0:T(1024)(128)(4,1)}), s8[3145728]{0:T(1024)(128)(4,1)S(1)}, s32[]{:S(2)}) async-start(s8[7340032]{0:T(1024)(128)(4,1)} %bitcast.5), calls=%async_computation.1 | async-start | bytes 6291456
  19.4 4.0 %copy-start = (bf16[1,7168,512]{2,1,0:T(8,128)(2,1)S(1)}, bf16[1,7168,512]{2,1,0:T(8,128)(2,1)}, u32[]{:S(2)}) copy-start(bf16[1,7168,512]{2,1,0:T(8,128)(2,1)} %param.10) | copy-start | bytes 22020100
  25.0 17.0 %copy-start.2 = (s32[4,2]{0,1:T(2,128)S(1)}, s32[4,2]{0,1:T(2,128)}, u32[]{:S(2)}) copy-start(s32[4,2]{0,1:T(2,128)} %param.7) | copy-start | bytes 100
  25.0 17.1 %copy-start.3 = (s32[4,2]{0,1:T(2,128)S(1)}, s32[4,2]{0,1:T(2,128)}, u32[]{:S(2)}) copy-start(s32[4,2]{0,1:T(2,128)} %param.8) | copy-start | bytes 100
  28.4 1.5 %collective-permute-start.13 = (bf16[3,4,7168]{2,1,0:T(4,128)(2,1)S(1)}, bf16[3,4,7168]{2,1,0:T(4,128)(2,1)S(1)}, u32[]{:S(2)}, u32[]{:S(2)}) collective-permute-start(bf16[3,4,7168]{2,1,0:T(4,128)(2,1)S(1)} %get-tuple-element.24), channel_id=1, source_target_pairs={{0,1},{1,0},{2,3},{3,2},{4,5},{5,4},{6,7},{7,6},{8,9},{9,8},{10,11... | collective-permute-start | bytes 516104 | tf_op jit(solution)/shard_map/ppermute | solution.py:29
  28.8 8.4 %collective-permute-start.12 = (bf16[4,4,7168]{2,1,0:T(4,128)(2,1)S(1)}, bf16[4,4,7168]{2,1,0:T(4,128)(2,1)S(1)}, u32[]{:S(2)}, u32[]{:S(2)}) collective-permute-start(bf16[4,4,7168]{2,1,0:T(4,128)(2,1)S(1)} %get-tuple-element.22), channel_id=1, source_target_pairs={{0,1},{1,0},{2,3},{3,2},{4,5},{5,4},{6,7},{7,6},{8,9},{9,8},{10,11... | collective-permute-start | bytes 688136 | tf_op jit(solution)/shard_map/ppermute | solution.py:29
  29.0 2.3 %collective-permute-start.18 = (bf16[1,4,7168]{2,1,0:T(4,128)(2,1)S(1)}, bf16[1,4,7168]{2,1,0:T(4,128)(2,1)S(1)}, u32[]{:S(2)}, u32[]{:S(2)}) collective-permute-start(bf16[1,4,7168]{2,1,0:T(4,128)(2,1)S(1)} %get-tuple-element.26), channel_id=1, source_target_pairs={{0,1},{1,0},{2,3},{3,2},{4,5},{5,4},{6,7},{7,6},{8,9},{9,8},{10,11... | collective-permute-start | bytes 172040 | tf_op jit(solution)/shard_map/ppermute | solution.py:29
  30.0 9.5 %collective-permute-start.14 = (bf16[2,4,7168]{2,1,0:T(4,128)(2,1)S(1)}, bf16[2,4,7168]{2,1,0:T(4,128)(2,1)S(1)}, u32[]{:S(2)}, u32[]{:S(2)}) collective-permute-start(bf16[2,4,7168]{2,1,0:T(4,128)(2,1)S(1)} %shard_map.66), channel_id=1, source_target_pairs={{0,2},{1,3},{2,0},{3,1},{4,6},{5,7},{6,4},{7,5},{8,10},{9,11},{10,... | collective-permute-start | bytes 344072 | tf_op jit(solution)/shard_map/ppermute | solution.py:24
  31.3 5.9 %collective-permute-start.19 = (bf16[1,4,7168]{2,1,0:T(4,128)(2,1)S(1)}, bf16[1,4,7168]{2,1,0:T(4,128)(2,1)S(1)}, u32[]{:S(2)}, u32[]{:S(2)}) collective-permute-start(bf16[1,4,7168]{2,1,0:T(4,128)(2,1)S(1)} %shard_map.71), channel_id=1, source_target_pairs={{0,2},{1,3},{2,0},{3,1},{4,6},{5,7},{6,4},{7,5},{8,10},{9,11},{10,... | collective-permute-start | bytes 172040 | tf_op jit(solution)/shard_map/ppermute | solution.py:24
  32.2 6.2 %collective-permute-start.16 = (bf16[1,4,7168]{2,1,0:T(4,128)(2,1)S(1)}, bf16[1,4,7168]{2,1,0:T(4,128)(2,1)S(1)}, u32[]{:S(2)}, u32[]{:S(2)}) collective-permute-start(bf16[1,4,7168]{2,1,0:T(4,128)(2,1)S(1)} %shard_map.69), channel_id=1, source_target_pairs={{0,2},{1,3},{2,0},{3,1},{4,6},{5,7},{6,4},{7,5},{8,10},{9,11},{10,... | collective-permute-start | bytes 172040 | tf_op jit(solution)/shard_map/ppermute | solution.py:24
  37.3 6.3 %collective-permute-start.20 = (bf16[1,4,7168]{2,1,0:T(4,128)(2,1)S(1)}, bf16[1,4,7168]{2,1,0:T(4,128)(2,1)S(1)}, u32[]{:S(2)}, u32[]{:S(2)}) collective-permute-start(bf16[1,4,7168]{2,1,0:T(4,128)(2,1)S(1)} %shard_map.72), channel_id=1, source_target_pairs={{0,12},{4,8},{8,4},{12,0},{1,13},{5,9},{9,5},{13,1},{2,14},{6,10},... | collective-permute-start | bytes 172040 | tf_op jit(solution)/shard_map/ppermute | solution.py:24
  38.5 6.2 %collective-permute-start.17 = (bf16[1,4,7168]{2,1,0:T(4,128)(2,1)S(1)}, bf16[1,4,7168]{2,1,0:T(4,128)(2,1)S(1)}, u32[]{:S(2)}, u32[]{:S(2)}) collective-permute-start(bf16[1,4,7168]{2,1,0:T(4,128)(2,1)S(1)} %shard_map.70), channel_id=1, source_target_pairs={{0,8},{4,12},{8,0},{12,4},{1,9},{5,13},{9,1},{13,5},{2,10},{6,14},... | collective-permute-start | bytes 172040 | tf_op jit(solution)/shard_map/ppermute | solution.py:24
  39.5 5.2 %collective-permute-start.15 = (bf16[1,4,7168]{2,1,0:T(4,128)(2,1)S(1)}, bf16[1,4,7168]{2,1,0:T(4,128)(2,1)S(1)}, u32[]{:S(2)}, u32[]{:S(2)}) collective-permute-start(bf16[1,4,7168]{2,1,0:T(4,128)(2,1)S(1)} %shard_map.68), channel_id=1, source_target_pairs={{0,4},{4,0},{8,12},{12,8},{1,5},{5,1},{9,13},{13,9},{2,6},{6,2},{1... | collective-permute-start | bytes 172040 | tf_op jit(solution)/shard_map/ppermute | solution.py:24

commit v5 on v4

--- a/solution.py
+++ b/solution.py
@@ -180,7 +180,7 @@
 L1 = 15
 L2 = 16
 E1 = 3
-XOR = True
+XOR = False
 DEPTH = 1792
 WIDTH = 1792
 
@@ -238,10 +238,9 @@
     n_x = lax.axis_size("tok") // CORES
     entered = enter(w_gate[0], w_up[0])
     arrived = [shift(tokens, "ep", k) for k in range(1, n_ep)]
-    lines = [tokens] + [shift(tokens, "tok", j, CORES) for j in range(1, n_x)]
-    stage = gather_rows([tokens], 1)[0]
-    arrived = gather_rows(arrived, HALVES)
-    whole = [stage] + [lines[j][None] for j in range(1, n_x)]
+    stage = gather_rows([gather_rows([tokens], 1)[0][0], arrived[0]], 1)[0]
+    arrived = gather_rows(arrived[1:], HALVES)
+    whole = [stage] + [shift(stage, "tok", j, CORES) for j in range(1, n_x)]
     whole += [core_swap(w) for w in whole]
     parted = []
     for half in range(HALVES):

time: 45.8 us -> 46.3 us (1.011)
  waiting for transfers between devices: 15 us -> 17.2 us
  local copies, waits for them, and re-layouts: 5.02 us -> 3.85 us
  starting transfers between devices: 19.3 us -> 18.8 us
    ppermute x12, waiting for transfers between devices: 13.6 us -> 16.6 us  [shift(): return lax.ppermute(value, axis, pairs)]
    unnamed x14, local copies, waits for them, and re-layouts: 5.02 us -> 3.85 us
    ppermute x9, waiting for transfers between devices: 1.37 us -> 0.58 us  [core_swap(): return lax.ppermute(value, 'tok', [(i, i ^ 1) for i in range(size)])]
    ppermute x12, starting transfers between devices: 17.3 us -> 16.6 us  [shift(): return lax.ppermute(value, axis, pairs)]
  transfers between devices with their start and end apart: 21 -> 21, of which waited for: 8 -> 10; matrix products, arithmetic and copies ran while one was open for 0% -> 0% of each run, Pallas kernels for 4% -> 4%
where the time goes in v5:
time: 46.3 us; the launch traced here: 46.1 us
  starting transfers between devices  18.8 us (41%)
  waiting for transfers between devices  17.2 us (37%)
  Pallas kernels  6.15 us (13%)
  local copies, waits for them, and re-layouts  3.85 us (8%)
    ppermute x12, waiting for transfers between devices, shift(): return lax.ppermute(value, axis, pairs)  16.6 us
    ppermute x12, starting transfers between devices, shift(): return lax.ppermute(value, axis, pairs)  16.6 us
    unnamed x14, local copies, waits for them, and re-layouts  3.85 us
    pallas_call x1, Pallas kernels, expert(): pl.pallas_call(functools.partial(second_kernel, len(second_blocks), len(o...  3.44 us
    ppermute x9, starting transfers between devices, core_swap(): return lax.ppermute(value, 'tok', [(i, i ^ 1) for i in range(size)])  2.16 us
    pallas_call x1, Pallas kernels, expert(): pl.pallas_call(functools.partial(first_kernel, len(first_blocks), depth),...  1.54 us
  transfers between devices with their start and end apart: 21, of which 10 were waited for; matrix products, arithmetic and copies ran while one was open for 0% of the time, Pallas kernels for 4%

profile of v5, /device:TPU:0, one launch (start us, length us, event | category | flops | bytes accessed | tf_op | source)
XLA Modules:
  0.0 46.1 jit_solution(5730982372682497417)
XLA Ops:
  0.0 3.1 %collective-permute-start = (bf16[4,7168]{1,0:T(4,128)(2,1)}, bf16[4,7168]{1,0:T(4,128)(2,1)S(1)}, u32[]{:S(2)}, u32[]{:S(2)}) collective-permute-start(bf16[4,7168]{1,0:T(4,128)(2,1)} %refs_0_.1), channel_id=1, source_target_pairs={{0,4},{4,8},{8,12},{12,0},{1,5},{5,9},{9,13},{13,1},{2,6},{6,10},{... | collective-permute-start | bytes 172040 | tf_op jit(solution)/shard_map/ppermute | solution.py:24
  3.1 0.9 %copy-done.1 = bf16[4,7168]{1,0:T(4,128)(2,1)S(1)} copy-done((bf16[4,7168]{1,0:T(4,128)(2,1)S(1)}, bf16[4,7168]{1,0:T(4,128)(2,1)}, u32[]{:S(2)}) %copy-start.1) | copy-done | bytes 57368
  3.9 3.5 %collective-permute-done.refs_1_ = bf16[4,7168]{1,0:T(4,128)(2,1)S(1)} collective-permute-done((bf16[4,7168]{1,0:T(4,128)(2,1)}, bf16[4,7168]{1,0:T(4,128)(2,1)S(1)}, u32[]{:S(2)}, u32[]{:S(2)}) %collective-permute-start) | collective-permute-done | bytes 57376 | tf_op jit(solution)/shard_map/ppermute | solution.py:24
  7.5 1.8 %collective-permute-start.3 = (bf16[2,4,7168]{2,1,0:T(4,128)(2,1)S(1)}, bf16[2,4,7168]{2,1,0:T(4,128)(2,1)S(1)}, u32[]{:S(2)}, u32[]{:S(2)}) collective-permute-start(bf16[2,4,7168]{2,1,0:T(4,128)(2,1)S(1)} %shard_map.65.refs_0_), channel_id=1, source_target_pairs={{0,2},{1,3},{2,0},{3,1},{4,6},{5,7},{6,4},{7,5},{8,10},{9,11},{10,... | collective-permute-start | bytes 344072 | tf_op jit(solution)/shard_map/ppermute | solution.py:24
  9.2 0.8 %collective-permute-start.1 = (bf16[4,7168]{1,0:T(4,128)(2,1)S(1)}, bf16[4,7168]{1,0:T(4,128)(2,1)S(1)}, u32[]{:S(2)}, u32[]{:S(2)}) collective-permute-start(bf16[4,7168]{1,0:T(4,128)(2,1)S(1)} %copy-done.1), channel_id=1, source_target_pairs={{0,8},{4,12},{8,0},{12,4},{1,9},{5,13},{9,1},{13,5},{2,10},{6,14},... | collective-permute-start | bytes 172040 | tf_op jit(solution)/shard_map/ppermute | solution.py:24
  10.0 1.3 %collective-permute-start.2 = (bf16[4,7168]{1,0:T(4,128)(2,1)S(1)}, bf16[4,7168]{1,0:T(4,128)(2,1)S(1)}, u32[]{:S(2)}, u32[]{:S(2)}) collective-permute-start(bf16[4,7168]{1,0:T(4,128)(2,1)S(1)} %copy-done.1), channel_id=1, source_target_pairs={{0,12},{4,0},{8,4},{12,8},{1,13},{5,1},{9,5},{13,9},{2,14},{6,2},{... | collective-permute-start | bytes 172040 | tf_op jit(solution)/shard_map/ppermute | solution.py:24
  11.4 3.0 %collective-permute-done.1.refs_0_ = bf16[4,7168]{1,0:T(4,128)(2,1)S(1)} collective-permute-done((bf16[4,7168]{1,0:T(4,128)(2,1)S(1)}, bf16[4,7168]{1,0:T(4,128)(2,1)S(1)}, u32[]{:S(2)}, u32[]{:S(2)}) %collective-permute-start.1) | collective-permute-done | bytes 57376 | tf_op jit(solution)/shard_map/ppermute | solution.py:24
  14.4 0.4 collective-permute-done.2.refs_1_
  14.8 0.6 %collective-permute-start.9 = (bf16[2,4,3584]{2,1,0:T(4,128)(2,1)S(1)}, bf16[2,4,3584]{2,1,0:T(4,128)(2,1)S(1)}, u32[]{:S(2)}, u32[]{:S(2)}) collective-permute-start(bf16[2,4,3584]{2,1,0:T(4,128)(2,1)S(1)} %get-tuple-element.17.refs_1_), channel_id=1, source_target_pairs={{0,2},{1,3},{2,0},{3,1},{4,6},{5,7},{6,4},{7,5},{8,10},{9,11},{10,... | collective-permute-start | bytes 172040 | tf_op jit(solution)/shard_map/ppermute | solution.py:24
  15.4 0.5 %collective-permute-start.7 = (bf16[2,4,7168]{2,1,0:T(4,128)(2,1)S(1)}, bf16[2,4,7168]{2,1,0:T(4,128)(2,1)S(1)}, u32[]{:S(2)}, u32[]{:S(2)}) collective-permute-start(bf16[2,4,7168]{2,1,0:T(4,128)(2,1)S(1)} %collective-permute-done.3.refs_2_), channel_id=1, source_target_pairs={{0,1},{1,0},{2,3},{3,2},{4,5},{5,4},{6,7},{7,6},{8,9},{9,8},{10,11... | collective-permute-start | bytes 344072 | tf_op jit(solution)/shard_map/ppermute | solution.py:29
  15.9 1.5 %collective-permute-start.4 = (bf16[2,4,3584]{2,1,0:T(4,128)(2,1)S(1)}, bf16[2,4,3584]{2,1,0:T(4,128)(2,1)S(1)}, u32[]{:S(2)}, u32[]{:S(2)}) collective-permute-start(bf16[2,4,3584]{2,1,0:T(4,128)(2,1)S(1)} %get-tuple-element.16.refs_1_), channel_id=1, source_target_pairs={{0,2},{1,3},{2,0},{3,1},{4,6},{5,7},{6,4},{7,5},{8,10},{9,11},{10,... | collective-permute-start | bytes 172040 | tf_op jit(solution)/shard_map/ppermute | solution.py:24
  17.4 1.7 %collective-permute-done.9.refs_3_ = bf16[2,4,3584]{2,1,0:T(4,128)(2,1)S(1)} collective-permute-done((bf16[2,4,3584]{2,1,0:T(4,128)(2,1)S(1)}, bf16[2,4,3584]{2,1,0:T(4,128)(2,1)S(1)}, u32[]{:S(2)}, u32[]{:S(2)}) %collective-permute-start.9) | collective-permute-done | bytes 57376 | tf_op jit(solution)/shard_map/ppermute | solution.py:24
  19.1 0.6 %collective-permute-start.6 = (bf16[2,4,3584]{2,1,0:T(4,128)(2,1)S(1)}, bf16[2,4,3584]{2,1,0:T(4,128)(2,1)S(1)}, u32[]{:S(2)}, u32[]{:S(2)}) collective-permute-start(bf16[2,4,3584]{2,1,0:T(4,128)(2,1)S(1)} %get-tuple-element.16.refs_1_), channel_id=1, source_target_pairs={{0,1},{1,0},{2,3},{3,2},{4,5},{5,4},{6,7},{7,6},{8,9},{9,8},{10,11... | collective-permute-start | bytes 172040 | tf_op jit(solution)/shard_map/ppermute | solution.py:29
  19.7 0.6 %collective-permute-done.4.refs_3_ = bf16[2,4,3584]{2,1,0:T(4,128)(2,1)S(1)} collective-permute-done((bf16[2,4,3584]{2,1,0:T(4,128)(2,1)S(1)}, bf16[2,4,3584]{2,1,0:T(4,128)(2,1)S(1)}, u32[]{:S(2)}, u32[]{:S(2)}) %collective-permute-start.4) | collective-permute-done | bytes 57376 | tf_op jit(solution)/shard_map/ppermute | solution.py:24
  20.4 0.6 %slice-done.1 = s8[3145728]{0:T(1024)(128)(4,1)S(1)} async-done(((s8[7340032]{0:T(1024)(128)(4,1)}), s8[3145728]{0:T(1024)(128)(4,1)S(1)}, s32[]{:S(2)}) %slice-start.1) | async-done | bytes 3145752
  21.0 2.2 %copy-done = bf16[1,7168,512]{2,1,0:T(8,128)(2,1)S(1)} copy-done((bf16[1,7168,512]{2,1,0:T(8,128)(2,1)S(1)}, bf16[1,7168,512]{2,1,0:T(8,128)(2,1)}, u32[]{:S(2)}) %copy-start) | copy-done | bytes 7340056
  23.1 1.5 %ffn_first.1 = (f32[64,512]{1,0:T(8,128)S(1)}, f32[64,512]{1,0:T(8,128)S(1)}, bf16[512,1792]{1,0:T(8,128)(2,1)S(1)}) custom-call(bf16[2,4,7168]{2,1,0:T(4,128)(2,1)S(1)} %shard_map.65.refs_0_, bf16[2,4,3584]{2,1,0:T(4,128)(2,1)S(1)} %get-tuple-element.17.refs_1_, bf16[2,4,7168]{2,1,0:T(4,128)(2,1)S(1)} %collective-permute-done.3.refs_2_, ...), custom_call_target="tpu_custom_call" | custom-call | flops 704643072 | bytes 11927552 | tf_op jit(solution)/shard_map/ffn_first/pallas_call | solution.py:150
  24.7 3.4 %ffn.1 = (bf16[4,4,7168]{2,1,0:T(4,128)(2,1)S(1)}, bf16[3,4,7168]{2,1,0:T(4,128)(2,1)S(1)}, bf16[1,4,7168]{2,1,0:T(4,128)(2,1)S(1)}, bf16[4,4,7168]{2,1,0:T(4,12...) custom-call(bf16[2,4,7168]{2,1,0:T(4,128)(2,1)S(1)} %shard_map.65.refs_0_, ...), custom_call_target="tpu_custom_call" | custom-call | flops 704643072 | bytes 11927552 | tf_op jit(solution)/shard_map/ffn/pallas_call | solution.py:160
  28.2 0.6 %collective-permute-start.13 = (bf16[3,4,7168]{2,1,0:T(4,128)(2,1)S(1)}, bf16[3,4,7168]{2,1,0:T(4,128)(2,1)S(1)}, u32[]{:S(2)}, u32[]{:S(2)}) collective-permute-start(bf16[3,4,7168]{2,1,0:T(4,128)(2,1)S(1)} %get-tuple-element.24), channel_id=1, source_target_pairs={{0,1},{1,0},{2,3},{3,2},{4,5},{5,4},{6,7},{7,6},{8,9},{9,8},{10,11... | collective-permute-start | bytes 516104 | tf_op jit(solution)/shard_map/ppermute | solution.py:29
  28.8 0.4 collective-permute-start.18
  29.3 0.5 %collective-permute-done.13.refs_1_ = bf16[3,4,7168]{2,1,0:T(4,128)(2,1)S(1)} collective-permute-done((bf16[3,4,7168]{2,1,0:T(4,128)(2,1)S(1)}, bf16[3,4,7168]{2,1,0:T(4,128)(2,1)S(1)}, u32[]{:S(2)}, u32[]{:S(2)}) %collective-permute-start.13) | collective-permute-done | bytes 172064 | tf_op jit(solution)/shard_map/ppermute | solution.py:29
  29.9 0.6 %collective-permute-start.14 = (bf16[2,4,7168]{2,1,0:T(4,128)(2,1)S(1)}, bf16[2,4,7168]{2,1,0:T(4,128)(2,1)S(1)}, u32[]{:S(2)}, u32[]{:S(2)}) collective-permute-start(bf16[2,4,7168]{2,1,0:T(4,128)(2,1)S(1)} %shard_map.67), channel_id=1, source_target_pairs={{0,2},{1,3},{2,0},{3,1},{4,6},{5,7},{6,4},{7,5},{8,10},{9,11},{10,... | collective-permute-start | bytes 344072 | tf_op jit(solution)/shard_map/ppermute | solution.py:24
  30.5 1.6 %collective-permute-start.19 = (bf16[1,4,7168]{2,1,0:T(4,128)(2,1)S(1)}, bf16[1,4,7168]{2,1,0:T(4,128)(2,1)S(1)}, u32[]{:S(2)}, u32[]{:S(2)}) collective-permute-start(bf16[1,4,7168]{2,1,0:T(4,128)(2,1)S(1)} %shard_map.72), channel_id=1, source_target_pairs={{0,2},{1,3},{2,0},{3,1},{4,6},{5,7},{6,4},{7,5},{8,10},{9,11},{10,... | collective-permute-start | bytes 172040 | tf_op jit(solution)/shard_map/ppermute | solution.py:24
  32.1 0.6 %collective-permute-start.16 = (bf16[1,4,7168]{2,1,0:T(4,128)(2,1)S(1)}, bf16[1,4,7168]{2,1,0:T(4,128)(2,1)S(1)}, u32[]{:S(2)}, u32[]{:S(2)}) collective-permute-start(bf16[1,4,7168]{2,1,0:T(4,128)(2,1)S(1)} %shard_map.70), channel_id=1, source_target_pairs={{0,2},{1,3},{2,0},{3,1},{4,6},{5,7},{6,4},{7,5},{8,10},{9,11},{10,... | collective-permute-start | bytes 172040 | tf_op jit(solution)/shard_map/ppermute | solution.py:24
  32.6 4.5 %collective-permute-done.19.refs_2_ = bf16[1,4,7168]{2,1,0:T(4,128)(2,1)S(1)} collective-permute-done((bf16[1,4,7168]{2,1,0:T(4,128)(2,1)S(1)}, bf16[1,4,7168]{2,1,0:T(4,128)(2,1)S(1)}, u32[]{:S(2)}, u32[]{:S(2)}) %collective-permute-start.19) | collective-permute-done | bytes 57376 | tf_op jit(solution)/shard_map/ppermute | solution.py:24
  37.2 1.0 %collective-permute-start.20 = (bf16[1,4,7168]{2,1,0:T(4,128)(2,1)S(1)}, bf16[1,4,7168]{2,1,0:T(4,128)(2,1)S(1)}, u32[]{:S(2)}, u32[]{:S(2)}) collective-permute-start(bf16[1,4,7168]{2,1,0:T(4,128)(2,1)S(1)} %shard_map.73), channel_id=1, source_target_pairs={{0,4},{4,8},{8,12},{12,0},{1,5},{5,9},{9,13},{13,1},{2,6},{6,10},{... | collective-permute-start | bytes 172040 | tf_op jit(solution)/shard_map/ppermute | solution.py:24
  38.3 2.2 %collective-permute-start.17 = (bf16[1,4,7168]{2,1,0:T(4,128)(2,1)S(1)}, bf16[1,4,7168]{2,1,0:T(4,128)(2,1)S(1)}, u32[]{:S(2)}, u32[]{:S(2)}) collective-permute-start(bf16[1,4,7168]{2,1,0:T(4,128)(2,1)S(1)} %shard_map.71), channel_id=1, source_target_pairs={{0,8},{4,12},{8,0},{12,4},{1,9},{5,13},{9,1},{13,5},{2,10},{6,14},... | collective-permute-start | bytes 172040 | tf_op jit(solution)/shard_map/ppermute | solution.py:24
  40.5 1.6 %collective-permute-start.15 = (bf16[1,4,7168]{2,1,0:T(4,128)(2,1)S(1)}, bf16[1,4,7168]{2,1,0:T(4,128)(2,1)S(1)}, u32[]{:S(2)}, u32[]{:S(2)}) collective-permute-start(bf16[1,4,7168]{2,1,0:T(4,128)(2,1)S(1)} %shard_map.69), channel_id=1, source_target_pairs={{0,12},{4,0},{8,4},{12,8},{1,13},{5,1},{9,5},{13,9},{2,14},{6,2},{... | collective-permute-start | bytes 172040 | tf_op jit(solution)/shard_map/ppermute | solution.py:24
  42.4 1.2 %collective-permute-done.20.refs_3_ = bf16[1,4,7168]{2,1,0:T(4,128)(2,1)S(1)} collective-permute-done((bf16[1,4,7168]{2,1,0:T(4,128)(2,1)S(1)}, bf16[1,4,7168]{2,1,0:T(4,128)(2,1)S(1)}, u32[]{:S(2)}, u32[]{:S(2)}) %collective-permute-start.20) | collective-permute-done | bytes 57376 | tf_op jit(solution)/shard_map/ppermute | solution.py:24
  43.5 1.5 %collective-permute-done.17.refs_2_ = bf16[1,4,7168]{2,1,0:T(4,128)(2,1)S(1)} collective-permute-done((bf16[1,4,7168]{2,1,0:T(4,128)(2,1)S(1)}, bf16[1,4,7168]{2,1,0:T(4,128)(2,1)S(1)}, u32[]{:S(2)}, u32[]{:S(2)}) %collective-permute-start.17) | collective-permute-done | bytes 57376 | tf_op jit(solution)/shard_map/ppermute | solution.py:24
  45.0 0.3 collective-permute-done.15.refs_1_
  45.2 0.9 %combine.1 = bf16[4,7168]{1,0:T(4,128)(2,1)} custom-call(s32[4,2]{1,0:T(4,128)S(1)} %copy.7.ids_ref, s32[4,2]{1,0:T(4,128)S(1)} %copy.8.gate_ref, bf16[1,4,7168]{2,1,0:T(4,128)(2,1)S(1)} %shard_map.68.refs_0_, bf16[1,4,7168]{2,1,0:T(4,128)(2,1)S(1)} %collective-permute-done.15.refs_1_, bf16[1,4,7168]{2,1,0:T(4,128)(2,1)S(1)} %collective-permute-done.17.refs_2_, ...), custom_call_target="tpu_custom_call" | custom-call | tf_op jit(solution)/shard_map/combine/pallas_call | solution.py:204
  (39 shorter events, 0.7 us)
Async XLA Ops:
  0.0 7.4 %collective-permute-start = (bf16[4,7168]{1,0:T(4,128)(2,1)}, bf16[4,7168]{1,0:T(4,128)(2,1)S(1)}, u32[]{:S(2)}, u32[]{:S(2)}) collective-permute-start(bf16[4,7168]{1,0:T(4,128)(2,1)} %refs_0_.1), channel_id=1, source_target_pairs={{0,4},{4,8},{8,12},{12,0},{1,5},{5,9},{9,13},{13,1},{2,6},{6,10},{... | collective-permute-start | bytes 172040 | tf_op jit(solution)/shard_map/ppermute | solution.py:24
  3.1 0.9 %copy-start.1 = (bf16[4,7168]{1,0:T(4,128)(2,1)S(1)}, bf16[4,7168]{1,0:T(4,128)(2,1)}, u32[]{:S(2)}) copy-start(bf16[4,7168]{1,0:T(4,128)(2,1)} %refs_0_.1) | copy-start | bytes 172036
  7.4 12.9 %slice-start = ((s8[7340032]{0:T(1024)(128)(4,1)}), s8[4194304]{0:T(1024)(128)(4,1)S(1)}, s32[]{:S(2)}) async-start(s8[7340032]{0:T(1024)(128)(4,1)} %bitcast.5), calls=%async_computation | async-start | bytes 8388608
  7.5 8.0 %collective-permute-start.3 = (bf16[2,4,7168]{2,1,0:T(4,128)(2,1)S(1)}, bf16[2,4,7168]{2,1,0:T(4,128)(2,1)S(1)}, u32[]{:S(2)}, u32[]{:S(2)}) collective-permute-start(bf16[2,4,7168]{2,1,0:T(4,128)(2,1)S(1)} %shard_map.65.refs_0_), channel_id=1, source_target_pairs={{0,2},{1,3},{2,0},{3,1},{4,6},{5,7},{6,4},{7,5},{8,10},{9,11},{10,... | collective-permute-start | bytes 344072 | tf_op jit(solution)/shard_map/ppermute | solution.py:24
  9.2 5.2 %collective-permute-start.1 = (bf16[4,7168]{1,0:T(4,128)(2,1)S(1)}, bf16[4,7168]{1,0:T(4,128)(2,1)S(1)}, u32[]{:S(2)}, u32[]{:S(2)}) collective-permute-start(bf16[4,7168]{1,0:T(4,128)(2,1)S(1)} %copy-done.1), channel_id=1, source_target_pairs={{0,8},{4,12},{8,0},{12,4},{1,9},{5,13},{9,1},{13,5},{2,10},{6,14},... | collective-permute-start | bytes 172040 | tf_op jit(solution)/shard_map/ppermute | solution.py:24
  10.0 4.8 %collective-permute-start.2 = (bf16[4,7168]{1,0:T(4,128)(2,1)S(1)}, bf16[4,7168]{1,0:T(4,128)(2,1)S(1)}, u32[]{:S(2)}, u32[]{:S(2)}) collective-permute-start(bf16[4,7168]{1,0:T(4,128)(2,1)S(1)} %copy-done.1), channel_id=1, source_target_pairs={{0,12},{4,0},{8,4},{12,8},{1,13},{5,1},{9,5},{13,9},{2,14},{6,2},{... | collective-permute-start | bytes 172040 | tf_op jit(solution)/shard_map/ppermute | solution.py:24
  14.8 4.3 %collective-permute-start.9 = (bf16[2,4,3584]{2,1,0:T(4,128)(2,1)S(1)}, bf16[2,4,3584]{2,1,0:T(4,128)(2,1)S(1)}, u32[]{:S(2)}, u32[]{:S(2)}) collective-permute-start(bf16[2,4,3584]{2,1,0:T(4,128)(2,1)S(1)} %get-tuple-element.17.refs_1_), channel_id=1, source_target_pairs={{0,2},{1,3},{2,0},{3,1},{4,6},{5,7},{6,4},{7,5},{8,10},{9,11},{10,... | collective-permute-start | bytes 172040 | tf_op jit(solution)/shard_map/ppermute | solution.py:24
  15.4 4.9 %collective-permute-start.5 = (bf16[2,4,7168]{2,1,0:T(4,128)(2,1)S(1)}, bf16[2,4,7168]{2,1,0:T(4,128)(2,1)S(1)}, u32[]{:S(2)}, u32[]{:S(2)}) collective-permute-start(bf16[2,4,7168]{2,1,0:T(4,128)(2,1)S(1)} %shard_map.65.refs_0_), channel_id=1, source_target_pairs={{0,1},{1,0},{2,3},{3,2},{4,5},{5,4},{6,7},{7,6},{8,9},{9,8},{10,11... | collective-permute-start | bytes 344072 | tf_op jit(solution)/shard_map/ppermute | solution.py:29
  15.4 4.9 %collective-permute-start.7 = (bf16[2,4,7168]{2,1,0:T(4,128)(2,1)S(1)}, bf16[2,4,7168]{2,1,0:T(4,128)(2,1)S(1)}, u32[]{:S(2)}, u32[]{:S(2)}) collective-permute-start(bf16[2,4,7168]{2,1,0:T(4,128)(2,1)S(1)} %collective-permute-done.3.refs_2_), channel_id=1, source_target_pairs={{0,1},{1,0},{2,3},{3,2},{4,5},{5,4},{6,7},{7,6},{8,9},{9,8},{10,11... | collective-permute-start | bytes 344072 | tf_op jit(solution)/shard_map/ppermute | solution.py:29
  15.9 3.2 %collective-permute-start.10 = (bf16[2,4,3584]{2,1,0:T(4,128)(2,1)S(1)}, bf16[2,4,3584]{2,1,0:T(4,128)(2,1)S(1)}, u32[]{:S(2)}, u32[]{:S(2)}) collective-permute-start(bf16[2,4,3584]{2,1,0:T(4,128)(2,1)S(1)} %get-tuple-element.17.refs_1_), channel_id=1, source_target_pairs={{0,1},{1,0},{2,3},{3,2},{4,5},{5,4},{6,7},{7,6},{8,9},{9,8},{10,11... | collective-permute-start | bytes 172040 | tf_op jit(solution)/shard_map/ppermute | solution.py:29
  15.9 4.4 %collective-permute-start.4 = (bf16[2,4,3584]{2,1,0:T(4,128)(2,1)S(1)}, bf16[2,4,3584]{2,1,0:T(4,128)(2,1)S(1)}, u32[]{:S(2)}, u32[]{:S(2)}) collective-permute-start(bf16[2,4,3584]{2,1,0:T(4,128)(2,1)S(1)} %get-tuple-element.16.refs_1_), channel_id=1, source_target_pairs={{0,2},{1,3},{2,0},{3,1},{4,6},{5,7},{6,4},{7,5},{8,10},{9,11},{10,... | collective-permute-start | bytes 172040 | tf_op jit(solution)/shard_map/ppermute | solution.py:24
  19.1 1.2 %collective-permute-start.11 = (bf16[2,4,3584]{2,1,0:T(4,128)(2,1)S(1)}, bf16[2,4,3584]{2,1,0:T(4,128)(2,1)S(1)}, u32[]{:S(2)}, u32[]{:S(2)}) collective-permute-start(bf16[2,4,3584]{2,1,0:T(4,128)(2,1)S(1)} %collective-permute-done.9.refs_3_), channel_id=1, source_target_pairs={{0,1},{1,0},{2,3},{3,2},{4,5},{5,4},{6,7},{7,6},{8,9},{9,8},{10,11... | collective-permute-start | bytes 172040 | tf_op jit(solution)/shard_map/ppermute | solution.py:29
  19.1 1.9 %slice-start.1 = ((s8[7340032]{0:T(1024)(128)(4,1)}), s8[3145728]{0:T(1024)(128)(4,1)S(1)}, s32[]{:S(2)}) async-start(s8[7340032]{0:T(1024)(128)(4,1)} %bitcast.5), calls=%async_computation.1 | async-start | bytes 6291456
  19.1 4.0 %copy-start = (bf16[1,7168,512]{2,1,0:T(8,128)(2,1)S(1)}, bf16[1,7168,512]{2,1,0:T(8,128)(2,1)}, u32[]{:S(2)}) copy-start(bf16[1,7168,512]{2,1,0:T(8,128)(2,1)} %param.10) | copy-start | bytes 22020100
  19.1 5.6 %collective-permute-start.6 = (bf16[2,4,3584]{2,1,0:T(4,128)(2,1)S(1)}, bf16[2,4,3584]{2,1,0:T(4,128)(2,1)S(1)}, u32[]{:S(2)}, u32[]{:S(2)}) collective-permute-start(bf16[2,4,3584]{2,1,0:T(4,128)(2,1)S(1)} %get-tuple-element.16.refs_1_), channel_id=1, source_target_pairs={{0,1},{1,0},{2,3},{3,2},{4,5},{5,4},{6,7},{7,6},{8,9},{9,8},{10,11... | collective-permute-start | bytes 172040 | tf_op jit(solution)/shard_map/ppermute | solution.py:29
  20.3 4.4 %collective-permute-start.8 = (bf16[2,4,3584]{2,1,0:T(4,128)(2,1)S(1)}, bf16[2,4,3584]{2,1,0:T(4,128)(2,1)S(1)}, u32[]{:S(2)}, u32[]{:S(2)}) collective-permute-start(bf16[2,4,3584]{2,1,0:T(4,128)(2,1)S(1)} %collective-permute-done.4.refs_3_), channel_id=1, source_target_pairs={{0,1},{1,0},{2,3},{3,2},{4,5},{5,4},{6,7},{7,6},{8,9},{9,8},{10,11... | collective-permute-start | bytes 172040 | tf_op jit(solution)/shard_map/ppermute | solution.py:29
  24.7 17.4 %copy-start.2 = (s32[4,2]{0,1:T(2,128)S(1)}, s32[4,2]{0,1:T(2,128)}, u32[]{:S(2)}) copy-start(s32[4,2]{0,1:T(2,128)} %param.7) | copy-start | bytes 100
  24.7 17.5 %copy-start.3 = (s32[4,2]{0,1:T(2,128)S(1)}, s32[4,2]{0,1:T(2,128)}, u32[]{:S(2)}) copy-start(s32[4,2]{0,1:T(2,128)} %param.8) | copy-start | bytes 100
  28.2 1.6 %collective-permute-start.13 = (bf16[3,4,7168]{2,1,0:T(4,128)(2,1)S(1)}, bf16[3,4,7168]{2,1,0:T(4,128)(2,1)S(1)}, u32[]{:S(2)}, u32[]{:S(2)}) collective-permute-start(bf16[3,4,7168]{2,1,0:T(4,128)(2,1)S(1)} %get-tuple-element.24), channel_id=1, source_target_pairs={{0,1},{1,0},{2,3},{3,2},{4,5},{5,4},{6,7},{7,6},{8,9},{9,8},{10,11... | collective-permute-start | bytes 516104 | tf_op jit(solution)/shard_map/ppermute | solution.py:29
  28.8 8.4 %collective-permute-start.12 = (bf16[4,4,7168]{2,1,0:T(4,128)(2,1)S(1)}, bf16[4,4,7168]{2,1,0:T(4,128)(2,1)S(1)}, u32[]{:S(2)}, u32[]{:S(2)}) collective-permute-start(bf16[4,4,7168]{2,1,0:T(4,128)(2,1)S(1)} %get-tuple-element.22), channel_id=1, source_target_pairs={{0,1},{1,0},{2,3},{3,2},{4,5},{5,4},{6,7},{7,6},{8,9},{9,8},{10,11... | collective-permute-start | bytes 688136 | tf_op jit(solution)/shard_map/ppermute | solution.py:29
  28.8 1.6 %collective-permute-start.18 = (bf16[1,4,7168]{2,1,0:T(4,128)(2,1)S(1)}, bf16[1,4,7168]{2,1,0:T(4,128)(2,1)S(1)}, u32[]{:S(2)}, u32[]{:S(2)}) collective-permute-start(bf16[1,4,7168]{2,1,0:T(4,128)(2,1)S(1)} %get-tuple-element.26), channel_id=1, source_target_pairs={{0,1},{1,0},{2,3},{3,2},{4,5},{5,4},{6,7},{7,6},{8,9},{9,8},{10,11... | collective-permute-start | bytes 172040 | tf_op jit(solution)/shard_map/ppermute | solution.py:29
  29.9 10.6 %collective-permute-start.14 = (bf16[2,4,7168]{2,1,0:T(4,128)(2,1)S(1)}, bf16[2,4,7168]{2,1,0:T(4,128)(2,1)S(1)}, u32[]{:S(2)}, u32[]{:S(2)}) collective-permute-start(bf16[2,4,7168]{2,1,0:T(4,128)(2,1)S(1)} %shard_map.67), channel_id=1, source_target_pairs={{0,2},{1,3},{2,0},{3,1},{4,6},{5,7},{6,4},{7,5},{8,10},{9,11},{10,... | collective-permute-start | bytes 344072 | tf_op jit(solution)/shard_map/ppermute | solution.py:24
  30.5 6.7 %collective-permute-start.19 = (bf16[1,4,7168]{2,1,0:T(4,128)(2,1)S(1)}, bf16[1,4,7168]{2,1,0:T(4,128)(2,1)S(1)}, u32[]{:S(2)}, u32[]{:S(2)}) collective-permute-start(bf16[1,4,7168]{2,1,0:T(4,128)(2,1)S(1)} %shard_map.72), channel_id=1, source_target_pairs={{0,2},{1,3},{2,0},{3,1},{4,6},{5,7},{6,4},{7,5},{8,10},{9,11},{10,... | collective-permute-start | bytes 172040 | tf_op jit(solution)/shard_map/ppermute | solution.py:24
  32.1 6.1 %collective-permute-start.16 = (bf16[1,4,7168]{2,1,0:T(4,128)(2,1)S(1)}, bf16[1,4,7168]{2,1,0:T(4,128)(2,1)S(1)}, u32[]{:S(2)}, u32[]{:S(2)}) collective-permute-start(bf16[1,4,7168]{2,1,0:T(4,128)(2,1)S(1)} %shard_map.70), channel_id=1, source_target_pairs={{0,2},{1,3},{2,0},{3,1},{4,6},{5,7},{6,4},{7,5},{8,10},{9,11},{10,... | collective-permute-start | bytes 172040 | tf_op jit(solution)/shard_map/ppermute | solution.py:24
  37.2 6.3 %collective-permute-start.20 = (bf16[1,4,7168]{2,1,0:T(4,128)(2,1)S(1)}, bf16[1,4,7168]{2,1,0:T(4,128)(2,1)S(1)}, u32[]{:S(2)}, u32[]{:S(2)}) collective-permute-start(bf16[1,4,7168]{2,1,0:T(4,128)(2,1)S(1)} %shard_map.73), channel_id=1, source_target_pairs={{0,4},{4,8},{8,12},{12,0},{1,5},{5,9},{9,13},{13,1},{2,6},{6,10},{... | collective-permute-start | bytes 172040 | tf_op jit(solution)/shard_map/ppermute | solution.py:24
  38.3 6.7 %collective-permute-start.17 = (bf16[1,4,7168]{2,1,0:T(4,128)(2,1)S(1)}, bf16[1,4,7168]{2,1,0:T(4,128)(2,1)S(1)}, u32[]{:S(2)}, u32[]{:S(2)}) collective-permute-start(bf16[1,4,7168]{2,1,0:T(4,128)(2,1)S(1)} %shard_map.71), channel_id=1, source_target_pairs={{0,8},{4,12},{8,0},{12,4},{1,9},{5,13},{9,1},{13,5},{2,10},{6,14},... | collective-permute-start | bytes 172040 | tf_op jit(solution)/shard_map/ppermute | solution.py:24
  40.5 4.7 %collective-permute-start.15 = (bf16[1,4,7168]{2,1,0:T(4,128)(2,1)S(1)}, bf16[1,4,7168]{2,1,0:T(4,128)(2,1)S(1)}, u32[]{:S(2)}, u32[]{:S(2)}) collective-permute-start(bf16[1,4,7168]{2,1,0:T(4,128)(2,1)S(1)} %shard_map.69), channel_id=1, source_target_pairs={{0,12},{4,0},{8,4},{12,8},{1,13},{5,1},{9,5},{13,9},{2,14},{6,2},{... | collective-permute-start | bytes 172040 | tf_op jit(solution)/shard_map/ppermute | solution.py:24

commit v6 on v5

--- a/solution.py
+++ b/solution.py
@@ -9,6 +9,7 @@
 
 
 CORES = 2
+PARTS = 1
 MIB = 1 << 20
 VMEM_BYTES = 62 * MIB
 
@@ -185,30 +186,57 @@
 WIDTH = 1792
 
 
-def combine_kernel(ids_ref, gate_ref, *refs):
-    terms, out = refs[:-1], refs[-1]
+def gating_kernel(ids_ref, gate_ref, out):
     me = lax.axis_index("ep")
     ids = ids_ref[...]
     scores = gate_ref[...].astype(jnp.float32)
     weights = 2.5 * scores / jnp.sum(scores, axis=1, keepdims=True)
-    total = jnp.zeros(out.shape, jnp.float32)
-    for k, term in enumerate(terms):
-        label = me ^ k if mirrors(len(terms)) else lax.rem(me + k, len(terms))
+    for k in range(out.shape[0]):
+        label = me ^ k if mirrors(out.shape[0]) else lax.rem(me + k, out.shape[0])
         weight = jnp.sum(jnp.where(ids == label, weights, 0.0), axis=1, keepdims=True)
-        total = total + weight * term[0].astype(jnp.float32)
-    out[...] = total.astype(jnp.bfloat16)
-
-
-def combine(expert_ids, gate_fixed, terms):
+        out[k] = jnp.broadcast_to(weight, out.shape[1:])
+
+
+def gating(expert_ids, gate_fixed, n_ep):
     vmem = pl.BlockSpec(memory_space=pltpu.VMEM)
     return pl.pallas_call(
-        combine_kernel,
-        out_shape=jax.ShapeDtypeStruct(terms[0].shape[1:], jnp.bfloat16),
-        in_specs=[vmem] * (len(terms) + 2),
+        gating_kernel,
+        out_shape=jax.ShapeDtypeStruct((n_ep, expert_ids.shape[0], 128), jnp.float32),
+        in_specs=[vmem, vmem],
         out_specs=vmem,
-        compiler_params=pltpu.CompilerParams(vmem_limit_bytes=8 * MIB),
+        compiler_params=pltpu.CompilerParams(vmem_limit_bytes=2 * MIB),
+        name="gating",
+    )(expert_ids, gate_fixed)
+
+
+def combine_kernel(parts, weights_ref, *refs):
+    terms, out, buffer, semaphores = refs[:-3], refs[-3], refs[-2], refs[-1]
+    width = out.shape[1] // parts
+    copies = []
+    for i in range(parts):
+        at = slice(i * width, (i + 1) * width)
+        total = jnp.zeros((out.shape[0], width), jnp.float32)
+        for k, term in enumerate(terms):
+            total = total + weights_ref[k][:, :1] * term[0, :, at].astype(jnp.float32)
+        buffer[:, at] = total.astype(jnp.bfloat16)
+        copies.append(pltpu.make_async_copy(buffer.at[:, at], out.at[:, at], semaphores.at[i]))
+        copies[-1].start()
+    for copy in copies:
+        copy.wait()
+
+
+def combine(weights, terms, parts=PARTS):
+    shape = terms[0].shape[1:]
+    vmem = pl.BlockSpec(memory_space=pltpu.VMEM)
+    return pl.pallas_call(
+        functools.partial(combine_kernel, parts),
+        out_shape=jax.ShapeDtypeStruct(shape, jnp.bfloat16),
+        in_specs=[vmem] * (len(terms) + 1),
+        out_specs=pl.BlockSpec(memory_space=pl.ANY),
+        scratch_shapes=[pltpu.VMEM(shape, jnp.bfloat16), pltpu.SemaphoreType.DMA((parts,))],
+        compiler_params=pltpu.CompilerParams(vmem_limit_bytes=4 * MIB),
         name="combine",
-    )(expert_ids, gate_fixed, *terms)
+    )(weights, *terms)
 
 
 def sum_kernel(spans, *refs):
@@ -267,7 +295,7 @@
     for k in range(n_ep):
         total = add(1, (mine[0], k), (near, k), *far[k])
         terms.append(shift(total, "ep", -k) if k else total)
-    return combine(expert_ids, gate_fixed, terms)
+    return combine(gating(expert_ids, gate_fixed, n_ep), terms)
 
 
 def solution(mesh):

time: 46.3 us -> 46.2 us (level)
    pallas_call x1 -> x2, Pallas kernels: 0.88 us -> 0.96 us  [the longest x1 0.8 us: combine(): pl.pallas_call(functools.partial(combine_kernel, parts), out_shape=jax.Sh...]
where the time goes in v6:
time: 46.2 us; the launch traced here: 46 us
  starting transfers between devices  18.8 us (41%)
  waiting for transfers between devices  17.1 us (37%)
  Pallas kernels  6.23 us (13%)
  local copies, waits for them, and re-layouts  3.85 us (8%)
    ppermute x12, starting transfers between devices, shift(): return lax.ppermute(value, axis, pairs)  16.6 us
    ppermute x12, waiting for transfers between devices, shift(): return lax.ppermute(value, axis, pairs)  16.5 us
    unnamed x14, local copies, waits for them, and re-layouts  3.85 us
    pallas_call x1, Pallas kernels, expert(): pl.pallas_call(functools.partial(second_kernel, len(second_blocks), len(o...  3.44 us
    ppermute x9, starting transfers between devices, core_swap(): return lax.ppermute(value, 'tok', [(i, i ^ 1) for i in range(size)])  2.16 us
    pallas_call x1, Pallas kernels, expert(): pl.pallas_call(functools.partial(first_kernel, len(first_blocks), depth),...  1.54 us
  transfers between devices with their start and end apart: 21, of which 10 were waited for; matrix products, arithmetic and copies ran while one was open for 0% of the time, Pallas kernels for 4%

profile of v6, /device:TPU:0, one launch (start us, length us, event | category | flops | bytes accessed | tf_op | source)
XLA Modules:
  0.0 46.0 jit_solution(2421171593993065521)
XLA Ops:
  0.0 3.1 %collective-permute-start = (bf16[4,7168]{1,0:T(4,128)(2,1)}, bf16[4,7168]{1,0:T(4,128)(2,1)S(1)}, u32[]{:S(2)}, u32[]{:S(2)}) collective-permute-start(bf16[4,7168]{1,0:T(4,128)(2,1)} %refs_0_.1), channel_id=1, source_target_pairs={{0,4},{4,8},{8,12},{12,0},{1,5},{5,9},{9,13},{13,1},{2,6},{6,10},{... | collective-permute-start | bytes 172040 | tf_op jit(solution)/shard_map/ppermute | solution.py:25
  3.1 0.9 %copy-done.1 = bf16[4,7168]{1,0:T(4,128)(2,1)S(1)} copy-done((bf16[4,7168]{1,0:T(4,128)(2,1)S(1)}, bf16[4,7168]{1,0:T(4,128)(2,1)}, u32[]{:S(2)}) %copy-start.1) | copy-done | bytes 57368
  3.9 3.5 %collective-permute-done.refs_1_ = bf16[4,7168]{1,0:T(4,128)(2,1)S(1)} collective-permute-done((bf16[4,7168]{1,0:T(4,128)(2,1)}, bf16[4,7168]{1,0:T(4,128)(2,1)S(1)}, u32[]{:S(2)}, u32[]{:S(2)}) %collective-permute-start) | collective-permute-done | bytes 57376 | tf_op jit(solution)/shard_map/ppermute | solution.py:25
  7.5 1.8 %collective-permute-start.3 = (bf16[2,4,7168]{2,1,0:T(4,128)(2,1)S(1)}, bf16[2,4,7168]{2,1,0:T(4,128)(2,1)S(1)}, u32[]{:S(2)}, u32[]{:S(2)}) collective-permute-start(bf16[2,4,7168]{2,1,0:T(4,128)(2,1)S(1)} %shard_map.65.refs_0_), channel_id=1, source_target_pairs={{0,2},{1,3},{2,0},{3,1},{4,6},{5,7},{6,4},{7,5},{8,10},{9,11},{10,... | collective-permute-start | bytes 344072 | tf_op jit(solution)/shard_map/ppermute | solution.py:25
  9.2 0.8 %collective-permute-start.1 = (bf16[4,7168]{1,0:T(4,128)(2,1)S(1)}, bf16[4,7168]{1,0:T(4,128)(2,1)S(1)}, u32[]{:S(2)}, u32[]{:S(2)}) collective-permute-start(bf16[4,7168]{1,0:T(4,128)(2,1)S(1)} %copy-done.1), channel_id=1, source_target_pairs={{0,8},{4,12},{8,0},{12,4},{1,9},{5,13},{9,1},{13,5},{2,10},{6,14},... | collective-permute-start | bytes 172040 | tf_op jit(solution)/shard_map/ppermute | solution.py:25
  10.0 1.3 %collective-permute-start.2 = (bf16[4,7168]{1,0:T(4,128)(2,1)S(1)}, bf16[4,7168]{1,0:T(4,128)(2,1)S(1)}, u32[]{:S(2)}, u32[]{:S(2)}) collective-permute-start(bf16[4,7168]{1,0:T(4,128)(2,1)S(1)} %copy-done.1), channel_id=1, source_target_pairs={{0,12},{4,0},{8,4},{12,8},{1,13},{5,1},{9,5},{13,9},{2,14},{6,2},{... | collective-permute-start | bytes 172040 | tf_op jit(solution)/shard_map/ppermute | solution.py:25
  11.4 3.0 %collective-permute-done.1.refs_0_ = bf16[4,7168]{1,0:T(4,128)(2,1)S(1)} collective-permute-done((bf16[4,7168]{1,0:T(4,128)(2,1)S(1)}, bf16[4,7168]{1,0:T(4,128)(2,1)S(1)}, u32[]{:S(2)}, u32[]{:S(2)}) %collective-permute-start.1) | collective-permute-done | bytes 57376 | tf_op jit(solution)/shard_map/ppermute | solution.py:25
  14.4 0.4 collective-permute-done.2.refs_1_
  14.8 0.6 %collective-permute-start.9 = (bf16[2,4,3584]{2,1,0:T(4,128)(2,1)S(1)}, bf16[2,4,3584]{2,1,0:T(4,128)(2,1)S(1)}, u32[]{:S(2)}, u32[]{:S(2)}) collective-permute-start(bf16[2,4,3584]{2,1,0:T(4,128)(2,1)S(1)} %get-tuple-element.17.refs_1_), channel_id=1, source_target_pairs={{0,2},{1,3},{2,0},{3,1},{4,6},{5,7},{6,4},{7,5},{8,10},{9,11},{10,... | collective-permute-start | bytes 172040 | tf_op jit(solution)/shard_map/ppermute | solution.py:25
  15.4 0.5 %collective-permute-start.7 = (bf16[2,4,7168]{2,1,0:T(4,128)(2,1)S(1)}, bf16[2,4,7168]{2,1,0:T(4,128)(2,1)S(1)}, u32[]{:S(2)}, u32[]{:S(2)}) collective-permute-start(bf16[2,4,7168]{2,1,0:T(4,128)(2,1)S(1)} %collective-permute-done.3.refs_2_), channel_id=1, source_target_pairs={{0,1},{1,0},{2,3},{3,2},{4,5},{5,4},{6,7},{7,6},{8,9},{9,8},{10,11... | collective-permute-start | bytes 344072 | tf_op jit(solution)/shard_map/ppermute | solution.py:30
  15.9 1.5 %collective-permute-start.4 = (bf16[2,4,3584]{2,1,0:T(4,128)(2,1)S(1)}, bf16[2,4,3584]{2,1,0:T(4,128)(2,1)S(1)}, u32[]{:S(2)}, u32[]{:S(2)}) collective-permute-start(bf16[2,4,3584]{2,1,0:T(4,128)(2,1)S(1)} %get-tuple-element.16.refs_1_), channel_id=1, source_target_pairs={{0,2},{1,3},{2,0},{3,1},{4,6},{5,7},{6,4},{7,5},{8,10},{9,11},{10,... | collective-permute-start | bytes 172040 | tf_op jit(solution)/shard_map/ppermute | solution.py:25
  17.4 1.7 %collective-permute-done.9.refs_3_ = bf16[2,4,3584]{2,1,0:T(4,128)(2,1)S(1)} collective-permute-done((bf16[2,4,3584]{2,1,0:T(4,128)(2,1)S(1)}, bf16[2,4,3584]{2,1,0:T(4,128)(2,1)S(1)}, u32[]{:S(2)}, u32[]{:S(2)}) %collective-permute-start.9) | collective-permute-done | bytes 57376 | tf_op jit(solution)/shard_map/ppermute | solution.py:25
  19.1 0.6 %collective-permute-start.6 = (bf16[2,4,3584]{2,1,0:T(4,128)(2,1)S(1)}, bf16[2,4,3584]{2,1,0:T(4,128)(2,1)S(1)}, u32[]{:S(2)}, u32[]{:S(2)}) collective-permute-start(bf16[2,4,3584]{2,1,0:T(4,128)(2,1)S(1)} %get-tuple-element.16.refs_1_), channel_id=1, source_target_pairs={{0,1},{1,0},{2,3},{3,2},{4,5},{5,4},{6,7},{7,6},{8,9},{9,8},{10,11... | collective-permute-start | bytes 172040 | tf_op jit(solution)/shard_map/ppermute | solution.py:30
  19.7 0.6 %collective-permute-done.4.refs_3_ = bf16[2,4,3584]{2,1,0:T(4,128)(2,1)S(1)} collective-permute-done((bf16[2,4,3584]{2,1,0:T(4,128)(2,1)S(1)}, bf16[2,4,3584]{2,1,0:T(4,128)(2,1)S(1)}, u32[]{:S(2)}, u32[]{:S(2)}) %collective-permute-start.4) | collective-permute-done | bytes 57376 | tf_op jit(solution)/shard_map/ppermute | solution.py:25
  20.4 0.6 %slice-done.1 = s8[3145728]{0:T(1024)(128)(4,1)S(1)} async-done(((s8[7340032]{0:T(1024)(128)(4,1)}), s8[3145728]{0:T(1024)(128)(4,1)S(1)}, s32[]{:S(2)}) %slice-start.1) | async-done | bytes 3145752
  21.0 2.2 %copy-done = bf16[1,7168,512]{2,1,0:T(8,128)(2,1)S(1)} copy-done((bf16[1,7168,512]{2,1,0:T(8,128)(2,1)S(1)}, bf16[1,7168,512]{2,1,0:T(8,128)(2,1)}, u32[]{:S(2)}) %copy-start) | copy-done | bytes 7340056
  23.1 1.5 %ffn_first.1 = (f32[64,512]{1,0:T(8,128)S(1)}, f32[64,512]{1,0:T(8,128)S(1)}, bf16[512,1792]{1,0:T(8,128)(2,1)S(1)}) custom-call(bf16[2,4,7168]{2,1,0:T(4,128)(2,1)S(1)} %shard_map.65.refs_0_, bf16[2,4,3584]{2,1,0:T(4,128)(2,1)S(1)} %get-tuple-element.17.refs_1_, bf16[2,4,7168]{2,1,0:T(4,128)(2,1)S(1)} %collective-permute-done.3.refs_2_, ...), custom_call_target="tpu_custom_call" | custom-call | flops 704643072 | bytes 11927552 | tf_op jit(solution)/shard_map/ffn_first/pallas_call | solution.py:151
  24.7 3.4 %ffn.1 = (bf16[4,4,7168]{2,1,0:T(4,128)(2,1)S(1)}, bf16[3,4,7168]{2,1,0:T(4,128)(2,1)S(1)}, bf16[1,4,7168]{2,1,0:T(4,128)(2,1)S(1)}, bf16[4,4,7168]{2,1,0:T(4,12...) custom-call(bf16[2,4,7168]{2,1,0:T(4,128)(2,1)S(1)} %shard_map.65.refs_0_, ...), custom_call_target="tpu_custom_call" | custom-call | flops 704643072 | bytes 11927552 | tf_op jit(solution)/shard_map/ffn/pallas_call | solution.py:161
  28.2 0.6 %collective-permute-start.13 = (bf16[3,4,7168]{2,1,0:T(4,128)(2,1)S(1)}, bf16[3,4,7168]{2,1,0:T(4,128)(2,1)S(1)}, u32[]{:S(2)}, u32[]{:S(2)}) collective-permute-start(bf16[3,4,7168]{2,1,0:T(4,128)(2,1)S(1)} %get-tuple-element.24), channel_id=1, source_target_pairs={{0,1},{1,0},{2,3},{3,2},{4,5},{5,4},{6,7},{7,6},{8,9},{9,8},{10,11... | collective-permute-start | bytes 516104 | tf_op jit(solution)/shard_map/ppermute | solution.py:30
  28.8 0.4 collective-permute-start.18
  29.3 0.5 %collective-permute-done.13.refs_1_ = bf16[3,4,7168]{2,1,0:T(4,128)(2,1)S(1)} collective-permute-done((bf16[3,4,7168]{2,1,0:T(4,128)(2,1)S(1)}, bf16[3,4,7168]{2,1,0:T(4,128)(2,1)S(1)}, u32[]{:S(2)}, u32[]{:S(2)}) %collective-permute-start.13) | collective-permute-done | bytes 172064 | tf_op jit(solution)/shard_map/ppermute | solution.py:30
  29.9 0.6 %collective-permute-start.14 = (bf16[2,4,7168]{2,1,0:T(4,128)(2,1)S(1)}, bf16[2,4,7168]{2,1,0:T(4,128)(2,1)S(1)}, u32[]{:S(2)}, u32[]{:S(2)}) collective-permute-start(bf16[2,4,7168]{2,1,0:T(4,128)(2,1)S(1)} %shard_map.67), channel_id=1, source_target_pairs={{0,2},{1,3},{2,0},{3,1},{4,6},{5,7},{6,4},{7,5},{8,10},{9,11},{10,... | collective-permute-start | bytes 344072 | tf_op jit(solution)/shard_map/ppermute | solution.py:25
  30.5 1.6 %collective-permute-start.19 = (bf16[1,4,7168]{2,1,0:T(4,128)(2,1)S(1)}, bf16[1,4,7168]{2,1,0:T(4,128)(2,1)S(1)}, u32[]{:S(2)}, u32[]{:S(2)}) collective-permute-start(bf16[1,4,7168]{2,1,0:T(4,128)(2,1)S(1)} %shard_map.72), channel_id=1, source_target_pairs={{0,2},{1,3},{2,0},{3,1},{4,6},{5,7},{6,4},{7,5},{8,10},{9,11},{10,... | collective-permute-start | bytes 172040 | tf_op jit(solution)/shard_map/ppermute | solution.py:25
  32.1 0.6 %collective-permute-start.16 = (bf16[1,4,7168]{2,1,0:T(4,128)(2,1)S(1)}, bf16[1,4,7168]{2,1,0:T(4,128)(2,1)S(1)}, u32[]{:S(2)}, u32[]{:S(2)}) collective-permute-start(bf16[1,4,7168]{2,1,0:T(4,128)(2,1)S(1)} %shard_map.70), channel_id=1, source_target_pairs={{0,2},{1,3},{2,0},{3,1},{4,6},{5,7},{6,4},{7,5},{8,10},{9,11},{10,... | collective-permute-start | bytes 172040 | tf_op jit(solution)/shard_map/ppermute | solution.py:25
  32.6 4.5 %collective-permute-done.19.refs_2_ = bf16[1,4,7168]{2,1,0:T(4,128)(2,1)S(1)} collective-permute-done((bf16[1,4,7168]{2,1,0:T(4,128)(2,1)S(1)}, bf16[1,4,7168]{2,1,0:T(4,128)(2,1)S(1)}, u32[]{:S(2)}, u32[]{:S(2)}) %collective-permute-start.19) | collective-permute-done | bytes 57376 | tf_op jit(solution)/shard_map/ppermute | solution.py:25
  37.2 1.0 %collective-permute-start.20 = (bf16[1,4,7168]{2,1,0:T(4,128)(2,1)S(1)}, bf16[1,4,7168]{2,1,0:T(4,128)(2,1)S(1)}, u32[]{:S(2)}, u32[]{:S(2)}) collective-permute-start(bf16[1,4,7168]{2,1,0:T(4,128)(2,1)S(1)} %shard_map.73), channel_id=1, source_target_pairs={{0,4},{4,8},{8,12},{12,0},{1,5},{5,9},{9,13},{13,1},{2,6},{6,10},{... | collective-permute-start | bytes 172040 | tf_op jit(solution)/shard_map/ppermute | solution.py:25
  38.3 2.2 %collective-permute-start.17 = (bf16[1,4,7168]{2,1,0:T(4,128)(2,1)S(1)}, bf16[1,4,7168]{2,1,0:T(4,128)(2,1)S(1)}, u32[]{:S(2)}, u32[]{:S(2)}) collective-permute-start(bf16[1,4,7168]{2,1,0:T(4,128)(2,1)S(1)} %shard_map.71), channel_id=1, source_target_pairs={{0,8},{4,12},{8,0},{12,4},{1,9},{5,13},{9,1},{13,5},{2,10},{6,14},... | collective-permute-start | bytes 172040 | tf_op jit(solution)/shard_map/ppermute | solution.py:25
  40.5 1.6 %collective-permute-start.15 = (bf16[1,4,7168]{2,1,0:T(4,128)(2,1)S(1)}, bf16[1,4,7168]{2,1,0:T(4,128)(2,1)S(1)}, u32[]{:S(2)}, u32[]{:S(2)}) collective-permute-start(bf16[1,4,7168]{2,1,0:T(4,128)(2,1)S(1)} %shard_map.69), channel_id=1, source_target_pairs={{0,12},{4,0},{8,4},{12,8},{1,13},{5,1},{9,5},{13,9},{2,14},{6,2},{... | collective-permute-start | bytes 172040 | tf_op jit(solution)/shard_map/ppermute | solution.py:25
  42.5 1.0 %collective-permute-done.20.refs_3_ = bf16[1,4,7168]{2,1,0:T(4,128)(2,1)S(1)} collective-permute-done((bf16[1,4,7168]{2,1,0:T(4,128)(2,1)S(1)}, bf16[1,4,7168]{2,1,0:T(4,128)(2,1)S(1)}, u32[]{:S(2)}, u32[]{:S(2)}) %collective-permute-start.20) | collective-permute-done | bytes 57376 | tf_op jit(solution)/shard_map/ppermute | solution.py:25
  43.5 1.5 %collective-permute-done.17.refs_2_ = bf16[1,4,7168]{2,1,0:T(4,128)(2,1)S(1)} collective-permute-done((bf16[1,4,7168]{2,1,0:T(4,128)(2,1)S(1)}, bf16[1,4,7168]{2,1,0:T(4,128)(2,1)S(1)}, u32[]{:S(2)}, u32[]{:S(2)}) %collective-permute-start.17) | collective-permute-done | bytes 57376 | tf_op jit(solution)/shard_map/ppermute | solution.py:25
  45.0 0.3 collective-permute-done.15.refs_1_
  45.2 0.8 %combine.1 = bf16[4,7168]{1,0:T(4,128)(2,1)} custom-call(f32[4,4,128]{2,1,0:T(4,128)S(1)} %gating.1.weights_ref, bf16[1,4,7168]{2,1,0:T(4,128)(2,1)S(1)} %shard_map.68.refs_0_, bf16[1,4,7168]{2,1,0:T(4,128)(2,1)S(1)} %collective-permute-done.15.refs_1_, bf16[1,4,7168]{2,1,0:T(4,128)(2,1)S(1)} %collective-permute-done.17.refs_2_, ...), custom_call_target="tpu_custom_call" | custom-call | tf_op jit(solution)/shard_map/combine/pallas_call | solution.py:231
  (40 shorter events, 0.8 us)
Async XLA Ops:
  0.0 7.4 %collective-permute-start = (bf16[4,7168]{1,0:T(4,128)(2,1)}, bf16[4,7168]{1,0:T(4,128)(2,1)S(1)}, u32[]{:S(2)}, u32[]{:S(2)}) collective-permute-start(bf16[4,7168]{1,0:T(4,128)(2,1)} %refs_0_.1), channel_id=1, source_target_pairs={{0,4},{4,8},{8,12},{12,0},{1,5},{5,9},{9,13},{13,1},{2,6},{6,10},{... | collective-permute-start | bytes 172040 | tf_op jit(solution)/shard_map/ppermute | solution.py:25
  3.1 0.9 %copy-start.1 = (bf16[4,7168]{1,0:T(4,128)(2,1)S(1)}, bf16[4,7168]{1,0:T(4,128)(2,1)}, u32[]{:S(2)}) copy-start(bf16[4,7168]{1,0:T(4,128)(2,1)} %refs_0_.1) | copy-start | bytes 172036
  7.4 12.9 %slice-start = ((s8[7340032]{0:T(1024)(128)(4,1)}), s8[4194304]{0:T(1024)(128)(4,1)S(1)}, s32[]{:S(2)}) async-start(s8[7340032]{0:T(1024)(128)(4,1)} %bitcast.5), calls=%async_computation | async-start | bytes 8388608
  7.5 8.0 %collective-permute-start.3 = (bf16[2,4,7168]{2,1,0:T(4,128)(2,1)S(1)}, bf16[2,4,7168]{2,1,0:T(4,128)(2,1)S(1)}, u32[]{:S(2)}, u32[]{:S(2)}) collective-permute-start(bf16[2,4,7168]{2,1,0:T(4,128)(2,1)S(1)} %shard_map.65.refs_0_), channel_id=1, source_target_pairs={{0,2},{1,3},{2,0},{3,1},{4,6},{5,7},{6,4},{7,5},{8,10},{9,11},{10,... | collective-permute-start | bytes 344072 | tf_op jit(solution)/shard_map/ppermute | solution.py:25
  9.2 5.2 %collective-permute-start.1 = (bf16[4,7168]{1,0:T(4,128)(2,1)S(1)}, bf16[4,7168]{1,0:T(4,128)(2,1)S(1)}, u32[]{:S(2)}, u32[]{:S(2)}) collective-permute-start(bf16[4,7168]{1,0:T(4,128)(2,1)S(1)} %copy-done.1), channel_id=1, source_target_pairs={{0,8},{4,12},{8,0},{12,4},{1,9},{5,13},{9,1},{13,5},{2,10},{6,14},... | collective-permute-start | bytes 172040 | tf_op jit(solution)/shard_map/ppermute | solution.py:25
  10.0 4.8 %collective-permute-start.2 = (bf16[4,7168]{1,0:T(4,128)(2,1)S(1)}, bf16[4,7168]{1,0:T(4,128)(2,1)S(1)}, u32[]{:S(2)}, u32[]{:S(2)}) collective-permute-start(bf16[4,7168]{1,0:T(4,128)(2,1)S(1)} %copy-done.1), channel_id=1, source_target_pairs={{0,12},{4,0},{8,4},{12,8},{1,13},{5,1},{9,5},{13,9},{2,14},{6,2},{... | collective-permute-start | bytes 172040 | tf_op jit(solution)/shard_map/ppermute | solution.py:25
  14.8 4.3 %collective-permute-start.9 = (bf16[2,4,3584]{2,1,0:T(4,128)(2,1)S(1)}, bf16[2,4,3584]{2,1,0:T(4,128)(2,1)S(1)}, u32[]{:S(2)}, u32[]{:S(2)}) collective-permute-start(bf16[2,4,3584]{2,1,0:T(4,128)(2,1)S(1)} %get-tuple-element.17.refs_1_), channel_id=1, source_target_pairs={{0,2},{1,3},{2,0},{3,1},{4,6},{5,7},{6,4},{7,5},{8,10},{9,11},{10,... | collective-permute-start | bytes 172040 | tf_op jit(solution)/shard_map/ppermute | solution.py:25
  15.4 4.9 %collective-permute-start.5 = (bf16[2,4,7168]{2,1,0:T(4,128)(2,1)S(1)}, bf16[2,4,7168]{2,1,0:T(4,128)(2,1)S(1)}, u32[]{:S(2)}, u32[]{:S(2)}) collective-permute-start(bf16[2,4,7168]{2,1,0:T(4,128)(2,1)S(1)} %shard_map.65.refs_0_), channel_id=1, source_target_pairs={{0,1},{1,0},{2,3},{3,2},{4,5},{5,4},{6,7},{7,6},{8,9},{9,8},{10,11... | collective-permute-start | bytes 344072 | tf_op jit(solution)/shard_map/ppermute | solution.py:30
  15.4 4.9 %collective-permute-start.7 = (bf16[2,4,7168]{2,1,0:T(4,128)(2,1)S(1)}, bf16[2,4,7168]{2,1,0:T(4,128)(2,1)S(1)}, u32[]{:S(2)}, u32[]{:S(2)}) collective-permute-start(bf16[2,4,7168]{2,1,0:T(4,128)(2,1)S(1)} %collective-permute-done.3.refs_2_), channel_id=1, source_target_pairs={{0,1},{1,0},{2,3},{3,2},{4,5},{5,4},{6,7},{7,6},{8,9},{9,8},{10,11... | collective-permute-start | bytes 344072 | tf_op jit(solution)/shard_map/ppermute | solution.py:30
  15.9 3.2 %collective-permute-start.10 = (bf16[2,4,3584]{2,1,0:T(4,128)(2,1)S(1)}, bf16[2,4,3584]{2,1,0:T(4,128)(2,1)S(1)}, u32[]{:S(2)}, u32[]{:S(2)}) collective-permute-start(bf16[2,4,3584]{2,1,0:T(4,128)(2,1)S(1)} %get-tuple-element.17.refs_1_), channel_id=1, source_target_pairs={{0,1},{1,0},{2,3},{3,2},{4,5},{5,4},{6,7},{7,6},{8,9},{9,8},{10,11... | collective-permute-start | bytes 172040 | tf_op jit(solution)/shard_map/ppermute | solution.py:30
  15.9 4.4 %collective-permute-start.4 = (bf16[2,4,3584]{2,1,0:T(4,128)(2,1)S(1)}, bf16[2,4,3584]{2,1,0:T(4,128)(2,1)S(1)}, u32[]{:S(2)}, u32[]{:S(2)}) collective-permute-start(bf16[2,4,3584]{2,1,0:T(4,128)(2,1)S(1)} %get-tuple-element.16.refs_1_), channel_id=1, source_target_pairs={{0,2},{1,3},{2,0},{3,1},{4,6},{5,7},{6,4},{7,5},{8,10},{9,11},{10,... | collective-permute-start | bytes 172040 | tf_op jit(solution)/shard_map/ppermute | solution.py:25
  19.1 1.2 %collective-permute-start.11 = (bf16[2,4,3584]{2,1,0:T(4,128)(2,1)S(1)}, bf16[2,4,3584]{2,1,0:T(4,128)(2,1)S(1)}, u32[]{:S(2)}, u32[]{:S(2)}) collective-permute-start(bf16[2,4,3584]{2,1,0:T(4,128)(2,1)S(1)} %collective-permute-done.9.refs_3_), channel_id=1, source_target_pairs={{0,1},{1,0},{2,3},{3,2},{4,5},{5,4},{6,7},{7,6},{8,9},{9,8},{10,11... | collective-permute-start | bytes 172040 | tf_op jit(solution)/shard_map/ppermute | solution.py:30
  19.1 1.9 %slice-start.1 = ((s8[7340032]{0:T(1024)(128)(4,1)}), s8[3145728]{0:T(1024)(128)(4,1)S(1)}, s32[]{:S(2)}) async-start(s8[7340032]{0:T(1024)(128)(4,1)} %bitcast.5), calls=%async_computation.1 | async-start | bytes 6291456
  19.1 4.0 %copy-start = (bf16[1,7168,512]{2,1,0:T(8,128)(2,1)S(1)}, bf16[1,7168,512]{2,1,0:T(8,128)(2,1)}, u32[]{:S(2)}) copy-start(bf16[1,7168,512]{2,1,0:T(8,128)(2,1)} %param.10) | copy-start | bytes 22020100
  19.1 5.6 %collective-permute-start.6 = (bf16[2,4,3584]{2,1,0:T(4,128)(2,1)S(1)}, bf16[2,4,3584]{2,1,0:T(4,128)(2,1)S(1)}, u32[]{:S(2)}, u32[]{:S(2)}) collective-permute-start(bf16[2,4,3584]{2,1,0:T(4,128)(2,1)S(1)} %get-tuple-element.16.refs_1_), channel_id=1, source_target_pairs={{0,1},{1,0},{2,3},{3,2},{4,5},{5,4},{6,7},{7,6},{8,9},{9,8},{10,11... | collective-permute-start | bytes 172040 | tf_op jit(solution)/shard_map/ppermute | solution.py:30
  20.3 4.4 %collective-permute-start.8 = (bf16[2,4,3584]{2,1,0:T(4,128)(2,1)S(1)}, bf16[2,4,3584]{2,1,0:T(4,128)(2,1)S(1)}, u32[]{:S(2)}, u32[]{:S(2)}) collective-permute-start(bf16[2,4,3584]{2,1,0:T(4,128)(2,1)S(1)} %collective-permute-done.4.refs_3_), channel_id=1, source_target_pairs={{0,1},{1,0},{2,3},{3,2},{4,5},{5,4},{6,7},{7,6},{8,9},{9,8},{10,11... | collective-permute-start | bytes 172040 | tf_op jit(solution)/shard_map/ppermute | solution.py:30
  24.7 17.4 %copy-start.2 = (s32[4,2]{0,1:T(2,128)S(1)}, s32[4,2]{0,1:T(2,128)}, u32[]{:S(2)}) copy-start(s32[4,2]{0,1:T(2,128)} %param.7) | copy-start | bytes 100
  24.7 17.5 %copy-start.3 = (s32[4,2]{0,1:T(2,128)S(1)}, s32[4,2]{0,1:T(2,128)}, u32[]{:S(2)}) copy-start(s32[4,2]{0,1:T(2,128)} %param.8) | copy-start | bytes 100
  28.2 1.6 %collective-permute-start.13 = (bf16[3,4,7168]{2,1,0:T(4,128)(2,1)S(1)}, bf16[3,4,7168]{2,1,0:T(4,128)(2,1)S(1)}, u32[]{:S(2)}, u32[]{:S(2)}) collective-permute-start(bf16[3,4,7168]{2,1,0:T(4,128)(2,1)S(1)} %get-tuple-element.24), channel_id=1, source_target_pairs={{0,1},{1,0},{2,3},{3,2},{4,5},{5,4},{6,7},{7,6},{8,9},{9,8},{10,11... | collective-permute-start | bytes 516104 | tf_op jit(solution)/shard_map/ppermute | solution.py:30
  28.8 8.4 %collective-permute-start.12 = (bf16[4,4,7168]{2,1,0:T(4,128)(2,1)S(1)}, bf16[4,4,7168]{2,1,0:T(4,128)(2,1)S(1)}, u32[]{:S(2)}, u32[]{:S(2)}) collective-permute-start(bf16[4,4,7168]{2,1,0:T(4,128)(2,1)S(1)} %get-tuple-element.22), channel_id=1, source_target_pairs={{0,1},{1,0},{2,3},{3,2},{4,5},{5,4},{6,7},{7,6},{8,9},{9,8},{10,11... | collective-permute-start | bytes 688136 | tf_op jit(solution)/shard_map/ppermute | solution.py:30
  28.8 1.6 %collective-permute-start.18 = (bf16[1,4,7168]{2,1,0:T(4,128)(2,1)S(1)}, bf16[1,4,7168]{2,1,0:T(4,128)(2,1)S(1)}, u32[]{:S(2)}, u32[]{:S(2)}) collective-permute-start(bf16[1,4,7168]{2,1,0:T(4,128)(2,1)S(1)} %get-tuple-element.26), channel_id=1, source_target_pairs={{0,1},{1,0},{2,3},{3,2},{4,5},{5,4},{6,7},{7,6},{8,9},{9,8},{10,11... | collective-permute-start | bytes 172040 | tf_op jit(solution)/shard_map/ppermute | solution.py:30
  29.9 10.6 %collective-permute-start.14 = (bf16[2,4,7168]{2,1,0:T(4,128)(2,1)S(1)}, bf16[2,4,7168]{2,1,0:T(4,128)(2,1)S(1)}, u32[]{:S(2)}, u32[]{:S(2)}) collective-permute-start(bf16[2,4,7168]{2,1,0:T(4,128)(2,1)S(1)} %shard_map.67), channel_id=1, source_target_pairs={{0,2},{1,3},{2,0},{3,1},{4,6},{5,7},{6,4},{7,5},{8,10},{9,11},{10,... | collective-permute-start | bytes 344072 | tf_op jit(solution)/shard_map/ppermute | solution.py:25
  30.5 6.7 %collective-permute-start.19 = (bf16[1,4,7168]{2,1,0:T(4,128)(2,1)S(1)}, bf16[1,4,7168]{2,1,0:T(4,128)(2,1)S(1)}, u32[]{:S(2)}, u32[]{:S(2)}) collective-permute-start(bf16[1,4,7168]{2,1,0:T(4,128)(2,1)S(1)} %shard_map.72), channel_id=1, source_target_pairs={{0,2},{1,3},{2,0},{3,1},{4,6},{5,7},{6,4},{7,5},{8,10},{9,11},{10,... | collective-permute-start | bytes 172040 | tf_op jit(solution)/shard_map/ppermute | solution.py:25
  32.1 6.1 %collective-permute-start.16 = (bf16[1,4,7168]{2,1,0:T(4,128)(2,1)S(1)}, bf16[1,4,7168]{2,1,0:T(4,128)(2,1)S(1)}, u32[]{:S(2)}, u32[]{:S(2)}) collective-permute-start(bf16[1,4,7168]{2,1,0:T(4,128)(2,1)S(1)} %shard_map.70), channel_id=1, source_target_pairs={{0,2},{1,3},{2,0},{3,1},{4,6},{5,7},{6,4},{7,5},{8,10},{9,11},{10,... | collective-permute-start | bytes 172040 | tf_op jit(solution)/shard_map/ppermute | solution.py:25
  37.2 6.3 %collective-permute-start.20 = (bf16[1,4,7168]{2,1,0:T(4,128)(2,1)S(1)}, bf16[1,4,7168]{2,1,0:T(4,128)(2,1)S(1)}, u32[]{:S(2)}, u32[]{:S(2)}) collective-permute-start(bf16[1,4,7168]{2,1,0:T(4,128)(2,1)S(1)} %shard_map.73), channel_id=1, source_target_pairs={{0,4},{4,8},{8,12},{12,0},{1,5},{5,9},{9,13},{13,1},{2,6},{6,10},{... | collective-permute-start | bytes 172040 | tf_op jit(solution)/shard_map/ppermute | solution.py:25
  38.3 6.7 %collective-permute-start.17 = (bf16[1,4,7168]{2,1,0:T(4,128)(2,1)S(1)}, bf16[1,4,7168]{2,1,0:T(4,128)(2,1)S(1)}, u32[]{:S(2)}, u32[]{:S(2)}) collective-permute-start(bf16[1,4,7168]{2,1,0:T(4,128)(2,1)S(1)} %shard_map.71), channel_id=1, source_target_pairs={{0,8},{4,12},{8,0},{12,4},{1,9},{5,13},{9,1},{13,5},{2,10},{6,14},... | collective-permute-start | bytes 172040 | tf_op jit(solution)/shard_map/ppermute | solution.py:25
  40.5 4.7 %collective-permute-start.15 = (bf16[1,4,7168]{2,1,0:T(4,128)(2,1)S(1)}, bf16[1,4,7168]{2,1,0:T(4,128)(2,1)S(1)}, u32[]{:S(2)}, u32[]{:S(2)}) collective-permute-start(bf16[1,4,7168]{2,1,0:T(4,128)(2,1)S(1)} %shard_map.69), channel_id=1, source_target_pairs={{0,12},{4,0},{8,4},{12,8},{1,13},{5,1},{9,5},{13,9},{2,14},{6,2},{... | collective-permute-start | bytes 172040 | tf_op jit(solution)/shard_map/ppermute | solution.py:25
